TPU v7x, 1024 devices: a whole 4x4x32 slice. The times are simulated.
1024 devices in a mesh: dp: 128 (over z, y_hi, core), mp: 8 (over x, y_lo).
Axes of the slice: x: 4, y: 4 (y_hi: 2, y_lo: 2; y = y_hi * 2 + y_lo), z: 32, core: 2. Of those that a mesh axis runs over, the one named last changes fastest.
Arguments:
- frames: bfloat16 [24576, 1536], P('dp', 'mp'), may hold values from -24 to 24
- frame_owner: int32 [24576, 1], P('dp'), may hold values from 0 to 127; in each aligned block of 192 rows (0 to 191, 192 to 383, ...) at most 2 rows name the same one
- frame_valid: int32 [24576], P('dp'), may hold values 0 or 1
- norm_gain: float32 [1536], replicated, may hold values from 0.1 to 1.9
- value_weight: bfloat16 [1536, 1536], P('dp', 'mp'), may hold values from -0.15625 to 0.15625
- gate_weight: bfloat16 [1536, 1536], P('dp', 'mp'), may hold values from -0.15625 to 0.15625
- grad_owned: bfloat16 [128, 128, 2, 1536], P('dp', None, None, 'mp'), may hold values from -6 to 6
Outputs:
- gated_owned: bfloat16 [128, 128, 2, 1536], P('dp', None, None, 'mp')
- value_grad: float32 [1536, 1536], P('dp', 'mp')
- gate_grad: float32 [1536, 1536], P('dp', 'mp')
- normed_grad: bfloat16 [128, 128, 2, 1536], P('dp', None, None, 'mp')
Inputs may be any that keep to these rules, and one draw needn't show every extreme that they name: `frame_owner`: within the rows of one device (aligned blocks of 192 rows) no owner is named more than 2 times, a bound that some block reaches.
All inputs are finite; a program needn't handle non-finite values. No bound on the sum of `frame_valid` on one device may be relied on, other than what follows from the above.
Results may differ from a plain program's by a relative error of at most 0.013.
Values may be sent and summed in bfloat16 or wider, within the bound.
No kernel may reach another device: no remote copies, remote signals or barrier semaphores. Data moves between devices by JAX's collectives and lax.ppermute only.
A program may use at most 32 MiB of HBM per device.

v0:
```python
import jax
import jax.numpy as jnp
from jax import lax
from jax.sharding import PartitionSpec as P

epsilon = 1e-05


def normalize_project(whole, slot_live, norm_gain, value_full, gate_full):
    wide = whole.astype(jnp.float32)
    row_mean = jnp.mean(wide, axis=-1, keepdims=True)
    centred = wide - row_mean
    row_var = jnp.mean(centred * centred, axis=-1, keepdims=True)
    normed = (
        centred
        * lax.rsqrt(row_var + epsilon)
        * norm_gain
        * slot_live.astype(jnp.float32)[..., None]
    ).astype(jnp.bfloat16)
    value_act = jnp.einsum("skd,de->ske", normed, value_full, preferred_element_type=jnp.float32)
    gate_act = jnp.einsum("skd,de->ske", normed, gate_full, preferred_element_type=jnp.float32)
    return (normed, value_act, gate_act)


def column_term(normed_flat, delta):
    return lax.dot_general(
        normed_flat, delta, (((0,), (0,)), ((), ())), preferred_element_type=jnp.float32
    )


def body(frames, frame_owner, frame_valid, norm_gain, value_weight, gate_weight, grad_owned):
    peers = lax.axis_size("dp")
    capacity = grad_owned.shape[2]
    row_total = frames.shape[0]
    slot_total = peers * capacity
    dest_owner = frame_owner[:, 0]
    positions = jnp.arange(row_total, dtype=jnp.int32)
    earlier = positions[None, :] < positions[:, None]
    same_owner = dest_owner[:, None] == dest_owner[None, :]
    slot_index = jnp.sum((same_owner & earlier).astype(jnp.int32), axis=1)
    targets = dest_owner * capacity + slot_index
    placing = (jnp.arange(slot_total, dtype=jnp.int32)[:, None] == targets[None, :]).astype(
        jnp.bfloat16
    )
    send_buffer = (
        jnp.dot(placing, frames, preferred_element_type=jnp.float32)
        .astype(jnp.bfloat16)
        .reshape(peers, capacity, -1)
    )
    send_live = (
        jnp.dot(placing, frame_valid.astype(jnp.bfloat16), preferred_element_type=jnp.float32)
        .astype(jnp.bfloat16)
        .reshape(peers, capacity)
    )
    value_full, gate_full = (
        lax.all_gather(value_weight, "dp", axis=0, tiled=True),
        lax.all_gather(gate_weight, "dp", axis=0, tiled=True),
    )
    received_rows, live_recv = (
        lax.all_to_all(send_buffer, "dp", split_axis=0, concat_axis=0, tiled=True),
        lax.all_to_all(send_live, "dp", split_axis=0, concat_axis=0, tiled=True),
    )
    whole = lax.all_gather(received_rows, "mp", axis=2, tiled=True)
    normed, value_act, gate_act = normalize_project(
        whole, live_recv, norm_gain, value_full, gate_full
    )
    normed_flat = normed.reshape(slot_total, -1)
    value_flat = value_act.reshape(slot_total, -1)
    gate_sig = jax.nn.sigmoid(gate_act.reshape(slot_total, -1))
    live_col = live_recv.astype(jnp.float32).reshape(slot_total, 1)
    gated = (value_flat * gate_sig).astype(jnp.bfloat16)
    upstream = grad_owned.reshape(slot_total, -1).astype(jnp.float32)
    value_delta = (upstream * gate_sig * live_col).astype(jnp.bfloat16)
    gate_delta = (upstream * value_flat * gate_sig * (1.0 - gate_sig) * live_col).astype(
        jnp.bfloat16
    )
    scale = float(row_total * peers) ** (-0.5)
    value_grad = (
        lax.psum_scatter(
            column_term(normed_flat, value_delta), "dp", scatter_dimension=0, tiled=True
        )
        * scale
    )
    gate_grad = (
        lax.psum_scatter(
            column_term(normed_flat, gate_delta), "dp", scatter_dimension=0, tiled=True
        )
        * scale
    )
    contract_last = (((1,), (1,)), ((), ()))
    partial_grad = lax.dot_general(
        value_delta, value_full, contract_last, preferred_element_type=jnp.float32
    ) + lax.dot_general(gate_delta, gate_full, contract_last, preferred_element_type=jnp.float32)
    input_grad = lax.psum_scatter(
        partial_grad.astype(jnp.bfloat16), "mp", scatter_dimension=1, tiled=True
    )
    gated_owned = gated.reshape(1, peers, capacity, -1)
    normed_grad = input_grad.reshape(1, peers, capacity, -1)
    return (gated_owned, value_grad, gate_grad, normed_grad)


def solution(mesh):
    placed = (
        P("dp", "mp"),
        P("dp", None),
        P("dp"),
        P(),
        P("dp", "mp"),
        P("dp", "mp"),
        P("dp", None, None, "mp"),
    )
    return jax.shard_map(
        body,
        mesh=mesh,
        in_specs=placed,
        out_specs=(
            P("dp", None, None, "mp"),
            P("dp", "mp"),
            P("dp", "mp"),
            P("dp", None, None, "mp"),
        ),
        check_vma=False,
    )
```

profile of v0, /device:TPU:1, one launch (start us, length us, event | category | flops | bytes accessed | tf_op | source)
XLA Modules:
  0.0 969.8 jit_solution(13287267255146576392)
XLA Ops:
  10.5 33.8 %all-to-all-start.1 = ((bf16[128,1,2]{2,1,0:T(2,128)(2,1)}), bf16[128,1,2]{2,1,0:T(2,128)(2,1)S(1)}, u32[]{:S(2)}, u32[]{:S(2)}) async-start(bf16[128,1,2]{2,1,0:T(2,128)(2,1)} %all_to_all.12), calls=%async_computation.1 | async-start | bytes 131072 | tf_op jit(solution)/shard_map/all_to_all | solution.py:61
  45.4 25.4 %all-to-all-done.1 = bf16[128,1,2]{2,1,0:T(2,128)(2,1)S(1)} async-done(((bf16[128,1,2]{2,1,0:T(2,128)(2,1)}), bf16[128,1,2]{2,1,0:T(2,128)(2,1)S(1)}, u32[]{:S(2)}, u32[]{:S(2)}) %all-to-all-start.1) | async-done | bytes 544 | tf_op jit(solution)/shard_map/all_to_all | solution.py:61
  70.8 5.7 all-to-all-start
  76.6 150.7 %all-gather = bf16[128,12,192]{2,1,0:T(8,128)(2,1)S(1)} all-gather(bf16[1,12,192]{2,1,0:T(8,128)(2,1)} %bitcast.52), channel_id=1, replica_groups=mesh['dp'=128,'mp'=8] {'dp'}, dimensions={0}, use_global_device_ids=true | all-gather | bytes 594432 | tf_op jit(solution)/shard_map/all_gather | solution.py:56
  227.7 145.5 %all-gather.1 = bf16[128,12,192]{2,1,0:T(8,128)(2,1)S(1)} all-gather(bf16[1,12,192]{2,1,0:T(8,128)(2,1)S(1)} %bitcast.53), channel_id=1, replica_groups=mesh['dp'=128,'mp'=8] {'dp'}, dimensions={0}, use_global_device_ids=true | all-gather | bytes 594432 | tf_op jit(solution)/shard_map/all_gather | solution.py:57
  375.3 23.9 %all_gather.9 = bf16[128,2,1536]{0,1,2:T(2,128)(2,1)S(1)} all-gather(bf16[128,2,192]{0,1,2:T(2,128)(2,1)S(1)} %copy.68), channel_id=1, replica_groups=mesh['dp'=128,'mp'=8] {'mp'}, dimensions={2}, use_global_device_ids=true | all-gather | bytes 884736 | tf_op jit(solution)/shard_map/all_gather | solution.py:63
  404.9 2.5 convolution_bitcast_fusion
  413.7 317.2 %fusion.36 = (f32[16,192]{1,0:T(8,128)S(1)}, f32[16,192]{1,0:T(8,128)S(1)}) fusion(f32[1536,192]{1,0:T(8,128)S(1)} %fusion.37, f32[1536,192]{1,0:T(8,128)S(1)} %copy-done.1), kind=kCustom, calls=%all-reduce-scatter.2 | all-reduce-scatter fusion | flops 786433 | bytes 2387968
  730.9 7.0 collective-permute-start.30
  737.9 8.6 collective-permute-start.29
  746.5 7.5 collective-permute-start.31
  754.0 4.3 collective-permute-start.63
  760.9 6.8 collective-permute-start.26
  767.8 10.4 %collective-permute-start.25 = (f32[16,192]{1,0:T(8,128)S(1)}, f32[16,192]{1,0:T(8,128)S(1)}, u32[]{:S(2)}, u32[]{:S(2)}) collective-permute-start(f32[16,192]{1,0:T(8,128)S(1)} %get-tuple-element.26), channel_id=1, source_target_pairs={{0,208},{8,216},{16,224},{24,232},{32,240},{40,248},{48,256},{56,2... | collective-permute-start | bytes 36872
  778.2 3.3 collective-permute-start.24
  784.2 4.6 collective-permute-start.21
  788.8 2.9 collective-permute-start.20
  791.8 3.2 collective-permute-start.19
  794.9 3.1 collective-permute-start.18
  800.2 5.6 collective-permute-start.16
  809.0 4.1 collective-permute-start.13
  813.1 4.3 collective-permute-start.12
  820.3 4.3 collective-permute-start.9
  824.6 4.1 collective-permute-start.8
  828.7 3.3 collective-permute-start.7
  833.4 4.4 collective-permute-start.5
  837.8 5.2 collective-permute-start.4
  845.5 3.5 collective-permute-start.1
  849.0 5.2 collective-permute-start
  855.6 2.5 collective-permute-start.61
  864.3 8.2 collective-permute-start.56
  876.1 3.4 collective-permute-start.53
  879.5 3.4 collective-permute-start.52
  882.9 3.7 collective-permute-start.51
  886.6 3.5 collective-permute-start.50
  890.1 6.7 collective-permute-start.49
  896.9 4.7 collective-permute-start.48
  904.2 3.3 collective-permute-start.45
  907.5 6.0 collective-permute-start.44
  916.2 3.7 collective-permute-start.41
  919.9 3.2 collective-permute-start.40
  926.7 3.3 collective-permute-start.37
  931.9 4.8 collective-permute-start.36
  936.7 2.6 collective-permute-start.35
  941.3 3.4 collective-permute-start.33
  944.7 6.3 collective-permute-start.32
  952.6 3.6 concatenate
  956.2 3.7 concatenate.1
  (157 shorter events, 63.5 us)
Async XLA Ops:
  10.5 60.3 %all-to-all-start.1 = ((bf16[128,1,2]{2,1,0:T(2,128)(2,1)}), bf16[128,1,2]{2,1,0:T(2,128)(2,1)S(1)}, u32[]{:S(2)}, u32[]{:S(2)}) async-start(bf16[128,1,2]{2,1,0:T(2,128)(2,1)} %all_to_all.12), calls=%async_computation.1 | async-start | bytes 131072 | tf_op jit(solution)/shard_map/all_to_all | solution.py:61
  70.8 304.3 %all-to-all-start = ((bf16[128,2,192]{2,1,0:T(2,128)(2,1)}), bf16[128,2,192]{2,1,0:T(2,128)(2,1)S(1)}, u32[]{:S(2)}, u32[]{:S(2)}) async-start(bf16[128,2,192]{2,1,0:T(2,128)(2,1)} %reshape.99), calls=%async_computation | async-start | bytes 262144 | tf_op jit(solution)/shard_map/all_to_all | solution.py:60
  76.5 884.6 %reduce-scatter.6.cloned.1.call-start = ((), (), s32[]{:S(2)}) async-start(), calls=%async_computation.3 | async-start | bytes 884736 | tf_op jit(solution)/shard_map/reduce_scatter | solution.py:94
  730.9 36.9 %collective-permute-start.30 = (f32[16,192]{1,0:T(8,128)S(1)}, f32[16,192]{1,0:T(8,128)S(1)}, u32[]{:S(2)}, u32[]{:S(2)}) collective-permute-start(f32[16,192]{1,0:T(8,128)S(1)} %get-tuple-element.26), channel_id=1, source_target_pairs={{0,248},{8,256},{16,264},{24,272},{32,280},{40,288},{48,296},{56,3... | collective-permute-start | bytes 36872
  737.9 40.4 %collective-permute-start.29 = (f32[16,192]{1,0:T(8,128)S(1)}, f32[16,192]{1,0:T(8,128)S(1)}, u32[]{:S(2)}, u32[]{:S(2)}) collective-permute-start(f32[16,192]{1,0:T(8,128)S(1)} %get-tuple-element.26), channel_id=1, source_target_pairs={{0,240},{8,248},{16,256},{24,264},{32,272},{40,280},{48,288},{56,2... | collective-permute-start | bytes 36872
  758.3 23.2 %collective-permute-start.28 = (f32[16,192]{1,0:T(8,128)S(1)}, f32[16,192]{1,0:T(8,128)S(1)}, u32[]{:S(2)}, u32[]{:S(2)}) collective-permute-start(f32[16,192]{1,0:T(8,128)S(1)} %get-tuple-element.26), channel_id=1, source_target_pairs={{0,232},{8,240},{16,248},{24,256},{32,264},{40,272},{48,280},{56,2... | collective-permute-start | bytes 36872
  759.6 23.2 %collective-permute-start.27 = (f32[16,192]{1,0:T(8,128)S(1)}, f32[16,192]{1,0:T(8,128)S(1)}, u32[]{:S(2)}, u32[]{:S(2)}) collective-permute-start(f32[16,192]{1,0:T(8,128)S(1)} %get-tuple-element.26), channel_id=1, source_target_pairs={{0,224},{8,232},{16,240},{24,248},{32,256},{40,264},{48,272},{56,2... | collective-permute-start | bytes 36872
  760.9 23.2 %collective-permute-start.26 = (f32[16,192]{1,0:T(8,128)S(1)}, f32[16,192]{1,0:T(8,128)S(1)}, u32[]{:S(2)}, u32[]{:S(2)}) collective-permute-start(f32[16,192]{1,0:T(8,128)S(1)} %get-tuple-element.26), channel_id=1, source_target_pairs={{0,216},{8,224},{16,232},{24,240},{32,248},{40,256},{48,264},{56,2... | collective-permute-start | bytes 36872
  767.8 21.0 %collective-permute-start.25 = (f32[16,192]{1,0:T(8,128)S(1)}, f32[16,192]{1,0:T(8,128)S(1)}, u32[]{:S(2)}, u32[]{:S(2)}) collective-permute-start(f32[16,192]{1,0:T(8,128)S(1)} %get-tuple-element.26), channel_id=1, source_target_pairs={{0,208},{8,216},{16,224},{24,232},{32,240},{40,248},{48,256},{56,2... | collective-permute-start | bytes 36872
  782.9 15.2 %collective-permute-start.22 = (f32[16,192]{1,0:T(8,128)S(1)}, f32[16,192]{1,0:T(8,128)S(1)}, u32[]{:S(2)}, u32[]{:S(2)}) collective-permute-start(f32[16,192]{1,0:T(8,128)S(1)} %get-tuple-element.26), channel_id=1, source_target_pairs={{0,184},{8,192},{16,200},{24,208},{32,216},{40,224},{48,232},{56,2... | collective-permute-start | bytes 36872
  784.2 15.9 %collective-permute-start.21 = (f32[16,192]{1,0:T(8,128)S(1)}, f32[16,192]{1,0:T(8,128)S(1)}, u32[]{:S(2)}, u32[]{:S(2)}) collective-permute-start(f32[16,192]{1,0:T(8,128)S(1)} %get-tuple-element.26), channel_id=1, source_target_pairs={{0,176},{8,184},{16,192},{24,200},{32,208},{40,216},{48,224},{56,2... | collective-permute-start | bytes 36872
  788.8 16.9 %collective-permute-start.20 = (f32[16,192]{1,0:T(8,128)S(1)}, f32[16,192]{1,0:T(8,128)S(1)}, u32[]{:S(2)}, u32[]{:S(2)}) collective-permute-start(f32[16,192]{1,0:T(8,128)S(1)} %get-tuple-element.26), channel_id=1, source_target_pairs={{0,168},{8,176},{16,184},{24,192},{32,200},{40,208},{48,216},{56,2... | collective-permute-start | bytes 36872
  791.8 16.0 %collective-permute-start.19 = (f32[16,192]{1,0:T(8,128)S(1)}, f32[16,192]{1,0:T(8,128)S(1)}, u32[]{:S(2)}, u32[]{:S(2)}) collective-permute-start(f32[16,192]{1,0:T(8,128)S(1)} %get-tuple-element.26), channel_id=1, source_target_pairs={{0,160},{8,168},{16,176},{24,184},{32,192},{40,200},{48,208},{56,2... | collective-permute-start | bytes 36872
  798.1 15.0 %collective-permute-start.17 = (f32[16,192]{1,0:T(8,128)S(1)}, f32[16,192]{1,0:T(8,128)S(1)}, u32[]{:S(2)}, u32[]{:S(2)}) collective-permute-start(f32[16,192]{1,0:T(8,128)S(1)} %get-tuple-element.26), channel_id=1, source_target_pairs={{0,144},{8,152},{16,160},{24,168},{32,176},{40,184},{48,192},{56,2... | collective-permute-start | bytes 36872
  800.2 17.3 %collective-permute-start.16 = (f32[16,192]{1,0:T(8,128)S(1)}, f32[16,192]{1,0:T(8,128)S(1)}, u32[]{:S(2)}, u32[]{:S(2)}) collective-permute-start(f32[16,192]{1,0:T(8,128)S(1)} %get-tuple-element.26), channel_id=1, source_target_pairs={{0,136},{8,144},{16,152},{24,160},{32,168},{40,176},{48,184},{56,1... | collective-permute-start | bytes 36872
  809.0 15.6 %collective-permute-start.13 = (f32[16,192]{1,0:T(8,128)S(1)}, f32[16,192]{1,0:T(8,128)S(1)}, u32[]{:S(2)}, u32[]{:S(2)}) collective-permute-start(f32[16,192]{1,0:T(8,128)S(1)} %get-tuple-element.26), channel_id=1, source_target_pairs={{0,112},{8,120},{16,128},{24,136},{32,144},{40,152},{48,160},{56,1... | collective-permute-start | bytes 36872
  813.1 15.6 %collective-permute-start.12 = (f32[16,192]{1,0:T(8,128)S(1)}, f32[16,192]{1,0:T(8,128)S(1)}, u32[]{:S(2)}, u32[]{:S(2)}) collective-permute-start(f32[16,192]{1,0:T(8,128)S(1)} %get-tuple-element.26), channel_id=1, source_target_pairs={{0,104},{8,112},{16,120},{24,128},{32,136},{40,144},{48,152},{56,1... | collective-permute-start | bytes 36872
  817.5 14.6 %collective-permute-start.11 = (f32[16,192]{1,0:T(8,128)S(1)}, f32[16,192]{1,0:T(8,128)S(1)}, u32[]{:S(2)}, u32[]{:S(2)}) collective-permute-start(f32[16,192]{1,0:T(8,128)S(1)} %get-tuple-element.26), channel_id=1, source_target_pairs={{0,96},{8,104},{16,112},{24,120},{32,128},{40,136},{48,144},{56,15... | collective-permute-start | bytes 36872
  818.8 14.6 %collective-permute-start.10 = (f32[16,192]{1,0:T(8,128)S(1)}, f32[16,192]{1,0:T(8,128)S(1)}, u32[]{:S(2)}, u32[]{:S(2)}) collective-permute-start(f32[16,192]{1,0:T(8,128)S(1)} %get-tuple-element.26), channel_id=1, source_target_pairs={{0,88},{8,96},{16,104},{24,112},{32,120},{40,128},{48,136},{56,144... | collective-permute-start | bytes 36872
  820.3 17.5 %collective-permute-start.9 = (f32[16,192]{1,0:T(8,128)S(1)}, f32[16,192]{1,0:T(8,128)S(1)}, u32[]{:S(2)}, u32[]{:S(2)}) collective-permute-start(f32[16,192]{1,0:T(8,128)S(1)} %get-tuple-element.26), channel_id=1, source_target_pairs={{0,80},{8,88},{16,96},{24,104},{32,112},{40,120},{48,128},{56,136}... | collective-permute-start | bytes 36872
  824.6 18.3 %collective-permute-start.8 = (f32[16,192]{1,0:T(8,128)S(1)}, f32[16,192]{1,0:T(8,128)S(1)}, u32[]{:S(2)}, u32[]{:S(2)}) collective-permute-start(f32[16,192]{1,0:T(8,128)S(1)} %get-tuple-element.26), channel_id=1, source_target_pairs={{0,72},{8,80},{16,88},{24,96},{32,104},{40,112},{48,120},{56,128},... | collective-permute-start | bytes 36872
  828.7 15.5 %collective-permute-start.7 = (f32[16,192]{1,0:T(8,128)S(1)}, f32[16,192]{1,0:T(8,128)S(1)}, u32[]{:S(2)}, u32[]{:S(2)}) collective-permute-start(f32[16,192]{1,0:T(8,128)S(1)} %get-tuple-element.26), channel_id=1, source_target_pairs={{0,64},{8,72},{16,80},{24,88},{32,96},{40,104},{48,112},{56,120},{... | collective-permute-start | bytes 36872
  833.4 15.6 %collective-permute-start.5 = (f32[16,192]{1,0:T(8,128)S(1)}, f32[16,192]{1,0:T(8,128)S(1)}, u32[]{:S(2)}, u32[]{:S(2)}) collective-permute-start(f32[16,192]{1,0:T(8,128)S(1)} %get-tuple-element.26), channel_id=1, source_target_pairs={{0,48},{8,56},{16,64},{24,72},{32,80},{40,88},{48,96},{56,104},{64... | collective-permute-start | bytes 36872
  837.8 16.5 %collective-permute-start.4 = (f32[16,192]{1,0:T(8,128)S(1)}, f32[16,192]{1,0:T(8,128)S(1)}, u32[]{:S(2)}, u32[]{:S(2)}) collective-permute-start(f32[16,192]{1,0:T(8,128)S(1)} %get-tuple-element.26), channel_id=1, source_target_pairs={{0,40},{8,48},{16,56},{24,64},{32,72},{40,80},{48,88},{56,96},{64,... | collective-permute-start | bytes 36872
  845.5 14.2 %collective-permute-start.1 = (f32[16,192]{1,0:T(8,128)S(1)}, f32[16,192]{1,0:T(8,128)S(1)}, u32[]{:S(2)}, u32[]{:S(2)}) collective-permute-start(f32[16,192]{1,0:T(8,128)S(1)} %get-tuple-element.26), channel_id=1, source_target_pairs={{0,16},{8,24},{16,32},{24,40},{32,48},{40,56},{48,64},{56,72},{64,... | collective-permute-start | bytes 36872
  858.1 14.4 %collective-permute-start.60 = (f32[16,192]{1,0:T(8,128)S(1)}, f32[16,192]{1,0:T(8,128)S(1)}, u32[]{:S(2)}, u32[]{:S(2)}) collective-permute-start(f32[16,192]{1,0:T(8,128)S(1)} %get-tuple-element.27), channel_id=1, source_target_pairs={{0,232},{8,240},{16,248},{24,256},{32,264},{40,272},{48,280},{56,2... | collective-permute-start | bytes 36872
  859.7 14.6 %collective-permute-start.59 = (f32[16,192]{1,0:T(8,128)S(1)}, f32[16,192]{1,0:T(8,128)S(1)}, u32[]{:S(2)}, u32[]{:S(2)}) collective-permute-start(f32[16,192]{1,0:T(8,128)S(1)} %get-tuple-element.27), channel_id=1, source_target_pairs={{0,224},{8,232},{16,240},{24,248},{32,256},{40,264},{48,272},{56,2... | collective-permute-start | bytes 36872
  861.1 15.0 %collective-permute-start.58 = (f32[16,192]{1,0:T(8,128)S(1)}, f32[16,192]{1,0:T(8,128)S(1)}, u32[]{:S(2)}, u32[]{:S(2)}) collective-permute-start(f32[16,192]{1,0:T(8,128)S(1)} %get-tuple-element.27), channel_id=1, source_target_pairs={{0,216},{8,224},{16,232},{24,240},{32,248},{40,256},{48,264},{56,2... | collective-permute-start | bytes 36872
  862.4 17.1 %collective-permute-start.57 = (f32[16,192]{1,0:T(8,128)S(1)}, f32[16,192]{1,0:T(8,128)S(1)}, u32[]{:S(2)}, u32[]{:S(2)}) collective-permute-start(f32[16,192]{1,0:T(8,128)S(1)} %get-tuple-element.27), channel_id=1, source_target_pairs={{0,208},{8,216},{16,224},{24,232},{32,240},{40,248},{48,256},{56,2... | collective-permute-start | bytes 36872
  864.3 18.6 %collective-permute-start.56 = (f32[16,192]{1,0:T(8,128)S(1)}, f32[16,192]{1,0:T(8,128)S(1)}, u32[]{:S(2)}, u32[]{:S(2)}) collective-permute-start(f32[16,192]{1,0:T(8,128)S(1)} %get-tuple-element.27), channel_id=1, source_target_pairs={{0,200},{8,208},{16,216},{24,224},{32,232},{40,240},{48,248},{56,2... | collective-permute-start | bytes 36872
  874.3 15.8 %collective-permute-start.54 = (f32[16,192]{1,0:T(8,128)S(1)}, f32[16,192]{1,0:T(8,128)S(1)}, u32[]{:S(2)}, u32[]{:S(2)}) collective-permute-start(f32[16,192]{1,0:T(8,128)S(1)} %get-tuple-element.27), channel_id=1, source_target_pairs={{0,184},{8,192},{16,200},{24,208},{32,216},{40,224},{48,232},{56,2... | collective-permute-start | bytes 36872
  876.1 20.8 %collective-permute-start.53 = (f32[16,192]{1,0:T(8,128)S(1)}, f32[16,192]{1,0:T(8,128)S(1)}, u32[]{:S(2)}, u32[]{:S(2)}) collective-permute-start(f32[16,192]{1,0:T(8,128)S(1)} %get-tuple-element.27), channel_id=1, source_target_pairs={{0,176},{8,184},{16,192},{24,200},{32,208},{40,216},{48,224},{56,2... | collective-permute-start | bytes 36872
  879.5 22.1 %collective-permute-start.52 = (f32[16,192]{1,0:T(8,128)S(1)}, f32[16,192]{1,0:T(8,128)S(1)}, u32[]{:S(2)}, u32[]{:S(2)}) collective-permute-start(f32[16,192]{1,0:T(8,128)S(1)} %get-tuple-element.27), channel_id=1, source_target_pairs={{0,168},{8,176},{16,184},{24,192},{32,200},{40,208},{48,216},{56,2... | collective-permute-start | bytes 36872
  882.9 20.0 %collective-permute-start.51 = (f32[16,192]{1,0:T(8,128)S(1)}, f32[16,192]{1,0:T(8,128)S(1)}, u32[]{:S(2)}, u32[]{:S(2)}) collective-permute-start(f32[16,192]{1,0:T(8,128)S(1)} %get-tuple-element.27), channel_id=1, source_target_pairs={{0,160},{8,168},{16,176},{24,184},{32,192},{40,200},{48,208},{56,2... | collective-permute-start | bytes 36872
  886.6 17.6 %collective-permute-start.50 = (f32[16,192]{1,0:T(8,128)S(1)}, f32[16,192]{1,0:T(8,128)S(1)}, u32[]{:S(2)}, u32[]{:S(2)}) collective-permute-start(f32[16,192]{1,0:T(8,128)S(1)} %get-tuple-element.27), channel_id=1, source_target_pairs={{0,152},{8,160},{16,168},{24,176},{32,184},{40,192},{48,200},{56,2... | collective-permute-start | bytes 36872
  890.1 17.4 %collective-permute-start.49 = (f32[16,192]{1,0:T(8,128)S(1)}, f32[16,192]{1,0:T(8,128)S(1)}, u32[]{:S(2)}, u32[]{:S(2)}) collective-permute-start(f32[16,192]{1,0:T(8,128)S(1)} %get-tuple-element.27), channel_id=1, source_target_pairs={{0,144},{8,152},{16,160},{24,168},{32,176},{40,184},{48,192},{56,2... | collective-permute-start | bytes 36872
  896.9 16.7 %collective-permute-start.48 = (f32[16,192]{1,0:T(8,128)S(1)}, f32[16,192]{1,0:T(8,128)S(1)}, u32[]{:S(2)}, u32[]{:S(2)}) collective-permute-start(f32[16,192]{1,0:T(8,128)S(1)} %get-tuple-element.27), channel_id=1, source_target_pairs={{0,136},{8,144},{16,152},{24,160},{32,168},{40,176},{48,184},{56,1... | collective-permute-start | bytes 36872
  904.2 15.7 %collective-permute-start.45 = (f32[16,192]{1,0:T(8,128)S(1)}, f32[16,192]{1,0:T(8,128)S(1)}, u32[]{:S(2)}, u32[]{:S(2)}) collective-permute-start(f32[16,192]{1,0:T(8,128)S(1)} %get-tuple-element.27), channel_id=1, source_target_pairs={{0,112},{8,120},{16,128},{24,136},{32,144},{40,152},{48,160},{56,1... | collective-permute-start | bytes 36872
  907.5 15.6 %collective-permute-start.44 = (f32[16,192]{1,0:T(8,128)S(1)}, f32[16,192]{1,0:T(8,128)S(1)}, u32[]{:S(2)}, u32[]{:S(2)}) collective-permute-start(f32[16,192]{1,0:T(8,128)S(1)} %get-tuple-element.27), channel_id=1, source_target_pairs={{0,104},{8,112},{16,120},{24,128},{32,136},{40,144},{48,152},{56,1... | collective-permute-start | bytes 36872
  916.2 15.7 %collective-permute-start.41 = (f32[16,192]{1,0:T(8,128)S(1)}, f32[16,192]{1,0:T(8,128)S(1)}, u32[]{:S(2)}, u32[]{:S(2)}) collective-permute-start(f32[16,192]{1,0:T(8,128)S(1)} %get-tuple-element.27), channel_id=1, source_target_pairs={{0,80},{8,88},{16,96},{24,104},{32,112},{40,120},{48,128},{56,136}... | collective-permute-start | bytes 36872
  919.9 16.8 %collective-permute-start.40 = (f32[16,192]{1,0:T(8,128)S(1)}, f32[16,192]{1,0:T(8,128)S(1)}, u32[]{:S(2)}, u32[]{:S(2)}) collective-permute-start(f32[16,192]{1,0:T(8,128)S(1)} %get-tuple-element.27), channel_id=1, source_target_pairs={{0,72},{8,80},{16,88},{24,96},{32,104},{40,112},{48,120},{56,128},... | collective-permute-start | bytes 36872
  923.1 16.1 %collective-permute-start.39 = (f32[16,192]{1,0:T(8,128)S(1)}, f32[16,192]{1,0:T(8,128)S(1)}, u32[]{:S(2)}, u32[]{:S(2)}) collective-permute-start(f32[16,192]{1,0:T(8,128)S(1)} %get-tuple-element.27), channel_id=1, source_target_pairs={{0,64},{8,72},{16,80},{24,88},{32,96},{40,104},{48,112},{56,120},{... | collective-permute-start | bytes 36872
  925.4 15.9 %collective-permute-start.38 = (f32[16,192]{1,0:T(8,128)S(1)}, f32[16,192]{1,0:T(8,128)S(1)}, u32[]{:S(2)}, u32[]{:S(2)}) collective-permute-start(f32[16,192]{1,0:T(8,128)S(1)} %get-tuple-element.27), channel_id=1, source_target_pairs={{0,56},{8,64},{16,72},{24,80},{32,88},{40,96},{48,104},{56,112},{6... | collective-permute-start | bytes 36872
  926.7 18.0 %collective-permute-start.37 = (f32[16,192]{1,0:T(8,128)S(1)}, f32[16,192]{1,0:T(8,128)S(1)}, u32[]{:S(2)}, u32[]{:S(2)}) collective-permute-start(f32[16,192]{1,0:T(8,128)S(1)} %get-tuple-element.27), channel_id=1, source_target_pairs={{0,48},{8,56},{16,64},{24,72},{32,80},{40,88},{48,96},{56,104},{64... | collective-permute-start | bytes 36872
  931.9 24.3 %collective-permute-start.36 = (f32[16,192]{1,0:T(8,128)S(1)}, f32[16,192]{1,0:T(8,128)S(1)}, u32[]{:S(2)}, u32[]{:S(2)}) collective-permute-start(f32[16,192]{1,0:T(8,128)S(1)} %get-tuple-element.27), channel_id=1, source_target_pairs={{0,40},{8,48},{16,56},{24,64},{32,72},{40,80},{48,88},{56,96},{64,... | collective-permute-start | bytes 36872
  936.7 19.5 %collective-permute-start.35 = (f32[16,192]{1,0:T(8,128)S(1)}, f32[16,192]{1,0:T(8,128)S(1)}, u32[]{:S(2)}, u32[]{:S(2)}) collective-permute-start(f32[16,192]{1,0:T(8,128)S(1)} %get-tuple-element.27), channel_id=1, source_target_pairs={{0,32},{8,40},{16,48},{24,56},{32,64},{40,72},{48,80},{56,88},{64,... | collective-permute-start | bytes 36872
  939.3 16.9 %collective-permute-start.34 = (f32[16,192]{1,0:T(8,128)S(1)}, f32[16,192]{1,0:T(8,128)S(1)}, u32[]{:S(2)}, u32[]{:S(2)}) collective-permute-start(f32[16,192]{1,0:T(8,128)S(1)} %get-tuple-element.27), channel_id=1, source_target_pairs={{0,24},{8,32},{16,40},{24,48},{32,56},{40,64},{48,72},{56,80},{64,... | collective-permute-start | bytes 36872
  941.3 15.0 %collective-permute-start.33 = (f32[16,192]{1,0:T(8,128)S(1)}, f32[16,192]{1,0:T(8,128)S(1)}, u32[]{:S(2)}, u32[]{:S(2)}) collective-permute-start(f32[16,192]{1,0:T(8,128)S(1)} %get-tuple-element.27), channel_id=1, source_target_pairs={{0,16},{8,24},{16,32},{24,40},{32,48},{40,56},{48,64},{56,72},{64,... | collective-permute-start | bytes 36872
  (27 other events, 605.6 us)
Sparse Core Ops, SparseCore 0:
  412.1 59.4 reduce-scatter.5
where the time goes:
time: 972 us; the launch traced here: 970 us
  blocking collectives  637 us (66%)
  starting transfers between devices  257 us (26%)
  waiting for transfers between devices  25.6 us (3%)
  local copies, waits for them, and re-layouts  20 us (2%)
  between operations  16 us (2%)
    unnamed x1, blocking collectives  317 us
    unnamed x64, starting transfers between devices  217 us
    all_gather x1, blocking collectives, body(): lax.all_gather(value_weight, 'dp', axis=0, tiled=True)  151 us
    all_gather x1, blocking collectives, body(): lax.all_gather(gate_weight, 'dp', axis=0, tiled=True)  145 us
    all_to_all x1, starting transfers between devices, body(): lax.all_to_all(send_live, 'dp', split_axis=0, concat_axis=0, tiled=True)  33.8 us
    all_to_all x1, waiting for transfers between devices, body(): lax.all_to_all(send_live, 'dp', split_axis=0, concat_axis=0, tiled=True)  25.4 us
    all_gather x1, blocking collectives, body(): whole = lax.all_gather(received_rows, 'mp', axis=2, tiled=True)  23.9 us
  transfers between devices with their start and end apart: 67, of which 1 were waited for; matrix products, arithmetic and copies ran while one was open for 34% of the time, Pallas kernels for 0%

commit v1 on v0

v1 whole, which is shorter than its diff:
```python
import jax
import jax.numpy as jnp
from jax import lax
from jax.experimental import pallas as pl
from jax.experimental.pallas import tpu as pltpu
from jax.sharding import Mesh, PartitionSpec as P

epsilon = 1e-05
bf16, f32, i32 = jnp.bfloat16, jnp.float32, jnp.int32
YC = ("yh", "co")
DP = ("z", "yh", "co")
MP = ("x", "yl")
INTERPRET = False


def nt(a, b):
    return lax.dot_general(a, b, (((1,), (1,)), ((), ())), preferred_element_type=f32)


def nn(a, b):
    return lax.dot_general(a, b, (((1,), (0,)), ((), ())), preferred_element_type=f32)


def tn(a, b):
    return lax.dot_general(a, b, (((0,), (0,)), ((), ())), preferred_element_type=f32)


def call(kernel, outs, *args, scratch=()):
    vmem = pl.BlockSpec(memory_space=pltpu.VMEM)
    return pl.pallas_call(
        kernel,
        in_specs=[vmem] * len(args),
        out_specs=[vmem] * len(outs),
        out_shape=[jax.ShapeDtypeStruct(s, d) for s, d in outs],
        scratch_shapes=list(scratch),
        interpret=INTERPRET,
    )(*args)


def natural_of(p):
    return ((p // 12) % 4) * 48 + (p // 48) * 12 + p % 12


def turn_kernel(rows_ref, out_ref, live_ref, *, width, peers):
    slots = 2 * peers
    lanes = rows_ref.shape[1]
    rows = rows_ref[...]
    place = lax.broadcasted_iota(i32, (width, lanes), 0)
    column = lax.broadcasted_iota(i32, (width, lanes), 1)
    pick = (column == natural_of(place)).astype(bf16)
    flag = (lax.broadcasted_iota(i32, (16, lanes), 1) == width).astype(bf16)
    source = lax.broadcasted_iota(i32, (slots, slots), 0)
    target = lax.broadcasted_iota(i32, (slots, slots), 1)
    order = (source == (target % peers) * 2 + target // peers).astype(bf16)
    turned = nt(jnp.concatenate([pick, flag], axis=0), rows).astype(bf16)
    ordered = nn(turned, order)
    out_ref[...] = ordered[:width].astype(bf16)
    live_ref[...] = ordered[width : width + 8]


def main_kernel(whole_ref, live_ref, gain_ref, w_ref, up_ref, gated_ref, dw_ref, partial_ref, normed_ref):
    blocks, width, slots = whole_ref.shape
    peers = slots // 2
    total = blocks * width
    live = live_ref[0:1, :]
    s = jnp.zeros((1, slots), f32)
    for m in range(blocks):
        s = s + jnp.sum(whole_ref[m].astype(f32), axis=0, keepdims=True)
    mean = s * (1.0 / total)
    s = jnp.zeros((1, slots), f32)
    for m in range(blocks):
        c = whole_ref[m].astype(f32) - mean
        s = s + jnp.sum(c * c, axis=0, keepdims=True)
    inv = lax.rsqrt(s * (1.0 / total) + epsilon)

    def w_block(m):
        return jnp.concatenate([w_ref[k, 48 * m : 48 * m + 48, :] for k in range(4)], axis=0)

    acc = jnp.zeros((2 * width, slots), f32)
    for m in range(blocks):
        c = whole_ref[m].astype(f32) - mean
        normed = (c * inv * gain_ref[m] * live).astype(bf16)
        normed_ref[m] = normed
        acc = acc + tn(w_block(m), normed)
    value, gate = acc[:width], acc[width:]
    sig = jax.nn.sigmoid(gate)
    up = jnp.concatenate([up_ref[0], up_ref[1]], axis=1).astype(f32)
    gated = (value * sig).astype(bf16)
    gated_ref[0] = gated[:, :peers]
    gated_ref[1] = gated[:, peers:]
    value_delta = (up * sig * live).astype(bf16)
    gate_delta = (up * value * sig * (1.0 - sig) * live).astype(bf16)
    delta = jnp.concatenate([value_delta, gate_delta], axis=0)
    for m in range(blocks):
        dw = nt(normed_ref[m], delta).astype(bf16)
        for k in range(4):
            dw_ref[k, 48 * m : 48 * m + 48, :] = dw[48 * k : 48 * k + 48]
        partial_ref[m] = nn(w_block(m), delta).astype(bf16)


def join_kernel(parts_ref, out_ref):
    blocks, width, slots = parts_ref.shape
    peers = slots // 2
    s = parts_ref[0].astype(f32)
    for m in range(1, blocks):
        s = s + parts_ref[m].astype(f32)
    place = lax.broadcasted_iota(i32, (width, width), 1)
    natural = lax.broadcasted_iota(i32, (width, width), 0)
    back = (natural_of(place) == natural).astype(bf16)
    out = nn(back, s.astype(bf16)).astype(bf16)
    out_ref[0] = out[:, :peers]
    out_ref[1] = out[:, peers:]


def spread(x, axis, count):
    return lax.all_to_all(jnp.broadcast_to(x[None], (count,) + x.shape), axis, 0, 0, tiled=True)


def body(frames, frame_owner, frame_valid, norm_gain, value_weight, gate_weight, grad_owned):
    z = lax.axis_size("z")
    blocks = lax.axis_size(MP)
    peers = 4 * z
    slots = 2 * peers
    rows, width = frames.shape
    group = value_weight.shape[0]
    lanes = -(-(width + 1) // 128) * 128

    shard = jnp.concatenate([value_weight, gate_weight], axis=1)
    w_z = spread(shard, "z", z)
    owner = frame_owner[:, 0]
    positions = jnp.arange(rows, dtype=i32)
    earlier = positions[None, :] < positions[:, None]
    same = owner[:, None] == owner[None, :]
    slot = jnp.sum((same & earlier).astype(i32), axis=1)
    targets = owner * 2 + slot
    placing = (jnp.arange(slots, dtype=i32)[:, None] == targets[None, :]).astype(bf16)
    flagged = jnp.concatenate(
        [frames, frame_valid.astype(bf16)[:, None], jnp.zeros((rows, lanes - width - 1), bf16)], axis=1
    )
    sent = jnp.dot(placing, flagged, preferred_element_type=f32).astype(bf16).reshape(peers, 2, lanes)
    got = lax.all_to_all(sent, DP, 0, 0, tiled=True).reshape(slots, lanes)
    turned, live = call(
        lambda *refs: turn_kernel(*refs, width=width, peers=peers),
        [((width, slots), bf16), ((8, slots), f32)],
        got,
    )
    whole = spread(turned, MP, blocks)
    w_full = spread(w_z.reshape(z * group, 2 * width), YC, 4)
    gain = norm_gain.reshape(blocks, 4, 4, 12).transpose(0, 2, 1, 3).reshape(blocks, width, 1)
    up = grad_owned.reshape(peers, 2, width).transpose(1, 2, 0)
    gated, dw, partial = call(
        main_kernel,
        [((2, width, peers), bf16), ((4, z * group, 2 * width), bf16), ((blocks, width, slots), bf16)],
        whole,
        live,
        gain,
        w_full,
        up,
        scratch=[pltpu.VMEM((blocks, width, slots), bf16)],
    )
    dw_yc = lax.all_to_all(dw, YC, 0, 0, tiled=True)
    dw_z = jnp.sum(dw_yc.astype(f32), axis=0).astype(bf16).reshape(z, group, 2 * width)
    dw_z = lax.all_to_all(dw_z, "z", 0, 0, tiled=True)
    parts = lax.all_to_all(partial, MP, 0, 0, tiled=True)
    (normed_grad,) = call(join_kernel, [((2, width, peers), bf16)], parts)
    scale = float(rows * peers) ** (-0.5)
    grads = jnp.sum(dw_z.astype(f32), axis=0) * scale

    def restore(x):
        return x.transpose(2, 0, 1).reshape(1, peers, 2, width)

    return (restore(gated), grads[:, :width], grads[:, width:], restore(normed_grad))


def solution(mesh):
    mp = mesh.shape["mp"]
    z = mesh.shape["dp"] // 4
    fine = Mesh(mesh.devices.reshape(z, 2, 2, mp // 2, 2), ("z", "yh", "co", "x", "yl"))
    slots = P(DP, None, None, MP)
    weights = P(DP, MP)
    return jax.shard_map(
        body,
        mesh=fine,
        in_specs=(P(DP, MP), P(DP, None), P(DP), P(), weights, weights, slots),
        out_specs=(slots, weights, weights, slots),
        check_vma=False,
    )
```

time: 972 us -> 272 us (0.28)
  blocking collectives: 637 us -> 20.8 us
  starting transfers between devices: 257 us -> 60.1 us
  waiting for transfers between devices: 25.6 us -> 163 us
  between operations: 16 us -> 0.74 us
  local copies, waits for them, and re-layouts: 20 us -> 9.37 us
  Pallas kernels: 0 us -> 9.78 us
    all_gather x3 -> x0, blocking collectives: 320 us -> none  [the longest x1 151 us: body(): lax.all_gather(value_weight, 'dp', axis=0, tiled=True)]
    unnamed x1 -> x0, blocking collectives: 317 us -> none
    unnamed x64 -> x0, starting transfers between devices: 217 us -> none
    all_to_all x2 -> x6, waiting for transfers between devices: 25.4 us -> 163 us  [the longest x3 74.3 us: spread(): lax.all_to_all(jnp.broadcast_to(x[None], (count,) + x.shape), axis, 0, 0,...]
    all_to_all x0 -> x1, blocking collectives: none -> 20.8 us  [body(): dw_yc = lax.all_to_all(dw, YC, 0, 0, tiled=True)]
    all_to_all x2 -> x6, starting transfers between devices: 39.5 us -> 60.1 us  [the longest x1 33.8 us: body(): got = lax.all_to_all(sent, DP, 0, 0, tiled=True).reshape(slots, lanes)]
    pallas_call x0 -> x3, Pallas kernels: none -> 9.78 us  [call(): pl.pallas_call(kernel, in_specs=[vmem] * len(args), out_specs=[vmem] * le...]
  transfers between devices with their start and end apart: 67 -> 6, of which waited for: 1 -> 6; matrix products, arithmetic and copies ran while one was open for 34% -> 1% of each run, Pallas kernels for 0% -> 1%
where the time goes in v1:
time: 272 us; the launch traced here: 269 us
  waiting for transfers between devices  163 us (60%)
  starting transfers between devices  60.1 us (22%)
  blocking collectives  20.8 us (8%)
  Pallas kernels  9.78 us (4%)
  local copies, waits for them, and re-layouts  9.37 us (3%)
  other arithmetic  3.48 us (1%)
    all_to_all x3, waiting for transfers between devices, spread(): lax.all_to_all(jnp.broadcast_to(x[None], (count,) + x.shape), axis, 0, 0,...  74.3 us
    all_to_all x1, waiting for transfers between devices, body(): dw_z = lax.all_to_all(dw_z, 'z', 0, 0, tiled=True)  48.7 us
    all_to_all x1, starting transfers between devices, body(): got = lax.all_to_all(sent, DP, 0, 0, tiled=True).reshape(slots, lanes)  33.8 us
    all_to_all x1, waiting for transfers between devices, body(): got = lax.all_to_all(sent, DP, 0, 0, tiled=True).reshape(slots, lanes)  29.7 us
    all_to_all x1, blocking collectives, body(): dw_yc = lax.all_to_all(dw, YC, 0, 0, tiled=True)  20.8 us
    all_to_all x3, starting transfers between devices, spread(): lax.all_to_all(jnp.broadcast_to(x[None], (count,) + x.shape), axis, 0, 0,...  18.9 us
    all_to_all x1, waiting for transfers between devices, body(): parts = lax.all_to_all(partial, MP, 0, 0, tiled=True)  10.4 us
    pallas_call x3, Pallas kernels, call(): pl.pallas_call(kernel, in_specs=[vmem] * len(args), out_specs=[vmem] * le...  9.78 us
  transfers between devices with their start and end apart: 6, of which 6 were waited for; matrix products, arithmetic and copies ran while one was open for 1% of the time, Pallas kernels for 1%

profile of v1, /device:TPU:1, one launch (start us, length us, event | category | flops | bytes accessed | tf_op | source)
XLA Modules:
  0.0 268.5 jit_solution(8632709496834465398)
XLA Ops:
  0.6 0.7 convert_element_type.16
  1.3 0.9 convert_reduce_fusion.1
  2.3 0.7 multiply_add_fusion
  2.9 0.1 broadcast_in_dim.35
  3.0 0.1 pad.4.clone
  3.1 1.1 convolution_convert_fusion
  4.3 0.7 reshape.44
  5.0 33.8 %all-to-all-start = ((bf16[128,2,256]{2,1,0:T(2,128)(2,1)}), bf16[128,2,256]{2,1,0:T(2,128)(2,1)S(1)}, u32[]{:S(2)}, u32[]{:S(2)}) async-start(bf16[128,2,256]{2,1,0:T(2,128)(2,1)} %reshape.44), calls=%async_computation | async-start | bytes 262144 | tf_op jit(solution)/shard_map/all_to_all | solution.py:141
  38.8 0.8 pad_maximum_fusion
  39.6 29.7 %all-to-all-done = bf16[128,2,256]{2,1,0:T(2,128)(2,1)S(1)} async-done(((bf16[128,2,256]{2,1,0:T(2,128)(2,1)}), bf16[128,2,256]{2,1,0:T(2,128)(2,1)S(1)}, u32[]{:S(2)}, u32[]{:S(2)}) %all-to-all-start) | async-done | bytes 131104 | tf_op jit(solution)/shard_map/all_to_all | solution.py:141
  69.3 0.8 broadcast_in_dim.15
  70.1 5.6 %all-to-all-start.2 = ((bf16[32,12,384]{2,1,0:T(8,128)(2,1)}), bf16[32,12,384]{2,1,0:T(8,128)(2,1)S(1)}, u32[]{:S(2)}, u32[]{:S(2)}) async-start(bf16[32,12,384]{2,1,0:T(8,128)(2,1)} %broadcast_in_dim.15), calls=%async_computation.2 | async-start | bytes 786432 | tf_op jit(solution)/shard_map/all_to_all | solution.py:116
  75.7 0.7 reshape.45.refs_0_
  76.4 1.9 shard_map.102
  78.3 49.5 %all-to-all-done.2 = bf16[32,12,384]{2,1,0:T(8,128)(2,1)S(1)} async-done(((bf16[32,12,384]{2,1,0:T(8,128)(2,1)}), bf16[32,12,384]{2,1,0:T(8,128)(2,1)S(1)}, u32[]{:S(2)}, u32[]{:S(2)}) %all-to-all-start.2) | async-done | bytes 294944 | tf_op jit(solution)/shard_map/all_to_all | solution.py:116
  127.8 1.8 broadcast_in_dim.14
  129.6 4.1 %all-to-all-start.1 = ((bf16[8,192,256]{2,1,0:T(8,128)(2,1)}), bf16[8,192,256]{2,1,0:T(8,128)(2,1)S(1)}, u32[]{:S(2)}, u32[]{:S(2)}) async-start(bf16[8,192,256]{2,1,0:T(8,128)(2,1)} %broadcast_in_dim.14), calls=%async_computation.1 | async-start | bytes 1572864 | tf_op jit(solution)/shard_map/all_to_all | solution.py:116
  133.8 0.1 broadcast_in_dim.16
  133.8 9.7 %all-to-all-done.1.whole_ref = bf16[8,192,256]{2,1,0:T(8,128)(2,1)S(1)} async-done(((bf16[8,192,256]{2,1,0:T(8,128)(2,1)}), bf16[8,192,256]{2,1,0:T(8,128)(2,1)S(1)}, u32[]{:S(2)}, u32[]{:S(2)}) %all-to-all-start.1) | async-done | bytes 786464 | tf_op jit(solution)/shard_map/all_to_all | solution.py:116
  143.5 0.0 copy-start.2
  143.5 1.2 broadcast_in_dim.34
  144.8 0.0 copy-start.3
  144.8 0.1 copy-done.2
  144.8 9.2 %all-to-all-start.3 = ((bf16[4,384,384]{2,1,0:T(8,128)(2,1)}), bf16[4,384,384]{2,1,0:T(8,128)(2,1)S(1)}, u32[]{:S(2)}, u32[]{:S(2)}) async-start(bf16[4,384,384]{2,1,0:T(8,128)(2,1)} %broadcast_in_dim.34), calls=%async_computation.3 | async-start | bytes 2359296 | tf_op jit(solution)/shard_map/all_to_all | solution.py:116
  154.0 0.0 copy-done.3
  154.0 0.1 reshape.46
  154.2 1.2 reshape.52.gain_ref
  155.3 15.1 %all-to-all-done.3.w_ref = bf16[4,384,384]{2,1,0:T(8,128)(2,1)S(1)} async-done(((bf16[4,384,384]{2,1,0:T(8,128)(2,1)}), bf16[4,384,384]{2,1,0:T(8,128)(2,1)S(1)}, u32[]{:S(2)}, u32[]{:S(2)}) %all-to-all-start.3) | async-done | bytes 1179680 | tf_op jit(solution)/shard_map/all_to_all | solution.py:116
  170.4 0.0 copy-start
  170.4 1.0 copy-done
  171.4 5.8 %shard_map.103 = (bf16[2,192,128]{2,1,0:T(8,128)(2,1)}, bf16[4,384,384]{2,1,0:T(8,128)(2,1)}, bf16[8,192,256]{2,1,0:T(8,128)(2,1)}) custom-call(bf16[8,192,256]{2,1,0:T(8,128)(2,1)} %copy-done.2, f32[8,256]{1,0:T(8,128)} %get-tuple-element.10.live_ref, f32[8,192,1]{2,1,0:T(8,128)} %reshape.52.gain_ref, bf16[4,384,384]{2,1,0:T(8,128)(2,1)} %copy-done, ...), custom_call_target="tpu_custom_call" | custom-call | tf_op jit(solution)/shard_map/pallas_call | solution.py:30
  177.3 20.8 %all_to_all.35 = bf16[4,384,384]{2,1,0:T(8,128)(2,1)S(1)} all-to-all(bf16[4,384,384]{2,1,0:T(8,128)(2,1)} %get-tuple-element.12), channel_id=1, replica_groups=mesh['z'=32,'yh'=2,'co'=2,'x'=4,'yl'=2] {'yh','co'}, dimensions={0} | all-to-all | bytes 2359296 | tf_op jit(solution)/shard_map/all_to_all | solution.py:161
  198.0 3.5 %all-to-all-start.6 = ((bf16[8,192,256]{2,1,0:T(8,128)(2,1)}), bf16[8,192,256]{2,1,0:T(8,128)(2,1)S(1)}, u32[]{:S(2)}, u32[]{:S(2)}) async-start(bf16[8,192,256]{2,1,0:T(8,128)(2,1)} %get-tuple-element.13), calls=%async_computation.6 | async-start | bytes 1572864 | tf_op jit(solution)/shard_map/all_to_all | solution.py:164
  201.6 0.3 reduce_sum.31
  201.9 0.8 reshape.50
  202.7 10.4 %all-to-all-done.6.parts_ref = bf16[8,192,256]{2,1,0:T(8,128)(2,1)S(1)} async-done(((bf16[8,192,256]{2,1,0:T(8,128)(2,1)}), bf16[8,192,256]{2,1,0:T(8,128)(2,1)S(1)}, u32[]{:S(2)}, u32[]{:S(2)}) %all-to-all-start.6) | async-done | bytes 786464 | tf_op jit(solution)/shard_map/all_to_all | solution.py:164
  213.1 0.0 copy-start.1
  213.1 3.9 %all-to-all-start.5 = ((bf16[32,12,384]{2,1,0:T(8,128)(2,1)}), bf16[32,12,384]{2,1,0:T(8,128)(2,1)S(1)}, u32[]{:S(2)}, u32[]{:S(2)}) async-start(bf16[32,12,384]{2,1,0:T(8,128)(2,1)} %reshape.50), calls=%async_computation.5 | async-start | bytes 786432 | tf_op jit(solution)/shard_map/all_to_all | solution.py:163
  217.0 0.0 copy-done.1
  217.0 2.0 shard_map.104
  219.0 48.7 %all-to-all-done.5 = bf16[32,12,384]{2,1,0:T(8,128)(2,1)S(1)} async-done(((bf16[32,12,384]{2,1,0:T(8,128)(2,1)}), bf16[32,12,384]{2,1,0:T(8,128)(2,1)S(1)}, u32[]{:S(2)}, u32[]{:S(2)}) %all-to-all-start.5) | async-done | bytes 294944 | tf_op jit(solution)/shard_map/all_to_all | solution.py:163
  267.7 0.1 convert_reduce_fusion
  267.8 0.7 fusion.8
  (3 shorter events, 0.0 us)
Async XLA Ops:
  5.0 64.3 %all-to-all-start = ((bf16[128,2,256]{2,1,0:T(2,128)(2,1)}), bf16[128,2,256]{2,1,0:T(2,128)(2,1)S(1)}, u32[]{:S(2)}, u32[]{:S(2)}) async-start(bf16[128,2,256]{2,1,0:T(2,128)(2,1)} %reshape.44), calls=%async_computation | async-start | bytes 262144 | tf_op jit(solution)/shard_map/all_to_all | solution.py:141
  70.1 57.7 %all-to-all-start.2 = ((bf16[32,12,384]{2,1,0:T(8,128)(2,1)}), bf16[32,12,384]{2,1,0:T(8,128)(2,1)S(1)}, u32[]{:S(2)}, u32[]{:S(2)}) async-start(bf16[32,12,384]{2,1,0:T(8,128)(2,1)} %broadcast_in_dim.15), calls=%async_computation.2 | async-start | bytes 786432 | tf_op jit(solution)/shard_map/all_to_all | solution.py:116
  129.6 13.9 %all-to-all-start.1 = ((bf16[8,192,256]{2,1,0:T(8,128)(2,1)}), bf16[8,192,256]{2,1,0:T(8,128)(2,1)S(1)}, u32[]{:S(2)}, u32[]{:S(2)}) async-start(bf16[8,192,256]{2,1,0:T(8,128)(2,1)} %broadcast_in_dim.14), calls=%async_computation.1 | async-start | bytes 1572864 | tf_op jit(solution)/shard_map/all_to_all | solution.py:116
  143.5 1.3 copy-start.2
  144.8 9.3 %copy-start.3 = (f32[1536]{0:T(1024)S(1)}, f32[1536]{0:T(1024)}, u32[]{:S(2)}) copy-start(f32[1536]{0:T(1024)} %param.10) | copy-start | bytes 18436
  144.8 25.6 %all-to-all-start.3 = ((bf16[4,384,384]{2,1,0:T(8,128)(2,1)}), bf16[4,384,384]{2,1,0:T(8,128)(2,1)S(1)}, u32[]{:S(2)}, u32[]{:S(2)}) async-start(bf16[4,384,384]{2,1,0:T(8,128)(2,1)} %broadcast_in_dim.34), calls=%async_computation.3 | async-start | bytes 2359296 | tf_op jit(solution)/shard_map/all_to_all | solution.py:116
  170.4 1.0 copy-start
  198.0 15.1 %all-to-all-start.6 = ((bf16[8,192,256]{2,1,0:T(8,128)(2,1)}), bf16[8,192,256]{2,1,0:T(8,128)(2,1)S(1)}, u32[]{:S(2)}, u32[]{:S(2)}) async-start(bf16[8,192,256]{2,1,0:T(8,128)(2,1)} %get-tuple-element.13), calls=%async_computation.6 | async-start | bytes 1572864 | tf_op jit(solution)/shard_map/all_to_all | solution.py:164
  213.1 3.9 %copy-start.1 = (bf16[8,192,256]{2,1,0:T(8,128)(2,1)}, bf16[8,192,256]{2,1,0:T(8,128)(2,1)S(1)}, u32[]{:S(2)}) copy-start(bf16[8,192,256]{2,1,0:T(8,128)(2,1)S(1)} %all-to-all-done.6.parts_ref) | copy-start | bytes 2359300
  213.1 54.6 %all-to-all-start.5 = ((bf16[32,12,384]{2,1,0:T(8,128)(2,1)}), bf16[32,12,384]{2,1,0:T(8,128)(2,1)S(1)}, u32[]{:S(2)}, u32[]{:S(2)}) async-start(bf16[32,12,384]{2,1,0:T(8,128)(2,1)} %reshape.50), calls=%async_computation.5 | async-start | bytes 786432 | tf_op jit(solution)/shard_map/all_to_all | solution.py:163

commit v2 on v1

v2 whole, which is shorter than its diff:
```python
import jax
import jax.numpy as jnp
from jax import lax
from jax.experimental import pallas as pl
from jax.experimental.pallas import tpu as pltpu
from jax.sharding import Mesh, PartitionSpec as P


epsilon = 1e-05
bf16, f32, i32 = jnp.bfloat16, jnp.float32, jnp.int32
YC = ("yh", "co")
DP = ("z", "yh", "co")
MP = ("x", "yl")
INTERPRET = False


def nt(a, b):
    return lax.dot_general(a, b, (((1,), (1,)), ((), ())), preferred_element_type=f32)


def nn(a, b):
    return lax.dot_general(a, b, (((1,), (0,)), ((), ())), preferred_element_type=f32)


def tn(a, b):
    return lax.dot_general(a, b, (((0,), (0,)), ((), ())), preferred_element_type=f32)


def call(kernel, outs, *args, limit=12):
    vmem = pl.BlockSpec(memory_space=pltpu.VMEM)
    smem = pl.BlockSpec(memory_space=pltpu.SMEM)
    return pl.pallas_call(
        kernel,
        in_specs=[smem if a.shape == (1,) else vmem for a in args],
        out_specs=[vmem] * len(outs),
        out_shape=[jax.ShapeDtypeStruct(s, d) for s, d in outs],
        compiler_params=pltpu.CompilerParams(vmem_limit_bytes=limit << 20),
        interpret=INTERPRET,
    )(*args)


def natural_of(p):
    return ((p // 12) % 4) * 48 + (p // 48) * 12 + p % 12


def turn_kernel(rows_ref, out_ref, live_ref, *, width, z):
    slots, lanes = rows_ref.shape
    peers = slots // 2
    rows = rows_ref[...]
    place = lax.broadcasted_iota(i32, (width, lanes), 0)
    column = lax.broadcasted_iota(i32, (width, lanes), 1)
    pick = (column == natural_of(place)).astype(bf16)
    flag = (lax.broadcasted_iota(i32, (16, lanes), 1) == width).astype(bf16)
    source = lax.broadcasted_iota(i32, (slots, slots), 0)
    target = lax.broadcasted_iota(i32, (slots, slots), 1)
    loader = target % peers
    order = (source == ((loader % 4) * z + loader // 4) * 2 + target // peers).astype(bf16)
    turned = nt(jnp.concatenate([pick, flag], axis=0), rows).astype(bf16)
    ordered = nn(turned, order)
    out_ref[...] = ordered[:width].astype(bf16)
    live_ref[...] = ordered[width : width + 8]


def block_of(own_ref, k, blocks):
    x, y = own_ref[0] // 2, own_ref[0] % 2
    return ((x + (blocks // 2 - k // 2)) % (blocks // 2)) * 2 + (y + k) % 2


def norm_kernel(own_ref, live_ref, gain_ref, *refs):
    normed_ref = refs[-1]
    blocks, width, slots = normed_ref.shape
    total = blocks * width
    live = live_ref[0:1, :]
    s = jnp.zeros((1, slots), f32)
    for k in range(blocks):
        s = s + jnp.sum(refs[k][...].astype(f32), axis=0, keepdims=True)
    mean = s * (1.0 / total)
    s = jnp.zeros((1, slots), f32)
    for k in range(blocks):
        c = refs[k][...].astype(f32) - mean
        s = s + jnp.sum(c * c, axis=0, keepdims=True)
    inv = lax.rsqrt(s * (1.0 / total) + epsilon)
    for k in range(blocks):
        c = refs[k][...].astype(f32) - mean
        normed_ref[k] = (c * inv * gain_ref[block_of(own_ref, k, blocks)] * live).astype(bf16)


def part_of(m):
    return pl.ds(pl.multiple_of(48 * m, 16), 48)


def w_block(w_ref, m):
    return jnp.concatenate([w_ref[j, part_of(m), :] for j in range(4)], axis=0)


def forward_kernel(own_ref, normed_ref, live_ref, w_ref, up_ref, gated_ref, dw_ref, delta_ref):
    blocks, width, slots = normed_ref.shape
    peers = slots // 2
    live = live_ref[0:1, :]
    acc = jnp.zeros((2 * width, slots), f32)
    for k in range(blocks):
        acc = acc + tn(w_block(w_ref, block_of(own_ref, k, blocks)), normed_ref[k])
    value, gate = acc[:width], acc[width:]
    sig = jax.nn.sigmoid(gate)
    up = jnp.concatenate([up_ref[0], up_ref[1]], axis=1).astype(f32)
    gated = (value * sig).astype(bf16)
    gated_ref[0] = gated[:, :peers]
    gated_ref[1] = gated[:, peers:]
    value_delta = (up * sig * live).astype(bf16)
    gate_delta = (up * value * sig * (1.0 - sig) * live).astype(bf16)
    delta = jnp.concatenate([value_delta, gate_delta], axis=0)
    delta_ref[...] = delta
    for k in range(blocks):
        dw = nt(normed_ref[k], delta).astype(bf16)
        m = block_of(own_ref, k, blocks)
        for j in range(4):
            dw_ref[j, part_of(m), :] = dw[48 * j : 48 * j + 48]


def backward_kernel(own_ref, w_ref, delta_ref, *partial_refs):
    blocks = len(partial_refs)
    for k in range(blocks):
        partial_refs[k][...] = nn(w_block(w_ref, block_of(own_ref, k, blocks)), delta_ref[...]).astype(bf16)


def join_kernel(*refs):
    out_ref = refs[-1]
    width, slots = refs[0].shape
    peers = slots // 2
    s = refs[0][...].astype(f32)
    for ref in refs[1:-1]:
        s = s + ref[...].astype(f32)
    place = lax.broadcasted_iota(i32, (width, width), 1)
    natural = lax.broadcasted_iota(i32, (width, width), 0)
    back = (natural_of(place) == natural).astype(bf16)
    out = nn(back, s.astype(bf16)).astype(bf16)
    out_ref[0] = out[:, :peers]
    out_ref[1] = out[:, peers:]


def spread(x, axis, count):
    return lax.all_to_all(jnp.broadcast_to(x[None], (count,) + x.shape), axis, 0, 0, tiled=True)


def hop(x, k, blocks, back):
    n = blocks // 2
    pairs = []
    for i in range(blocks):
        j = ((i // 2 + k // 2) % n) * 2 + (i % 2 + k) % 2
        pairs.append((j, i) if back else (i, j))
    return lax.ppermute(x, MP, pairs)


def tiles(x):
    return x.reshape(x.shape[0] // 4, 4, x.shape[1] // 128, 128).transpose(2, 0, 1, 3)


def body(frames, frame_owner, frame_valid, norm_gain, value_weight, gate_weight, grad_owned):
    z = lax.axis_size("z")
    blocks = lax.axis_size(MP)
    peers = 4 * z
    slots = 2 * peers
    rows, width = frames.shape
    group = value_weight.shape[0]
    columns = 2 * width
    wt = columns // 128 * group // 4
    lanes = -(-(width + 1) // 128) * 128
    halves = lanes // 128
    own = lax.axis_index(MP).astype(i32).reshape(1)

    shard = tiles(jnp.concatenate([value_weight, gate_weight], axis=1)).reshape(wt, 4, 128)
    owner = frame_owner[:, 0]
    positions = jnp.arange(rows, dtype=i32)
    earlier = positions[None, :] < positions[:, None]
    same = owner[:, None] == owner[None, :]
    slot = jnp.sum((same & earlier).astype(i32), axis=1)
    targets = owner * 2 + slot
    placing = (jnp.arange(slots, dtype=i32)[:, None] == targets[None, :]).astype(bf16)
    flagged = jnp.concatenate(
        [frames, frame_valid.astype(bf16)[:, None], jnp.zeros((rows, lanes - width - 1), bf16)], axis=1
    )
    sent = jnp.dot(placing, flagged, preferred_element_type=f32).astype(bf16)
    sent = sent.reshape(z, 2, 4, halves, 128).transpose(0, 3, 1, 2, 4).reshape(z, 2 * halves, 4, 128)
    sent = jnp.concatenate([jnp.broadcast_to(shard[None], (z,) + shard.shape), sent], axis=1)
    got = lax.all_to_all(sent, "z", 0, 0, tiled=True)
    rows_z = got[:, wt:].reshape(z, halves, 4, 2, 128).transpose(2, 0, 3, 1, 4).reshape(4, 2 * z, lanes)
    rows_y = lax.all_to_all(rows_z, YC, 0, 0, tiled=True)
    w_rows = got[:, :wt].reshape(z, columns // 128, group, 128).transpose(0, 2, 1, 3)
    w_rows = w_rows.reshape(z * group, columns)
    w_full = spread(w_rows, YC, 4)
    turned, live = call(
        lambda *refs: turn_kernel(*refs, width=width, z=z),
        [((width, slots), bf16), ((8, slots), f32)],
        rows_y.reshape(slots, lanes),
    )
    whole = [turned] + [hop(turned, k, blocks, False) for k in range(1, blocks)]
    gain = norm_gain.reshape(blocks, 4, 4, 12).transpose(0, 2, 1, 3).reshape(blocks, width, 1)
    (normed,) = call(norm_kernel, [((blocks, width, slots), bf16)], own, live, gain, *whole)
    up = grad_owned.reshape(peers, 2, width).transpose(1, 2, 0)
    gated, dw, delta = call(
        forward_kernel,
        [((2, width, peers), bf16), ((4, z * group, columns), bf16), ((columns, slots), bf16)],
        own,
        normed,
        live,
        w_full,
        up,
    )
    dw_y = lax.all_to_all(dw, YC, 0, 0, tiled=True)
    partial = call(backward_kernel, [((width, slots), bf16)] * blocks, own, w_full, delta)
    dw_y = jnp.sum(dw_y.astype(f32), axis=0).astype(bf16)
    dw_y = dw_y.reshape(z, group, columns // 128, 128).transpose(0, 2, 1, 3).reshape(z, wt, 4, 128)
    dw_z = lax.all_to_all(dw_y, "z", 0, 0, tiled=True)
    parts = [partial[0]] + [hop(partial[k], k, blocks, True) for k in range(1, blocks)]
    (normed_grad,) = call(join_kernel, [((2, width, peers), bf16)], *parts)
    scale = float(rows * peers) ** (-0.5)
    grads = jnp.sum(dw_z.astype(f32), axis=0) * scale
    grads = grads.reshape(columns // 128, group, 128).transpose(1, 0, 2).reshape(group, columns)

    def restore(x):
        return x.transpose(2, 0, 1).reshape(1, peers, 2, width)

    return (restore(gated), grads[:, :width], grads[:, width:], restore(normed_grad))


def solution(mesh):
    mp = mesh.shape["mp"]
    z = mesh.shape["dp"] // 4
    fine = Mesh(mesh.devices.reshape(z, 2, 2, mp // 2, 2), ("z", "yh", "co", "x", "yl"))
    slots = P(DP, None, None, MP)
    weights = P(DP, MP)
    return jax.shard_map(
        body,
        mesh=fine,
        in_specs=(P(DP, MP), P(DP, None), P(DP), P(), weights, weights, slots),
        out_specs=(slots, weights, weights, slots),
        check_vma=False,
    )
```

time: 272 us -> 215 us (0.79)
  waiting for transfers between devices: 163 us -> 26 us
  blocking collectives: 20.8 us -> 108 us
  Pallas kernels: 9.78 us -> 5.06 us
    all_to_all x1 -> x2, blocking collectives: 20.8 us -> 108 us  [the longest x1 84.4 us: body(): got = lax.all_to_all(sent, 'z', 0, 0, tiled=True)]
    all_to_all x3 -> x1, waiting for transfers between devices: 74.3 us -> 0.01 us  [spread(): lax.all_to_all(jnp.broadcast_to(x[None], (count,) + x.shape), axis, 0, 0,...]
    all_to_all x3 -> x2, waiting for transfers between devices: 88.8 us -> 18.7 us  [the longest x1 14.1 us: body(): dw_z = lax.all_to_all(dw_y, 'z', 0, 0, tiled=True)]
    ppermute x0 -> x14, starting transfers between devices: none -> 45.2 us  [hop(): return lax.ppermute(x, MP, pairs)]
    all_to_all x3 -> x2, starting transfers between devices: 41.2 us -> 10.4 us  [the longest x1 6.57 us: body(): rows_y = lax.all_to_all(rows_z, YC, 0, 0, tiled=True)]
    all_to_all x3 -> x1, starting transfers between devices: 18.9 us -> 4.67 us  [spread(): lax.all_to_all(jnp.broadcast_to(x[None], (count,) + x.shape), axis, 0, 0,...]
    ppermute x0 -> x14, waiting for transfers between devices: none -> 7.29 us  [hop(): return lax.ppermute(x, MP, pairs)]
    pallas_call x3 -> x5, Pallas kernels: 9.78 us -> 5.06 us  [call(): pl.pallas_call(kernel, in_specs=[smem if a.shape == (1,) else vmem for a...]
  transfers between devices with their start and end apart: 6 -> 17, of which waited for: 6 -> 6; matrix products, arithmetic and copies ran while one was open for 1% -> 0% of each run, Pallas kernels for 1% -> 1%
where the time goes in v2:
time: 215 us; the launch traced here: 213 us
  blocking collectives  108 us (50%)
  starting transfers between devices  60.3 us (28%)
  waiting for transfers between devices  26 us (12%)
  local copies, waits for them, and re-layouts  6.85 us (3%)
  Pallas kernels  5.06 us (2%)
  other arithmetic  3.82 us (2%)
    all_to_all x1, blocking collectives, body(): got = lax.all_to_all(sent, 'z', 0, 0, tiled=True)  84.4 us
    ppermute x14, starting transfers between devices, hop(): return lax.ppermute(x, MP, pairs)  45.2 us
    all_to_all x1, blocking collectives, body(): dw_y = lax.all_to_all(dw, YC, 0, 0, tiled=True)  24 us
    all_to_all x1, waiting for transfers between devices, body(): dw_z = lax.all_to_all(dw_y, 'z', 0, 0, tiled=True)  14.1 us
    ppermute x14, waiting for transfers between devices, hop(): return lax.ppermute(x, MP, pairs)  7.29 us
    all_to_all x1, starting transfers between devices, body(): rows_y = lax.all_to_all(rows_z, YC, 0, 0, tiled=True)  6.57 us
    pallas_call x5, Pallas kernels, call(): pl.pallas_call(kernel, in_specs=[smem if a.shape == (1,) else vmem for a...  5.06 us
    all_to_all x1, starting transfers between devices, spread(): lax.all_to_all(jnp.broadcast_to(x[None], (count,) + x.shape), axis, 0, 0,...  4.67 us
  transfers between devices with their start and end apart: 17, of which 6 were waited for; matrix products, arithmetic and copies ran while one was open for 0% of the time, Pallas kernels for 1%

profile of v2, /device:TPU:1, one launch (start us, length us, event | category | flops | bytes accessed | tf_op | source)
XLA Modules:
  0.0 212.7 jit_solution(15135324295121538576)
XLA Ops:
  0.6 0.7 convert_element_type.16
  1.3 0.9 convert_reduce_fusion.1
  2.3 0.7 multiply_add_fusion
  2.9 0.8 pad_maximum_fusion.1
  3.9 1.1 convolution_convert_fusion
  5.3 0.3 pad_maximum_fusion
  5.6 84.4 %all_to_all.25 = bf16[32,13,4,128]{3,2,1,0:T(4,128)(2,1)S(1)} all-to-all(bf16[32,13,4,128]{3,2,1,0:T(4,128)(2,1)S(1)} %pad_maximum_fusion), channel_id=1, replica_groups=mesh['z'=32,'yh'=2,'co'=2,'x'=4,'yl'=2] {'z'}, dimensions={0} | all-to-all | bytes 851968 | tf_op jit(solution)/shard_map/all_to_all | solution.py:185
  90.2 0.1 copy.45
  90.3 0.7 reshape.76
  91.0 6.6 %all-to-all-start.1 = ((bf16[4,64,256]{2,1,0:T(8,128)(2,1)}), bf16[4,64,256]{2,1,0:T(8,128)(2,1)S(1)}, u32[]{:S(2)}, u32[]{:S(2)}) async-start(bf16[4,64,256]{2,1,0:T(8,128)(2,1)} %reshape.76), calls=%async_computation.1 | async-start | bytes 262144 | tf_op jit(solution)/shard_map/all_to_all | solution.py:187
  97.8 0.3 copy.49
  98.1 4.6 %all-to-all-done.1 = bf16[4,64,256]{2,1,0:T(8,128)(2,1)S(1)} async-done(((bf16[4,64,256]{2,1,0:T(8,128)(2,1)}), bf16[4,64,256]{2,1,0:T(8,128)(2,1)S(1)}, u32[]{:S(2)}, u32[]{:S(2)}) %all-to-all-start.1) | async-done | bytes 131104 | tf_op jit(solution)/shard_map/all_to_all | solution.py:187
  102.7 1.2 broadcast_in_dim.29
  103.8 4.7 %all-to-all-start.2 = ((bf16[4,384,384]{2,1,0:T(8,128)(2,1)}), bf16[4,384,384]{2,1,0:T(8,128)(2,1)S(1)}, u32[]{:S(2)}, u32[]{:S(2)}) async-start(bf16[4,384,384]{2,1,0:T(8,128)(2,1)} %broadcast_in_dim.29), calls=%async_computation.2 | async-start | bytes 2359296 | tf_op jit(solution)/shard_map/all_to_all | solution.py:142
  108.5 0.3 shard_map.102
  108.9 4.5 %collective-permute-start.6 = (bf16[192,256]{1,0:T(8,128)(2,1)S(1)}, bf16[192,256]{1,0:T(8,128)(2,1)S(1)}, u32[]{:S(2)}, u32[]{:S(2)}) collective-permute-start(bf16[192,256]{1,0:T(8,128)(2,1)S(1)} %get-tuple-element.18.refs_0_), channel_id=1, source_target_pairs={{0,7},{1,6},{2,1},{3,0},{4,3},{5,2},{6,5},{7,4},{8,15},{9,14},{10,... | collective-permute-start | bytes 294920 | tf_op jit(solution)/shard_map/ppermute | solution.py:151
  113.4 2.5 %collective-permute-start.5 = (bf16[192,256]{1,0:T(8,128)(2,1)S(1)}, bf16[192,256]{1,0:T(8,128)(2,1)S(1)}, u32[]{:S(2)}, u32[]{:S(2)}) collective-permute-start(bf16[192,256]{1,0:T(8,128)(2,1)S(1)} %get-tuple-element.18.refs_0_), channel_id=1, source_target_pairs={{0,6},{1,7},{2,0},{3,1},{4,2},{5,3},{6,4},{7,5},{8,14},{9,15},{10,... | collective-permute-start | bytes 294920 | tf_op jit(solution)/shard_map/ppermute | solution.py:151
  115.8 2.9 %collective-permute-start.4 = (bf16[192,256]{1,0:T(8,128)(2,1)S(1)}, bf16[192,256]{1,0:T(8,128)(2,1)S(1)}, u32[]{:S(2)}, u32[]{:S(2)}) collective-permute-start(bf16[192,256]{1,0:T(8,128)(2,1)S(1)} %get-tuple-element.18.refs_0_), channel_id=1, source_target_pairs={{0,5},{1,4},{2,7},{3,6},{4,1},{5,0},{6,3},{7,2},{8,13},{9,12},{10,... | collective-permute-start | bytes 294920 | tf_op jit(solution)/shard_map/ppermute | solution.py:151
  118.8 4.7 %collective-permute-start.3 = (bf16[192,256]{1,0:T(8,128)(2,1)S(1)}, bf16[192,256]{1,0:T(8,128)(2,1)S(1)}, u32[]{:S(2)}, u32[]{:S(2)}) collective-permute-start(bf16[192,256]{1,0:T(8,128)(2,1)S(1)} %get-tuple-element.18.refs_0_), channel_id=1, source_target_pairs={{0,4},{1,5},{2,6},{3,7},{4,0},{5,1},{6,2},{7,3},{8,12},{9,13},{10,... | collective-permute-start | bytes 294920 | tf_op jit(solution)/shard_map/ppermute | solution.py:151
  123.4 2.9 %collective-permute-start.2 = (bf16[192,256]{1,0:T(8,128)(2,1)S(1)}, bf16[192,256]{1,0:T(8,128)(2,1)S(1)}, u32[]{:S(2)}, u32[]{:S(2)}) collective-permute-start(bf16[192,256]{1,0:T(8,128)(2,1)S(1)} %get-tuple-element.18.refs_0_), channel_id=1, source_target_pairs={{0,3},{1,2},{2,5},{3,4},{4,7},{5,6},{6,1},{7,0},{8,11},{9,10},{10,... | collective-permute-start | bytes 294920 | tf_op jit(solution)/shard_map/ppermute | solution.py:151
  126.4 1.9 collective-permute-start.1
  128.3 3.0 %collective-permute-start = (bf16[192,256]{1,0:T(8,128)(2,1)S(1)}, bf16[192,256]{1,0:T(8,128)(2,1)S(1)}, u32[]{:S(2)}, u32[]{:S(2)}) collective-permute-start(bf16[192,256]{1,0:T(8,128)(2,1)S(1)} %get-tuple-element.18.refs_0_), channel_id=1, source_target_pairs={{0,1},{1,0},{2,3},{3,2},{4,5},{5,4},{6,7},{7,6},{8,9},{9,8},{10,11... | collective-permute-start | bytes 294920 | tf_op jit(solution)/shard_map/ppermute | solution.py:151
  131.5 0.3 reshape.87.gain_ref
  131.8 1.2 collective-permute-done.1.refs_2_
  132.9 0.7 collective-permute-done.refs_1_
  133.7 0.6 copy-done.1
  134.3 0.9 copy-done.2
  135.2 0.7 shard_map.103.normed_ref
  135.9 0.2 copy-done
  136.1 2.5 %shard_map.104 = (bf16[2,192,128]{2,1,0:T(8,128)(2,1)}, bf16[4,384,384]{2,1,0:T(8,128)(2,1)S(1)}, bf16[384,256]{1,0:T(8,128)(2,1)S(1)}) custom-call(s32[1]{0:T(128)} %bitcast.own_ref, bf16[8,192,256]{2,1,0:T(8,128)(2,1)S(1)} %shard_map.103.normed_ref, f32[8,256]{1,0:T(8,128)S(1)} %get-tuple-element.17.live_ref, ...), custom_call_target="tpu_custom_call" | custom-call | tf_op jit(solution)/shard_map/pallas_call | solution.py:32
  138.6 24.0 %all_to_all.26 = bf16[4,384,384]{2,1,0:T(8,128)(2,1)S(1)} all-to-all(bf16[4,384,384]{2,1,0:T(8,128)(2,1)S(1)} %get-tuple-element.20), channel_id=1, replica_groups=mesh['z'=32,'yh'=2,'co'=2,'x'=4,'yl'=2] {'yh','co'}, dimensions={0} | all-to-all | bytes 2359296 | tf_op jit(solution)/shard_map/all_to_all | solution.py:209
  162.7 0.3 reduce_sum.31
  163.2 0.9 copy.51
  164.0 3.9 %all-to-all-start.4 = ((bf16[32,9,4,128]{3,2,1,0:T(4,128)(2,1)}), bf16[32,9,4,128]{3,2,1,0:T(4,128)(2,1)S(1)}, u32[]{:S(2)}, u32[]{:S(2)}) async-start(bf16[32,9,4,128]{3,2,1,0:T(4,128)(2,1)} %copy.51), calls=%async_computation.4 | async-start | bytes 589824 | tf_op jit(solution)/shard_map/all_to_all | solution.py:213
  167.9 0.6 shard_map.105
  168.5 1.9 collective-permute-start.7
  170.4 4.9 %collective-permute-start.8 = (bf16[192,256]{1,0:T(8,128)(2,1)S(1)}, bf16[192,256]{1,0:T(8,128)(2,1)S(1)}, u32[]{:S(2)}, u32[]{:S(2)}) collective-permute-start(bf16[192,256]{1,0:T(8,128)(2,1)S(1)} %get-tuple-element.24), channel_id=1, source_target_pairs={{2,0},{3,1},{4,2},{5,3},{6,4},{7,5},{0,6},{1,7},{10,8},{11,9},{12,... | collective-permute-start | bytes 294920 | tf_op jit(solution)/shard_map/ppermute | solution.py:151
  175.3 3.6 %collective-permute-start.9 = (bf16[192,256]{1,0:T(8,128)(2,1)S(1)}, bf16[192,256]{1,0:T(8,128)(2,1)S(1)}, u32[]{:S(2)}, u32[]{:S(2)}) collective-permute-start(bf16[192,256]{1,0:T(8,128)(2,1)S(1)} %get-tuple-element.25), channel_id=1, source_target_pairs={{3,0},{2,1},{5,2},{4,3},{7,4},{6,5},{1,6},{0,7},{11,8},{10,9},{13,... | collective-permute-start | bytes 294920 | tf_op jit(solution)/shard_map/ppermute | solution.py:151
  178.9 1.9 collective-permute-start.10
  180.8 4.6 %collective-permute-start.11 = (bf16[192,256]{1,0:T(8,128)(2,1)S(1)}, bf16[192,256]{1,0:T(8,128)(2,1)S(1)}, u32[]{:S(2)}, u32[]{:S(2)}) collective-permute-start(bf16[192,256]{1,0:T(8,128)(2,1)S(1)} %get-tuple-element.27), channel_id=1, source_target_pairs={{5,0},{4,1},{7,2},{6,3},{1,4},{0,5},{3,6},{2,7},{13,8},{12,9},{15,... | collective-permute-start | bytes 294920 | tf_op jit(solution)/shard_map/ppermute | solution.py:151
  185.4 2.8 %collective-permute-start.12 = (bf16[192,256]{1,0:T(8,128)(2,1)S(1)}, bf16[192,256]{1,0:T(8,128)(2,1)S(1)}, u32[]{:S(2)}, u32[]{:S(2)}) collective-permute-start(bf16[192,256]{1,0:T(8,128)(2,1)S(1)} %get-tuple-element.28), channel_id=1, source_target_pairs={{6,0},{7,1},{0,2},{1,3},{2,4},{3,5},{4,6},{5,7},{14,8},{15,9},{8,1... | collective-permute-start | bytes 294920 | tf_op jit(solution)/shard_map/ppermute | solution.py:151
  188.3 3.1 %collective-permute-start.13 = (bf16[192,256]{1,0:T(8,128)(2,1)S(1)}, bf16[192,256]{1,0:T(8,128)(2,1)S(1)}, u32[]{:S(2)}, u32[]{:S(2)}) collective-permute-start(bf16[192,256]{1,0:T(8,128)(2,1)S(1)} %get-tuple-element.29), channel_id=1, source_target_pairs={{7,0},{6,1},{1,2},{0,3},{3,4},{2,5},{5,6},{4,7},{15,8},{14,9},{9,1... | collective-permute-start | bytes 294920 | tf_op jit(solution)/shard_map/ppermute | solution.py:151
  191.4 0.9 collective-permute-done.12.refs_6_
  192.3 4.5 %collective-permute-done.13.refs_7_ = bf16[192,256]{1,0:T(8,128)(2,1)S(1)} collective-permute-done((bf16[192,256]{1,0:T(8,128)(2,1)S(1)}, bf16[192,256]{1,0:T(8,128)(2,1)S(1)}, u32[]{:S(2)}, u32[]{:S(2)}) %collective-permute-start.13) | collective-permute-done | bytes 98336 | tf_op jit(solution)/shard_map/ppermute | solution.py:151
  196.8 0.9 shard_map.106
  197.7 14.1 %all-to-all-done.4 = bf16[32,9,4,128]{3,2,1,0:T(4,128)(2,1)S(1)} async-done(((bf16[32,9,4,128]{3,2,1,0:T(4,128)(2,1)}), bf16[32,9,4,128]{3,2,1,0:T(4,128)(2,1)S(1)}, u32[]{:S(2)}, u32[]{:S(2)}) %all-to-all-start.4) | async-done | bytes 294944 | tf_op jit(solution)/shard_map/all_to_all | solution.py:213
  211.8 0.1 convert_reduce_fusion
  212.0 0.7 fusion.8
  (39 shorter events, 1.1 us)
Async XLA Ops:
  91.0 11.6 %all-to-all-start.1 = ((bf16[4,64,256]{2,1,0:T(8,128)(2,1)}), bf16[4,64,256]{2,1,0:T(8,128)(2,1)S(1)}, u32[]{:S(2)}, u32[]{:S(2)}) async-start(bf16[4,64,256]{2,1,0:T(8,128)(2,1)} %reshape.76), calls=%async_computation.1 | async-start | bytes 262144 | tf_op jit(solution)/shard_map/all_to_all | solution.py:187
  103.8 27.5 %copy-start.3 = (f32[1536]{0:T(1024)S(1)}, f32[1536]{0:T(1024)}, u32[]{:S(2)}) copy-start(f32[1536]{0:T(1024)} %param.10) | copy-start | bytes 18436
  103.8 32.1 %all-to-all-start.2 = ((bf16[4,384,384]{2,1,0:T(8,128)(2,1)}), bf16[4,384,384]{2,1,0:T(8,128)(2,1)S(1)}, u32[]{:S(2)}, u32[]{:S(2)}) async-start(bf16[4,384,384]{2,1,0:T(8,128)(2,1)} %broadcast_in_dim.29), calls=%async_computation.2 | async-start | bytes 2359296 | tf_op jit(solution)/shard_map/all_to_all | solution.py:142
  108.9 17.5 %collective-permute-start.6 = (bf16[192,256]{1,0:T(8,128)(2,1)S(1)}, bf16[192,256]{1,0:T(8,128)(2,1)S(1)}, u32[]{:S(2)}, u32[]{:S(2)}) collective-permute-start(bf16[192,256]{1,0:T(8,128)(2,1)S(1)} %get-tuple-element.18.refs_0_), channel_id=1, source_target_pairs={{0,7},{1,6},{2,1},{3,0},{4,3},{5,2},{6,5},{7,4},{8,15},{9,14},{10,... | collective-permute-start | bytes 294920 | tf_op jit(solution)/shard_map/ppermute | solution.py:151
  113.4 14.9 %collective-permute-start.5 = (bf16[192,256]{1,0:T(8,128)(2,1)S(1)}, bf16[192,256]{1,0:T(8,128)(2,1)S(1)}, u32[]{:S(2)}, u32[]{:S(2)}) collective-permute-start(bf16[192,256]{1,0:T(8,128)(2,1)S(1)} %get-tuple-element.18.refs_0_), channel_id=1, source_target_pairs={{0,6},{1,7},{2,0},{3,1},{4,2},{5,3},{6,4},{7,5},{8,14},{9,15},{10,... | collective-permute-start | bytes 294920 | tf_op jit(solution)/shard_map/ppermute | solution.py:151
  115.8 15.9 %collective-permute-start.4 = (bf16[192,256]{1,0:T(8,128)(2,1)S(1)}, bf16[192,256]{1,0:T(8,128)(2,1)S(1)}, u32[]{:S(2)}, u32[]{:S(2)}) collective-permute-start(bf16[192,256]{1,0:T(8,128)(2,1)S(1)} %get-tuple-element.18.refs_0_), channel_id=1, source_target_pairs={{0,5},{1,4},{2,7},{3,6},{4,1},{5,0},{6,3},{7,2},{8,13},{9,12},{10,... | collective-permute-start | bytes 294920 | tf_op jit(solution)/shard_map/ppermute | solution.py:151
  118.8 13.0 %collective-permute-start.3 = (bf16[192,256]{1,0:T(8,128)(2,1)S(1)}, bf16[192,256]{1,0:T(8,128)(2,1)S(1)}, u32[]{:S(2)}, u32[]{:S(2)}) collective-permute-start(bf16[192,256]{1,0:T(8,128)(2,1)S(1)} %get-tuple-element.18.refs_0_), channel_id=1, source_target_pairs={{0,4},{1,5},{2,6},{3,7},{4,0},{5,1},{6,2},{7,3},{8,12},{9,13},{10,... | collective-permute-start | bytes 294920 | tf_op jit(solution)/shard_map/ppermute | solution.py:151
  123.4 8.4 %collective-permute-start.2 = (bf16[192,256]{1,0:T(8,128)(2,1)S(1)}, bf16[192,256]{1,0:T(8,128)(2,1)S(1)}, u32[]{:S(2)}, u32[]{:S(2)}) collective-permute-start(bf16[192,256]{1,0:T(8,128)(2,1)S(1)} %get-tuple-element.18.refs_0_), channel_id=1, source_target_pairs={{0,3},{1,2},{2,5},{3,4},{4,7},{5,6},{6,1},{7,0},{8,11},{9,10},{10,... | collective-permute-start | bytes 294920 | tf_op jit(solution)/shard_map/ppermute | solution.py:151
  126.4 6.6 %collective-permute-start.1 = (bf16[192,256]{1,0:T(8,128)(2,1)S(1)}, bf16[192,256]{1,0:T(8,128)(2,1)S(1)}, u32[]{:S(2)}, u32[]{:S(2)}) collective-permute-start(bf16[192,256]{1,0:T(8,128)(2,1)S(1)} %get-tuple-element.18.refs_0_), channel_id=1, source_target_pairs={{0,2},{1,3},{2,4},{3,5},{4,6},{5,7},{6,0},{7,1},{8,10},{9,11},{10,... | collective-permute-start | bytes 294920 | tf_op jit(solution)/shard_map/ppermute | solution.py:151
  128.3 5.4 %collective-permute-start = (bf16[192,256]{1,0:T(8,128)(2,1)S(1)}, bf16[192,256]{1,0:T(8,128)(2,1)S(1)}, u32[]{:S(2)}, u32[]{:S(2)}) collective-permute-start(bf16[192,256]{1,0:T(8,128)(2,1)S(1)} %get-tuple-element.18.refs_0_), channel_id=1, source_target_pairs={{0,1},{1,0},{2,3},{3,2},{4,5},{5,4},{6,7},{7,6},{8,9},{9,8},{10,11... | collective-permute-start | bytes 294920 | tf_op jit(solution)/shard_map/ppermute | solution.py:151
  133.7 0.6 copy-start.1
  134.3 0.9 copy-start.2
  135.2 0.9 copy-start
  164.0 47.8 %all-to-all-start.4 = ((bf16[32,9,4,128]{3,2,1,0:T(4,128)(2,1)}), bf16[32,9,4,128]{3,2,1,0:T(4,128)(2,1)S(1)}, u32[]{:S(2)}, u32[]{:S(2)}) async-start(bf16[32,9,4,128]{3,2,1,0:T(4,128)(2,1)} %copy.51), calls=%async_computation.4 | async-start | bytes 589824 | tf_op jit(solution)/shard_map/all_to_all | solution.py:213
  168.5 17.0 %collective-permute-start.7 = (bf16[192,256]{1,0:T(8,128)(2,1)S(1)}, bf16[192,256]{1,0:T(8,128)(2,1)S(1)}, u32[]{:S(2)}, u32[]{:S(2)}) collective-permute-start(bf16[192,256]{1,0:T(8,128)(2,1)S(1)} %get-tuple-element.23), channel_id=1, source_target_pairs={{1,0},{0,1},{3,2},{2,3},{5,4},{4,5},{7,6},{6,7},{9,8},{8,9},{11,10... | collective-permute-start | bytes 294920 | tf_op jit(solution)/shard_map/ppermute | solution.py:151
  170.4 17.9 %collective-permute-start.8 = (bf16[192,256]{1,0:T(8,128)(2,1)S(1)}, bf16[192,256]{1,0:T(8,128)(2,1)S(1)}, u32[]{:S(2)}, u32[]{:S(2)}) collective-permute-start(bf16[192,256]{1,0:T(8,128)(2,1)S(1)} %get-tuple-element.24), channel_id=1, source_target_pairs={{2,0},{3,1},{4,2},{5,3},{6,4},{7,5},{0,6},{1,7},{10,8},{11,9},{12,... | collective-permute-start | bytes 294920 | tf_op jit(solution)/shard_map/ppermute | solution.py:151
  175.3 16.1 %collective-permute-start.9 = (bf16[192,256]{1,0:T(8,128)(2,1)S(1)}, bf16[192,256]{1,0:T(8,128)(2,1)S(1)}, u32[]{:S(2)}, u32[]{:S(2)}) collective-permute-start(bf16[192,256]{1,0:T(8,128)(2,1)S(1)} %get-tuple-element.25), channel_id=1, source_target_pairs={{3,0},{2,1},{5,2},{4,3},{7,4},{6,5},{1,6},{0,7},{11,8},{10,9},{13,... | collective-permute-start | bytes 294920 | tf_op jit(solution)/shard_map/ppermute | solution.py:151
  178.9 12.5 %collective-permute-start.10 = (bf16[192,256]{1,0:T(8,128)(2,1)S(1)}, bf16[192,256]{1,0:T(8,128)(2,1)S(1)}, u32[]{:S(2)}, u32[]{:S(2)}) collective-permute-start(bf16[192,256]{1,0:T(8,128)(2,1)S(1)} %get-tuple-element.26), channel_id=1, source_target_pairs={{4,0},{5,1},{6,2},{7,3},{0,4},{1,5},{2,6},{3,7},{12,8},{13,9},{14,... | collective-permute-start | bytes 294920 | tf_op jit(solution)/shard_map/ppermute | solution.py:151
  180.8 10.6 %collective-permute-start.11 = (bf16[192,256]{1,0:T(8,128)(2,1)S(1)}, bf16[192,256]{1,0:T(8,128)(2,1)S(1)}, u32[]{:S(2)}, u32[]{:S(2)}) collective-permute-start(bf16[192,256]{1,0:T(8,128)(2,1)S(1)} %get-tuple-element.27), channel_id=1, source_target_pairs={{5,0},{4,1},{7,2},{6,3},{1,4},{0,5},{3,6},{2,7},{13,8},{12,9},{15,... | collective-permute-start | bytes 294920 | tf_op jit(solution)/shard_map/ppermute | solution.py:151
  185.4 6.9 %collective-permute-start.12 = (bf16[192,256]{1,0:T(8,128)(2,1)S(1)}, bf16[192,256]{1,0:T(8,128)(2,1)S(1)}, u32[]{:S(2)}, u32[]{:S(2)}) collective-permute-start(bf16[192,256]{1,0:T(8,128)(2,1)S(1)} %get-tuple-element.28), channel_id=1, source_target_pairs={{6,0},{7,1},{0,2},{1,3},{2,4},{3,5},{4,6},{5,7},{14,8},{15,9},{8,1... | collective-permute-start | bytes 294920 | tf_op jit(solution)/shard_map/ppermute | solution.py:151
  188.3 8.5 %collective-permute-start.13 = (bf16[192,256]{1,0:T(8,128)(2,1)S(1)}, bf16[192,256]{1,0:T(8,128)(2,1)S(1)}, u32[]{:S(2)}, u32[]{:S(2)}) collective-permute-start(bf16[192,256]{1,0:T(8,128)(2,1)S(1)} %get-tuple-element.29), channel_id=1, source_target_pairs={{7,0},{6,1},{1,2},{0,3},{3,4},{2,5},{5,6},{4,7},{15,8},{14,9},{9,1... | collective-permute-start | bytes 294920 | tf_op jit(solution)/shard_map/ppermute | solution.py:151

commit v3 on v2

--- a/solution.py
+++ b/solution.py
@@ -8,8 +8,8 @@
 
 epsilon = 1e-05
 bf16, f32, i32 = jnp.bfloat16, jnp.float32, jnp.int32
-YC = ("yh", "co")
-DP = ("z", "yh", "co")
+NEAR = ("zl", "yh", "co")
+DP = ("zh", "zl", "yh", "co")
 MP = ("x", "yl")
 INTERPRET = False
 
@@ -40,10 +40,10 @@
 
 
 def natural_of(p):
-    return ((p // 12) % 4) * 48 + (p // 48) * 12 + p % 12
-
-
-def turn_kernel(rows_ref, out_ref, live_ref, *, width, z):
+    return ((p // 12) % 2) * 96 + (p // 24) * 12 + p % 12
+
+
+def turn_kernel(rows_ref, out_ref, live_ref, *, width, far):
     slots, lanes = rows_ref.shape
     peers = slots // 2
     rows = rows_ref[...]
@@ -54,7 +54,7 @@
     source = lax.broadcasted_iota(i32, (slots, slots), 0)
     target = lax.broadcasted_iota(i32, (slots, slots), 1)
     loader = target % peers
-    order = (source == ((loader % 4) * z + loader // 4) * 2 + target // peers).astype(bf16)
+    order = (source == ((loader % 8) * far + loader // 8) * 2 + target // peers).astype(bf16)
     turned = nt(jnp.concatenate([pick, flag], axis=0), rows).astype(bf16)
     ordered = nn(turned, order)
     out_ref[...] = ordered[:width].astype(bf16)
@@ -73,24 +73,20 @@
     live = live_ref[0:1, :]
     s = jnp.zeros((1, slots), f32)
     for k in range(blocks):
-        s = s + jnp.sum(refs[k][...].astype(f32), axis=0, keepdims=True)
+        s = s + jnp.sum(refs[k // 2][k % 2].astype(f32), axis=0, keepdims=True)
     mean = s * (1.0 / total)
     s = jnp.zeros((1, slots), f32)
     for k in range(blocks):
-        c = refs[k][...].astype(f32) - mean
+        c = refs[k // 2][k % 2].astype(f32) - mean
         s = s + jnp.sum(c * c, axis=0, keepdims=True)
     inv = lax.rsqrt(s * (1.0 / total) + epsilon)
     for k in range(blocks):
-        c = refs[k][...].astype(f32) - mean
+        c = refs[k // 2][k % 2].astype(f32) - mean
         normed_ref[k] = (c * inv * gain_ref[block_of(own_ref, k, blocks)] * live).astype(bf16)
 
 
-def part_of(m):
-    return pl.ds(pl.multiple_of(48 * m, 16), 48)
-
-
 def w_block(w_ref, m):
-    return jnp.concatenate([w_ref[j, part_of(m), :] for j in range(4)], axis=0)
+    return jnp.concatenate([w_ref[j, m] for j in range(8)], axis=0)
 
 
 def forward_kernel(own_ref, normed_ref, live_ref, w_ref, up_ref, gated_ref, dw_ref, delta_ref):
@@ -111,25 +107,26 @@
     delta = jnp.concatenate([value_delta, gate_delta], axis=0)
     delta_ref[...] = delta
     for k in range(blocks):
-        dw = nt(normed_ref[k], delta).astype(bf16)
+        dw = nt(normed_ref[k], delta)
         m = block_of(own_ref, k, blocks)
-        for j in range(4):
-            dw_ref[j, part_of(m), :] = dw[48 * j : 48 * j + 48]
+        for j in range(8):
+            dw_ref[j, m] = dw[24 * j : 24 * j + 24].astype(bf16)
 
 
 def backward_kernel(own_ref, w_ref, delta_ref, *partial_refs):
-    blocks = len(partial_refs)
-    for k in range(blocks):
-        partial_refs[k][...] = nn(w_block(w_ref, block_of(own_ref, k, blocks)), delta_ref[...]).astype(bf16)
+    blocks = 2 * len(partial_refs)
+    for k in range(blocks):
+        w = w_block(w_ref, block_of(own_ref, k, blocks))
+        partial_refs[k // 2][k % 2] = nn(w, delta_ref[...]).astype(bf16)
 
 
 def join_kernel(*refs):
-    out_ref = refs[-1]
-    width, slots = refs[0].shape
+    across_ref, out_ref = refs[-2:]
+    width, slots = across_ref.shape[1:]
     peers = slots // 2
-    s = refs[0][...].astype(f32)
-    for ref in refs[1:-1]:
-        s = s + ref[...].astype(f32)
+    s = jnp.zeros((width, slots), f32)
+    for k, ref in enumerate(refs[:-2]):
+        s = s + ref[0].astype(f32) + across_ref[k].astype(f32)
     place = lax.broadcasted_iota(i32, (width, width), 1)
     natural = lax.broadcasted_iota(i32, (width, width), 0)
     back = (natural_of(place) == natural).astype(bf16)
@@ -142,13 +139,13 @@
     return lax.all_to_all(jnp.broadcast_to(x[None], (count,) + x.shape), axis, 0, 0, tiled=True)
 
 
-def hop(x, k, blocks, back):
-    n = blocks // 2
-    pairs = []
-    for i in range(blocks):
-        j = ((i // 2 + k // 2) % n) * 2 + (i % 2 + k) % 2
-        pairs.append((j, i) if back else (i, j))
-    return lax.ppermute(x, MP, pairs)
+def hop(x, step):
+    n = lax.axis_size("x")
+    return lax.ppermute(x, "x", [(i, (i + step) % n) for i in range(n)])
+
+
+def swap(x):
+    return lax.ppermute(x, "yl", [(0, 1), (1, 0)])
 
 
 def tiles(x):
@@ -156,9 +153,9 @@
 
 
 def body(frames, frame_owner, frame_valid, norm_gain, value_weight, gate_weight, grad_owned):
-    z = lax.axis_size("z")
+    far = lax.axis_size("zh")
     blocks = lax.axis_size(MP)
-    peers = 4 * z
+    peers = 8 * far
     slots = 2 * peers
     rows, width = frames.shape
     group = value_weight.shape[0]
@@ -180,39 +177,43 @@
         [frames, frame_valid.astype(bf16)[:, None], jnp.zeros((rows, lanes - width - 1), bf16)], axis=1
     )
     sent = jnp.dot(placing, flagged, preferred_element_type=f32).astype(bf16)
-    sent = sent.reshape(z, 2, 4, halves, 128).transpose(0, 3, 1, 2, 4).reshape(z, 2 * halves, 4, 128)
-    sent = jnp.concatenate([jnp.broadcast_to(shard[None], (z,) + shard.shape), sent], axis=1)
-    got = lax.all_to_all(sent, "z", 0, 0, tiled=True)
-    rows_z = got[:, wt:].reshape(z, halves, 4, 2, 128).transpose(2, 0, 3, 1, 4).reshape(4, 2 * z, lanes)
-    rows_y = lax.all_to_all(rows_z, YC, 0, 0, tiled=True)
-    w_rows = got[:, :wt].reshape(z, columns // 128, group, 128).transpose(0, 2, 1, 3)
-    w_rows = w_rows.reshape(z * group, columns)
-    w_full = spread(w_rows, YC, 4)
+    sent = sent.reshape(far, 4, 4, halves, 128).transpose(0, 3, 1, 2, 4).reshape(far, 4 * halves, 4, 128)
+    sent = jnp.concatenate([jnp.broadcast_to(shard[None], (far,) + shard.shape), sent], axis=1)
+    got = lax.all_to_all(sent, "zh", 0, 0, tiled=True)
+    rows_z = got[:, wt:].reshape(far, halves, 8, 2, 128).transpose(2, 0, 3, 1, 4).reshape(8, 2 * far, lanes)
+    rows_y = lax.all_to_all(rows_z, NEAR, 0, 0, tiled=True)
+    w_rows = got[:, :wt].reshape(far, columns // 128, group, 128).transpose(0, 2, 1, 3)
+    w_rows = w_rows.reshape(far * group, columns)
+    w_full = spread(w_rows, NEAR, 8)
+    w_full = w_full.reshape(8, blocks, 2 * group, columns)
     turned, live = call(
-        lambda *refs: turn_kernel(*refs, width=width, z=z),
+        lambda *refs: turn_kernel(*refs, width=width, far=far),
         [((width, slots), bf16), ((8, slots), f32)],
         rows_y.reshape(slots, lanes),
     )
-    whole = [turned] + [hop(turned, k, blocks, False) for k in range(1, blocks)]
-    gain = norm_gain.reshape(blocks, 4, 4, 12).transpose(0, 2, 1, 3).reshape(blocks, width, 1)
+    pair = jnp.stack([turned, swap(turned)])
+    whole = [pair] + [hop(pair, dx) for dx in range(1, blocks // 2)]
+    gain = norm_gain.reshape(blocks, 2, 8, 12).transpose(0, 2, 1, 3).reshape(blocks, width, 1)
     (normed,) = call(norm_kernel, [((blocks, width, slots), bf16)], own, live, gain, *whole)
     up = grad_owned.reshape(peers, 2, width).transpose(1, 2, 0)
     gated, dw, delta = call(
         forward_kernel,
-        [((2, width, peers), bf16), ((4, z * group, columns), bf16), ((columns, slots), bf16)],
+        [((2, width, peers), bf16), ((8, blocks, 2 * group, columns), bf16), ((columns, slots), bf16)],
         own,
         normed,
         live,
         w_full,
         up,
     )
-    dw_y = lax.all_to_all(dw, YC, 0, 0, tiled=True)
-    partial = call(backward_kernel, [((width, slots), bf16)] * blocks, own, w_full, delta)
+    dw_y = lax.all_to_all(dw.reshape(8, far * group, columns), NEAR, 0, 0, tiled=True)
+    partial = call(backward_kernel, [((2, width, slots), bf16)] * (blocks // 2), own, w_full, delta)
     dw_y = jnp.sum(dw_y.astype(f32), axis=0).astype(bf16)
-    dw_y = dw_y.reshape(z, group, columns // 128, 128).transpose(0, 2, 1, 3).reshape(z, wt, 4, 128)
-    dw_z = lax.all_to_all(dw_y, "z", 0, 0, tiled=True)
-    parts = [partial[0]] + [hop(partial[k], k, blocks, True) for k in range(1, blocks)]
-    (normed_grad,) = call(join_kernel, [((2, width, peers), bf16)], *parts)
+    dw_y = dw_y.reshape(far, group, columns // 128, 128).transpose(0, 2, 1, 3).reshape(far, wt, 4, 128)
+    dw_z = lax.all_to_all(dw_y, "zh", 0, 0, tiled=True)
+    parts = [partial[0]] + [hop(partial[dx], -dx) for dx in range(1, blocks // 2)]
+    other = jnp.stack([p[1] for p in parts])
+    across = swap(other)
+    (normed_grad,) = call(join_kernel, [((2, width, peers), bf16)], *parts, across)
     scale = float(rows * peers) ** (-0.5)
     grads = jnp.sum(dw_z.astype(f32), axis=0) * scale
     grads = grads.reshape(columns // 128, group, 128).transpose(1, 0, 2).reshape(group, columns)
@@ -225,8 +226,8 @@
 
 def solution(mesh):
     mp = mesh.shape["mp"]
-    z = mesh.shape["dp"] // 4
-    fine = Mesh(mesh.devices.reshape(z, 2, 2, mp // 2, 2), ("z", "yh", "co", "x", "yl"))
+    far = mesh.shape["dp"] // 8
+    fine = Mesh(mesh.devices.reshape(far, 2, 2, 2, mp // 2, 2), DP + MP)
     slots = P(DP, None, None, MP)
     weights = P(DP, MP)
     return jax.shard_map(

time: 215 us -> 194 us (0.902)
  blocking collectives: 108 us -> 80.1 us
  waiting for transfers between devices: 26 us -> 46.7 us
  starting transfers between devices: 60.3 us -> 49.5 us
    ppermute x14 -> x8, waiting for transfers between devices: 7.29 us -> 41.2 us  [the longest x2 23.6 us: swap(): return lax.ppermute(x, 'yl', [(0, 1), (1, 0)])]
    all_to_all x2, blocking collectives: 108 us -> 80.1 us  [the longest x1 56.6 us: body(): got = lax.all_to_all(sent, 'zh', 0, 0, tiled=True)]
    ppermute x14 -> x8, starting transfers between devices: 45.2 us -> 20.8 us  [the longest x6 16.6 us: hop(): return lax.ppermute(x, 'x', [(i, (i + step) % n) for i in range(n)])]
    all_to_all x2, starting transfers between devices: 10.4 us -> 24.2 us  [the longest x1 14.1 us: body(): rows_y = lax.all_to_all(rows_z, NEAR, 0, 0, tiled=True)]
    all_to_all x2, waiting for transfers between devices: 18.7 us -> 5.54 us  [the longest x1 5.54 us: body(): rows_y = lax.all_to_all(rows_z, NEAR, 0, 0, tiled=True)]
  transfers between devices with their start and end apart: 17 -> 11, of which waited for: 6 -> 7; matrix products, arithmetic and copies ran while one was open for 0% -> 0% of each run, Pallas kernels for 1% -> 1%
where the time goes in v3:
time: 194 us; the launch traced here: 193 us
  blocking collectives  80.1 us (41%)
  starting transfers between devices  49.5 us (26%)
  waiting for transfers between devices  46.7 us (24%)
  local copies, waits for them, and re-layouts  5.62 us (3%)
  Pallas kernels  5.08 us (3%)
  other arithmetic  3.6 us (2%)
    all_to_all x1, blocking collectives, body(): got = lax.all_to_all(sent, 'zh', 0, 0, tiled=True)  56.6 us
    ppermute x2, waiting for transfers between devices, swap(): return lax.ppermute(x, 'yl', [(0, 1), (1, 0)])  23.6 us
    all_to_all x1, blocking collectives, body(): lax.all_to_all(dw.reshape(8, far * group, columns), NEAR, 0, 0, tiled=True)  23.5 us
    ppermute x6, waiting for transfers between devices, hop(): return lax.ppermute(x, 'x', [(i, (i + step) % n) for i in range(n)])  17.6 us
    ppermute x6, starting transfers between devices, hop(): return lax.ppermute(x, 'x', [(i, (i + step) % n) for i in range(n)])  16.6 us
    all_to_all x1, starting transfers between devices, body(): rows_y = lax.all_to_all(rows_z, NEAR, 0, 0, tiled=True)  14.1 us
    all_to_all x1, starting transfers between devices, body(): dw_z = lax.all_to_all(dw_y, 'zh', 0, 0, tiled=True)  10 us
    all_to_all x1, waiting for transfers between devices, body(): rows_y = lax.all_to_all(rows_z, NEAR, 0, 0, tiled=True)  5.54 us
  transfers between devices with their start and end apart: 11, of which 7 were waited for; matrix products, arithmetic and copies ran while one was open for 0% of the time, Pallas kernels for 1%

profile of v3, /device:TPU:1, one launch (start us, length us, event | category | flops | bytes accessed | tf_op | source)
XLA Modules:
  0.0 192.7 jit_solution(15976233369307324330)
XLA Ops:
  0.6 0.7 convert_element_type.16
  1.3 0.9 convert_reduce_fusion.1
  2.3 0.7 multiply_add_fusion
  2.9 0.8 pad_maximum_fusion.3
  3.8 0.1 broadcast_in_dim.30
  3.9 0.1 pad.10.clone
  3.9 1.1 convolution_convert_fusion
  5.1 0.1 copy.42
  5.3 0.2 pad_maximum_fusion.1
  5.5 56.6 %all_to_all.25 = bf16[16,17,4,128]{3,2,1,0:T(4,128)(2,1)S(1)} all-to-all(bf16[16,17,4,128]{3,2,1,0:T(4,128)(2,1)S(1)} %pad_maximum_fusion.1), channel_id=1, replica_groups=mesh['zh'=16,'zl'=2,'yh'=2,'co'=2,'x'=4,'yl'=2] {'zh'}, dimensions={0} | all-to-all | bytes 557056 | tf_op jit(solution)/shard_map/all_to_all | solution.py:182
  62.2 0.1 copy.53
  62.2 0.1 copy.45
  62.4 0.7 reshape.82
  63.1 14.1 %all-to-all-start.1 = ((bf16[8,32,256]{2,1,0:T(8,128)(2,1)}), bf16[8,32,256]{2,1,0:T(8,128)(2,1)S(1)}, u32[]{:S(2)}, u32[]{:S(2)}) async-start(bf16[8,32,256]{2,1,0:T(8,128)(2,1)} %reshape.82), calls=%async_computation.1 | async-start | bytes 262144 | tf_op jit(solution)/shard_map/all_to_all | solution.py:184
  77.2 0.1 slice.33
  77.3 0.1 copy.49
  77.5 5.5 %all-to-all-done.1 = bf16[8,32,256]{2,1,0:T(8,128)(2,1)S(1)} async-done(((bf16[8,32,256]{2,1,0:T(8,128)(2,1)}), bf16[8,32,256]{2,1,0:T(8,128)(2,1)S(1)}, u32[]{:S(2)}, u32[]{:S(2)}) %all-to-all-start.1) | async-done | bytes 131104 | tf_op jit(solution)/shard_map/all_to_all | solution.py:184
  83.0 1.1 broadcast_in_dim.29
  84.1 4.5 %all-to-all-start.2 = ((bf16[8,192,384]{2,1,0:T(8,128)(2,1)}), bf16[8,192,384]{2,1,0:T(8,128)(2,1)S(1)}, u32[]{:S(2)}, u32[]{:S(2)}) async-start(bf16[8,192,384]{2,1,0:T(8,128)(2,1)} %broadcast_in_dim.29), calls=%async_computation.2 | async-start | bytes 2359296 | tf_op jit(solution)/shard_map/all_to_all | solution.py:139
  88.6 0.3 shard_map.102
  89.0 2.3 %collective-permute-start = (bf16[192,256]{1,0:T(8,128)(2,1)S(1)}, bf16[192,256]{1,0:T(8,128)(2,1)S(1)}, u32[]{:S(2)}, u32[]{:S(2)}) collective-permute-start(bf16[192,256]{1,0:T(8,128)(2,1)S(1)} %get-tuple-element.14), channel_id=1, source_target_pairs={{0,1},{1,0},{2,3},{3,2},{4,5},{5,4},{6,7},{7,6},{8,9},{9,8},{10,11... | collective-permute-start | bytes 294920 | tf_op jit(solution)/shard_map/ppermute | solution.py:148
  91.3 13.7 %collective-permute-done = bf16[192,256]{1,0:T(8,128)(2,1)S(1)} collective-permute-done((bf16[192,256]{1,0:T(8,128)(2,1)S(1)}, bf16[192,256]{1,0:T(8,128)(2,1)S(1)}, u32[]{:S(2)}, u32[]{:S(2)}) %collective-permute-start) | collective-permute-done | bytes 98336 | tf_op jit(solution)/shard_map/ppermute | solution.py:148
  105.0 4.4 %collective-permute-start.3 = (bf16[2,192,256]{2,1,0:T(8,128)(2,1)S(1)}, bf16[2,192,256]{2,1,0:T(8,128)(2,1)S(1)}, u32[]{:S(2)}, u32[]{:S(2)}) collective-permute-start(bf16[2,192,256]{2,1,0:T(8,128)(2,1)S(1)} %pad_maximum_fusion.2.refs_0_), channel_id=1, source_target_pairs={{0,6},{2,0},{4,2},{6,4},{1,7},{3,1},{5,3},{7,5},{8,14},{10,8},{12,... | collective-permute-start | bytes 589832 | tf_op jit(solution)/shard_map/ppermute | solution.py:144
  109.4 2.4 %collective-permute-start.2 = (bf16[2,192,256]{2,1,0:T(8,128)(2,1)S(1)}, bf16[2,192,256]{2,1,0:T(8,128)(2,1)S(1)}, u32[]{:S(2)}, u32[]{:S(2)}) collective-permute-start(bf16[2,192,256]{2,1,0:T(8,128)(2,1)S(1)} %pad_maximum_fusion.2.refs_0_), channel_id=1, source_target_pairs={{0,4},{2,6},{4,0},{6,2},{1,5},{3,7},{5,1},{7,3},{8,12},{10,14},{12... | collective-permute-start | bytes 589832 | tf_op jit(solution)/shard_map/ppermute | solution.py:144
  111.8 2.5 %collective-permute-start.1 = (bf16[2,192,256]{2,1,0:T(8,128)(2,1)S(1)}, bf16[2,192,256]{2,1,0:T(8,128)(2,1)S(1)}, u32[]{:S(2)}, u32[]{:S(2)}) collective-permute-start(bf16[2,192,256]{2,1,0:T(8,128)(2,1)S(1)} %pad_maximum_fusion.2.refs_0_), channel_id=1, source_target_pairs={{0,2},{2,4},{4,6},{6,0},{1,3},{3,5},{5,7},{7,1},{8,10},{10,12},{12... | collective-permute-start | bytes 589832 | tf_op jit(solution)/shard_map/ppermute | solution.py:144
  114.3 0.1 reshape.84
  114.5 0.3 reshape.95.gain_ref
  114.9 3.5 %collective-permute-done.2.refs_2_ = bf16[2,192,256]{2,1,0:T(8,128)(2,1)S(1)} collective-permute-done((bf16[2,192,256]{2,1,0:T(8,128)(2,1)S(1)}, bf16[2,192,256]{2,1,0:T(8,128)(2,1)S(1)}, u32[]{:S(2)}, u32[]{:S(2)}) %collective-permute-start.2) | collective-permute-done | bytes 196640 | tf_op jit(solution)/shard_map/ppermute | solution.py:144
  118.3 5.1 %collective-permute-done.1.refs_1_ = bf16[2,192,256]{2,1,0:T(8,128)(2,1)S(1)} collective-permute-done((bf16[2,192,256]{2,1,0:T(8,128)(2,1)S(1)}, bf16[2,192,256]{2,1,0:T(8,128)(2,1)S(1)}, u32[]{:S(2)}, u32[]{:S(2)}) %collective-permute-start.1) | collective-permute-done | bytes 196640 | tf_op jit(solution)/shard_map/ppermute | solution.py:144
  123.4 0.7 shard_map.103.normed_ref
  124.2 0.9 copy-done
  125.0 2.5 %shard_map.104 = (bf16[2,192,128]{2,1,0:T(8,128)(2,1)}, bf16[8,8,24,384]{3,2,1,0:T(8,128)(2,1)S(1)}, bf16[384,256]{1,0:T(8,128)(2,1)S(1)}) custom-call(s32[1]{0:T(128)} %bitcast.own_ref, bf16[8,192,256]{2,1,0:T(8,128)(2,1)S(1)} %shard_map.103.normed_ref, f32[8,256]{1,0:T(8,128)S(1)} %get-tuple-element.13.live_ref, bf16[8,8,24,384]{3,2,1,0:T(8,128)(2,1)S(1)} %bitcast.39, ...), custom_call_target="tpu_custom_call" | custom-call | tf_op jit(solution)/shard_map/pallas_call | solution.py:32
  127.6 23.5 %all_to_all.26 = bf16[8,192,384]{2,1,0:T(8,128)(2,1)S(1)} all-to-all(bf16[8,192,384]{2,1,0:T(8,128)(2,1)S(1)} %bitcast.41), channel_id=1, replica_groups=mesh['zh'=16,'zl'=2,'yh'=2,'co'=2,'x'=4,'yl'=2] {'zl','yh','co'}, dimensions={0} | all-to-all | bytes 2359296 | tf_op jit(solution)/shard_map/all_to_all | solution.py:208
  151.1 0.2 reduce_sum.31
  151.3 0.7 copy.51
  152.0 10.0 %all-to-all-start.4 = ((bf16[16,9,4,128]{3,2,1,0:T(4,128)(2,1)}), bf16[16,9,4,128]{3,2,1,0:T(4,128)(2,1)S(1)}, u32[]{:S(2)}, u32[]{:S(2)}) async-start(bf16[16,9,4,128]{3,2,1,0:T(4,128)(2,1)} %copy.51), calls=%async_computation.4 | async-start | bytes 294912 | tf_op jit(solution)/shard_map/all_to_all | solution.py:212
  162.1 0.6 shard_map.105
  162.7 2.2 %collective-permute-start.4 = (bf16[2,192,256]{2,1,0:T(8,128)(2,1)S(1)}, bf16[2,192,256]{2,1,0:T(8,128)(2,1)S(1)}, u32[]{:S(2)}, u32[]{:S(2)}) collective-permute-start(bf16[2,192,256]{2,1,0:T(8,128)(2,1)S(1)} %get-tuple-element.19), channel_id=1, source_target_pairs={{0,6},{2,0},{4,2},{6,4},{1,7},{3,1},{5,3},{7,5},{8,14},{10,8},{12,... | collective-permute-start | bytes 589832 | tf_op jit(solution)/shard_map/ppermute | solution.py:144
  164.9 2.4 %collective-permute-start.5 = (bf16[2,192,256]{2,1,0:T(8,128)(2,1)S(1)}, bf16[2,192,256]{2,1,0:T(8,128)(2,1)S(1)}, u32[]{:S(2)}, u32[]{:S(2)}) collective-permute-start(bf16[2,192,256]{2,1,0:T(8,128)(2,1)S(1)} %get-tuple-element.20), channel_id=1, source_target_pairs={{0,4},{2,6},{4,0},{6,2},{1,5},{3,7},{5,1},{7,3},{8,12},{10,14},{12... | collective-permute-start | bytes 589832 | tf_op jit(solution)/shard_map/ppermute | solution.py:144
  167.3 2.7 %collective-permute-start.6 = (bf16[2,192,256]{2,1,0:T(8,128)(2,1)S(1)}, bf16[2,192,256]{2,1,0:T(8,128)(2,1)S(1)}, u32[]{:S(2)}, u32[]{:S(2)}) collective-permute-start(bf16[2,192,256]{2,1,0:T(8,128)(2,1)S(1)} %get-tuple-element.21), channel_id=1, source_target_pairs={{0,2},{2,4},{4,6},{6,0},{1,3},{3,5},{5,7},{7,1},{8,10},{10,12},{12... | collective-permute-start | bytes 589832 | tf_op jit(solution)/shard_map/ppermute | solution.py:144
  170.0 3.3 %collective-permute-done.5.refs_2_ = bf16[2,192,256]{2,1,0:T(8,128)(2,1)S(1)} collective-permute-done((bf16[2,192,256]{2,1,0:T(8,128)(2,1)S(1)}, bf16[2,192,256]{2,1,0:T(8,128)(2,1)S(1)}, u32[]{:S(2)}, u32[]{:S(2)}) %collective-permute-start.5) | collective-permute-done | bytes 196640 | tf_op jit(solution)/shard_map/ppermute | solution.py:144
  173.3 5.7 %collective-permute-done.6.refs_3_ = bf16[2,192,256]{2,1,0:T(8,128)(2,1)S(1)} collective-permute-done((bf16[2,192,256]{2,1,0:T(8,128)(2,1)S(1)}, bf16[2,192,256]{2,1,0:T(8,128)(2,1)S(1)}, u32[]{:S(2)}, u32[]{:S(2)}) %collective-permute-start.6) | collective-permute-done | bytes 196640 | tf_op jit(solution)/shard_map/ppermute | solution.py:144
  179.1 0.1 pad_maximum_fusion
  179.1 1.9 collective-permute-start.7
  181.1 9.9 %collective-permute-done.7.refs_4_ = bf16[4,192,256]{2,1,0:T(8,128)(2,1)S(1)} collective-permute-done((bf16[4,192,256]{2,1,0:T(8,128)(2,1)S(1)}, bf16[4,192,256]{2,1,0:T(8,128)(2,1)S(1)}, u32[]{:S(2)}, u32[]{:S(2)}) %collective-permute-start.7) | collective-permute-done | bytes 393248 | tf_op jit(solution)/shard_map/ppermute | solution.py:148
  191.0 0.9 shard_map.106
  191.9 0.1 convert_reduce_fusion
  192.0 0.7 fusion.8
  (29 shorter events, 0.5 us)
Async XLA Ops:
  63.1 19.9 %all-to-all-start.1 = ((bf16[8,32,256]{2,1,0:T(8,128)(2,1)}), bf16[8,32,256]{2,1,0:T(8,128)(2,1)S(1)}, u32[]{:S(2)}, u32[]{:S(2)}) async-start(bf16[8,32,256]{2,1,0:T(8,128)(2,1)} %reshape.82), calls=%async_computation.1 | async-start | bytes 262144 | tf_op jit(solution)/shard_map/all_to_all | solution.py:184
  84.1 30.2 %copy-start.1 = (f32[1536]{0:T(1024)S(1)}, f32[1536]{0:T(1024)}, u32[]{:S(2)}) copy-start(f32[1536]{0:T(1024)} %param.10) | copy-start | bytes 18436
  84.1 40.0 %all-to-all-start.2 = ((bf16[8,192,384]{2,1,0:T(8,128)(2,1)}), bf16[8,192,384]{2,1,0:T(8,128)(2,1)S(1)}, u32[]{:S(2)}, u32[]{:S(2)}) async-start(bf16[8,192,384]{2,1,0:T(8,128)(2,1)} %broadcast_in_dim.29), calls=%async_computation.2 | async-start | bytes 2359296 | tf_op jit(solution)/shard_map/all_to_all | solution.py:139
  89.0 16.0 %collective-permute-start = (bf16[192,256]{1,0:T(8,128)(2,1)S(1)}, bf16[192,256]{1,0:T(8,128)(2,1)S(1)}, u32[]{:S(2)}, u32[]{:S(2)}) collective-permute-start(bf16[192,256]{1,0:T(8,128)(2,1)S(1)} %get-tuple-element.14), channel_id=1, source_target_pairs={{0,1},{1,0},{2,3},{3,2},{4,5},{5,4},{6,7},{7,6},{8,9},{9,8},{10,11... | collective-permute-start | bytes 294920 | tf_op jit(solution)/shard_map/ppermute | solution.py:148
  105.0 9.9 %collective-permute-start.3 = (bf16[2,192,256]{2,1,0:T(8,128)(2,1)S(1)}, bf16[2,192,256]{2,1,0:T(8,128)(2,1)S(1)}, u32[]{:S(2)}, u32[]{:S(2)}) collective-permute-start(bf16[2,192,256]{2,1,0:T(8,128)(2,1)S(1)} %pad_maximum_fusion.2.refs_0_), channel_id=1, source_target_pairs={{0,6},{2,0},{4,2},{6,4},{1,7},{3,1},{5,3},{7,5},{8,14},{10,8},{12,... | collective-permute-start | bytes 589832 | tf_op jit(solution)/shard_map/ppermute | solution.py:144
  109.4 8.9 %collective-permute-start.2 = (bf16[2,192,256]{2,1,0:T(8,128)(2,1)S(1)}, bf16[2,192,256]{2,1,0:T(8,128)(2,1)S(1)}, u32[]{:S(2)}, u32[]{:S(2)}) collective-permute-start(bf16[2,192,256]{2,1,0:T(8,128)(2,1)S(1)} %pad_maximum_fusion.2.refs_0_), channel_id=1, source_target_pairs={{0,4},{2,6},{4,0},{6,2},{1,5},{3,7},{5,1},{7,3},{8,12},{10,14},{12... | collective-permute-start | bytes 589832 | tf_op jit(solution)/shard_map/ppermute | solution.py:144
  111.8 11.6 %collective-permute-start.1 = (bf16[2,192,256]{2,1,0:T(8,128)(2,1)S(1)}, bf16[2,192,256]{2,1,0:T(8,128)(2,1)S(1)}, u32[]{:S(2)}, u32[]{:S(2)}) collective-permute-start(bf16[2,192,256]{2,1,0:T(8,128)(2,1)S(1)} %pad_maximum_fusion.2.refs_0_), channel_id=1, source_target_pairs={{0,2},{2,4},{4,6},{6,0},{1,3},{3,5},{5,7},{7,1},{8,10},{10,12},{12... | collective-permute-start | bytes 589832 | tf_op jit(solution)/shard_map/ppermute | solution.py:144
  124.1 0.9 copy-start
  152.0 39.8 %all-to-all-start.4 = ((bf16[16,9,4,128]{3,2,1,0:T(4,128)(2,1)}), bf16[16,9,4,128]{3,2,1,0:T(4,128)(2,1)S(1)}, u32[]{:S(2)}, u32[]{:S(2)}) async-start(bf16[16,9,4,128]{3,2,1,0:T(4,128)(2,1)} %copy.51), calls=%async_computation.4 | async-start | bytes 294912 | tf_op jit(solution)/shard_map/all_to_all | solution.py:212
  162.7 7.3 %collective-permute-start.4 = (bf16[2,192,256]{2,1,0:T(8,128)(2,1)S(1)}, bf16[2,192,256]{2,1,0:T(8,128)(2,1)S(1)}, u32[]{:S(2)}, u32[]{:S(2)}) collective-permute-start(bf16[2,192,256]{2,1,0:T(8,128)(2,1)S(1)} %get-tuple-element.19), channel_id=1, source_target_pairs={{0,6},{2,0},{4,2},{6,4},{1,7},{3,1},{5,3},{7,5},{8,14},{10,8},{12,... | collective-permute-start | bytes 589832 | tf_op jit(solution)/shard_map/ppermute | solution.py:144
  164.9 8.4 %collective-permute-start.5 = (bf16[2,192,256]{2,1,0:T(8,128)(2,1)S(1)}, bf16[2,192,256]{2,1,0:T(8,128)(2,1)S(1)}, u32[]{:S(2)}, u32[]{:S(2)}) collective-permute-start(bf16[2,192,256]{2,1,0:T(8,128)(2,1)S(1)} %get-tuple-element.20), channel_id=1, source_target_pairs={{0,4},{2,6},{4,0},{6,2},{1,5},{3,7},{5,1},{7,3},{8,12},{10,14},{12... | collective-permute-start | bytes 589832 | tf_op jit(solution)/shard_map/ppermute | solution.py:144
  167.3 11.7 %collective-permute-start.6 = (bf16[2,192,256]{2,1,0:T(8,128)(2,1)S(1)}, bf16[2,192,256]{2,1,0:T(8,128)(2,1)S(1)}, u32[]{:S(2)}, u32[]{:S(2)}) collective-permute-start(bf16[2,192,256]{2,1,0:T(8,128)(2,1)S(1)} %get-tuple-element.21), channel_id=1, source_target_pairs={{0,2},{2,4},{4,6},{6,0},{1,3},{3,5},{5,7},{7,1},{8,10},{10,12},{12... | collective-permute-start | bytes 589832 | tf_op jit(solution)/shard_map/ppermute | solution.py:144
  179.1 11.8 %collective-permute-start.7 = (bf16[4,192,256]{2,1,0:T(8,128)(2,1)S(1)}, bf16[4,192,256]{2,1,0:T(8,128)(2,1)S(1)}, u32[]{:S(2)}, u32[]{:S(2)}) collective-permute-start(bf16[4,192,256]{2,1,0:T(8,128)(2,1)S(1)} %pad_maximum_fusion), channel_id=1, source_target_pairs={{0,1},{1,0},{2,3},{3,2},{4,5},{5,4},{6,7},{7,6},{8,9},{9,8},{10,11... | collective-permute-start | bytes 1179656 | tf_op jit(solution)/shard_map/ppermute | solution.py:148

commit v4 on v3

v4 whole, which is shorter than its diff:
```python
import jax
import jax.numpy as jnp
from jax import lax
from jax.experimental import pallas as pl
from jax.experimental.pallas import tpu as pltpu
from jax.sharding import Mesh, PartitionSpec as P


epsilon = 1e-05
bf16, f32, i32 = jnp.bfloat16, jnp.float32, jnp.int32
NEAR = ("zl", "yh")
DP = ("zh", "zl", "yh", "co")
MP = ("x", "yl")
INTERPRET = False


def nt(a, b):
    return lax.dot_general(a, b, (((1,), (1,)), ((), ())), preferred_element_type=f32)


def nn(a, b):
    return lax.dot_general(a, b, (((1,), (0,)), ((), ())), preferred_element_type=f32)


def tn(a, b):
    return lax.dot_general(a, b, (((0,), (0,)), ((), ())), preferred_element_type=f32)


def call(kernel, outs, *args, limit=12):
    vmem = pl.BlockSpec(memory_space=pltpu.VMEM)
    smem = pl.BlockSpec(memory_space=pltpu.SMEM)
    return pl.pallas_call(
        kernel,
        in_specs=[smem if a.shape == (2,) else vmem for a in args],
        out_specs=[vmem] * len(outs),
        out_shape=[jax.ShapeDtypeStruct(s, d) for s, d in outs],
        compiler_params=pltpu.CompilerParams(vmem_limit_bytes=limit << 20),
        interpret=INTERPRET,
    )(*args)


def natural_of(p, co):
    core = (p // 96 + co) % 2
    return ((p // 12) % 2) * 96 + (((p // 24) % 4) * 2 + core) * 12 + p % 12


def send_kernel(frames_ref, owner_ref, valid_ref, out_ref):
    rows, width = frames_ref.shape
    slots, lanes = out_ref.shape
    owner = owner_ref[...]
    down = jnp.transpose(jnp.broadcast_to(owner, (rows, rows)))
    earlier = lax.broadcasted_iota(i32, (rows, rows), 0) < lax.broadcasted_iota(i32, (rows, rows), 1)
    slot = jnp.sum(jnp.where((down == owner) & earlier, 1.0, 0.0), axis=0, keepdims=True).astype(i32)
    hit = lax.broadcasted_iota(i32, (slots, rows), 0) == owner * 2 + slot
    placed = nn(jnp.where(hit, 1.0, 0.0).astype(bf16), frames_ref[...])
    live = jnp.sum(jnp.where(hit & (valid_ref[...] > 0), 1.0, 0.0), axis=1, keepdims=True)
    pad = lax.broadcasted_iota(i32, (slots, lanes - width), 1) == 0
    out_ref[...] = jnp.concatenate([placed, jnp.where(pad, live, 0.0)], axis=1).astype(bf16)


def turn_kernel(own_ref, rows_ref, out_ref, live_ref):
    width, slots = out_ref.shape[1:]
    peers = slots // 2
    far = peers // 8
    lanes = rows_ref.shape[-1]
    place = lax.broadcasted_iota(i32, (width, lanes), 0)
    column = lax.broadcasted_iota(i32, (width, lanes), 1)
    pick = (column == natural_of(place, own_ref[1])).astype(bf16)
    flag = (lax.broadcasted_iota(i32, (16, lanes), 1) == width).astype(bf16)
    pick = jnp.concatenate([pick, flag], axis=0)
    source = lax.broadcasted_iota(i32, (slots, slots), 0)
    target = lax.broadcasted_iota(i32, (slots, slots), 1)
    loader = target % peers
    order = (source == ((loader % 8) * far + loader // 8) * 2 + target // peers).astype(bf16)
    for y in range(2):
        rows = jnp.concatenate([rows_ref[n, y] for n in range(8)], axis=0)
        ordered = nn(nt(pick, rows).astype(bf16), order)
        out_ref[y] = ordered[:width].astype(bf16)
    live_ref[...] = ordered[width : width + 8]


def block_of(own_ref, k, blocks, relative=False):
    x, y = own_ref[0] // 2, own_ref[0] % 2
    y = (y + k) % 2 if relative else k % 2
    return ((x + (blocks // 2 - k // 2)) % (blocks // 2)) * 2 + y


def norm_kernel(own_ref, live_ref, gain_ref, *refs):
    normed_ref = refs[-1]
    blocks, width, slots = normed_ref.shape
    total = blocks * width
    live = live_ref[0:1, :]
    s = jnp.zeros((1, slots), f32)
    for k in range(blocks):
        s = s + jnp.sum(refs[k // 2][k % 2].astype(f32), axis=0, keepdims=True)
    mean = s * (1.0 / total)
    s = jnp.zeros((1, slots), f32)
    for k in range(blocks):
        c = refs[k // 2][k % 2].astype(f32) - mean
        s = s + jnp.sum(c * c, axis=0, keepdims=True)
    inv = lax.rsqrt(s * (1.0 / total) + epsilon)
    for k in range(blocks):
        c = refs[k // 2][k % 2].astype(f32) - mean
        normed_ref[k] = (c * inv * gain_ref[block_of(own_ref, k, blocks)] * live).astype(bf16)


def w_block(wa_ref, wb_ref, m):
    return jnp.concatenate([ref[j, m] for ref in (wa_ref, wb_ref) for j in range(4)], axis=0)


def forward_kernel(own_ref, normed_ref, live_ref, wa_ref, wb_ref, up_ref, gated_ref, da_ref, db_ref, delta_ref):
    blocks, width, slots = normed_ref.shape
    peers = slots // 2
    live = live_ref[0:1, :]
    acc = jnp.zeros((2 * width, slots), f32)
    for k in range(blocks):
        acc = acc + tn(w_block(wa_ref, wb_ref, block_of(own_ref, k, blocks)), normed_ref[k])
    value, gate = acc[:width], acc[width:]
    sig = jax.nn.sigmoid(gate)
    up = jnp.concatenate([up_ref[0], up_ref[1]], axis=1).astype(f32)
    gated = (value * sig).astype(bf16)
    gated_ref[0] = gated[:, :peers]
    gated_ref[1] = gated[:, peers:]
    value_delta = (up * sig * live).astype(bf16)
    gate_delta = (up * value * sig * (1.0 - sig) * live).astype(bf16)
    delta = jnp.concatenate([value_delta, gate_delta], axis=0)
    delta_ref[...] = delta
    for k in range(blocks):
        dw = nt(normed_ref[k], delta)
        m = block_of(own_ref, k, blocks)
        for j in range(4):
            da_ref[j, m] = dw[24 * j : 24 * j + 24].astype(bf16)
            db_ref[j, m] = dw[24 * j + 96 : 24 * j + 120].astype(bf16)


def backward_kernel(own_ref, wa_ref, wb_ref, delta_ref, *partial_refs):
    blocks = 2 * len(partial_refs)
    for k in range(blocks):
        w = w_block(wa_ref, wb_ref, block_of(own_ref, k, blocks, True))
        partial_refs[k // 2][k % 2] = nn(w, delta_ref[...]).astype(bf16)


def join_kernel(own_ref, *refs):
    across_ref, out_ref = refs[-2:]
    width, slots = across_ref.shape[1:]
    peers = slots // 2
    s = jnp.zeros((width, slots), f32)
    for k, ref in enumerate(refs[:-2]):
        s = s + ref[0].astype(f32) + across_ref[k].astype(f32)
    place = lax.broadcasted_iota(i32, (width, width), 1)
    natural = lax.broadcasted_iota(i32, (width, width), 0)
    back = (natural_of(place, own_ref[1]) == natural).astype(bf16)
    out = nn(back, s.astype(bf16)).astype(bf16)
    out_ref[0] = out[:, :peers]
    out_ref[1] = out[:, peers:]


def spread(x, axis, count):
    return lax.all_to_all(jnp.broadcast_to(x[None], (count,) + x.shape), axis, 0, 0, tiled=True)


def hop(x, step):
    n = lax.axis_size("x")
    return lax.ppermute(x, "x", [(i, (i + step) % n) for i in range(n)])


def swap(x, axis):
    return lax.ppermute(x, axis, [(0, 1), (1, 0)])


def tiles(x):
    return x.reshape(x.shape[0] // 4, 4, x.shape[1] // 128, 128).transpose(2, 0, 1, 3)


def body(frames, frame_owner, frame_valid, norm_gain, value_weight, gate_weight, grad_owned):
    far = lax.axis_size("zh")
    blocks = lax.axis_size(MP)
    peers = 8 * far
    slots = 2 * peers
    rows, width = frames.shape
    group = value_weight.shape[0]
    columns = 2 * width
    wt = columns // 128 * group // 4
    lanes = -(-(width + 1) // 128) * 128
    halves = lanes // 128
    core = lax.axis_index("co").astype(i32)
    own = jnp.stack([lax.axis_index(MP).astype(i32), core])

    shard = tiles(jnp.concatenate([value_weight, gate_weight], axis=1)).reshape(wt, 4, 128)
    (sent,) = call(
        send_kernel, [((slots, lanes), bf16)], frames, frame_owner.reshape(1, rows), frame_valid.reshape(1, rows)
    )
    sent = sent.reshape(far, 4, 4, halves, 128).transpose(0, 3, 1, 2, 4).reshape(far, 4 * halves, 4, 128)
    sent = jnp.concatenate([jnp.broadcast_to(shard[None], (far,) + shard.shape), sent], axis=1)
    got = lax.all_to_all(sent, "zh", 0, 0, tiled=True)
    rows_z = got[:, wt:].reshape(far, halves, 8, 2, 128).transpose(2, 0, 3, 1, 4).reshape(8, 1, 2 * far, lanes)
    rows_z = jnp.broadcast_to(rows_z, (8, 2, 2 * far, lanes)).reshape(16, 2 * far, lanes)
    rows_y = lax.all_to_all(rows_z, ("zl", "yh", "co", "yl"), 0, 0, tiled=True)
    w_rows = got[:, :wt].reshape(far, columns // 128, group, 128).transpose(0, 2, 1, 3)
    w_rows = w_rows.reshape(far * group, columns)
    w_own = spread(w_rows, NEAR, 4)
    w_other = swap(w_own, "co")
    w_own = w_own.reshape(4, blocks, 2 * group, columns)
    w_other = w_other.reshape(4, blocks, 2 * group, columns)
    turned, live = call(
        turn_kernel,
        [((2, width, slots), bf16), ((8, slots), f32)],
        own,
        rows_y.reshape(8, 2, 2 * far, lanes),
    )
    whole = [turned] + [hop(turned, dx) for dx in range(1, blocks // 2)]
    gain = norm_gain.reshape(blocks, 2, 4, 2, 12).transpose(0, 3, 2, 1, 4)
    gain = jnp.where(core == 0, gain, gain[:, ::-1]).reshape(blocks, width, 1)
    (normed,) = call(norm_kernel, [((blocks, width, slots), bf16)], own, live, gain, *whole)
    up = grad_owned.reshape(peers, 2, width).transpose(1, 2, 0)
    near = (4, blocks, 2 * group, columns)
    gated, dw_own, dw_other, delta = call(
        forward_kernel,
        [((2, width, peers), bf16), (near, bf16), (near, bf16), ((columns, slots), bf16)],
        own,
        normed,
        live,
        w_own,
        w_other,
        up,
    )
    dw_c = swap(dw_other.reshape(4, far * group, columns), "co")
    partial = call(
        backward_kernel, [((2, width, slots), bf16)] * (blocks // 2), own, w_own, w_other, delta
    )
    dw_c = (dw_c.astype(f32) + dw_own.reshape(4, far * group, columns).astype(f32)).astype(bf16)
    dw_y = lax.all_to_all(dw_c, NEAR, 0, 0, tiled=True)
    dw_y = jnp.sum(dw_y.astype(f32), axis=0).astype(bf16)
    dw_y = dw_y.reshape(far, group, columns // 128, 128).transpose(0, 2, 1, 3).reshape(far, wt, 4, 128)
    dw_z = lax.all_to_all(dw_y, "zh", 0, 0, tiled=True)
    parts = [partial[0]] + [hop(partial[dx], -dx) for dx in range(1, blocks // 2)]
    other = []
    for part in parts:
        other.append(part[1:])
    across = swap(jnp.concatenate(other), "yl")
    (normed_grad,) = call(join_kernel, [((2, width, peers), bf16)], own, *parts, across)
    scale = float(rows * peers) ** (-0.5)
    grads = jnp.sum(dw_z.astype(f32), axis=0) * scale
    grads = grads.reshape(columns // 128, group, 128).transpose(1, 0, 2).reshape(group, columns)

    def restore(x):
        return x.transpose(2, 0, 1).reshape(1, peers, 2, width)

    return (restore(gated), grads[:, :width], grads[:, width:], restore(normed_grad))


def solution(mesh):
    mp = mesh.shape["mp"]
    far = mesh.shape["dp"] // 8
    fine = Mesh(mesh.devices.reshape(far, 2, 2, 2, mp // 2, 2), DP + MP)
    slots = P(DP, None, None, MP)
    weights = P(DP, MP)
    return jax.shard_map(
        body,
        mesh=fine,
        in_specs=(P(DP, MP), P(DP, None), P(DP), P(), weights, weights, slots),
        out_specs=(slots, weights, weights, slots),
        check_vma=False,
    )
```

time: 194 us -> 181 us (0.933)
  waiting for transfers between devices: 46.7 us -> 35.3 us
  blocking collectives: 80.1 us -> 69 us
  starting transfers between devices: 49.5 us -> 58.3 us
  Pallas kernels: 5.08 us -> 8.41 us
  other arithmetic: 3.6 us -> 0.81 us
    ppermute x2 -> x3, waiting for transfers between devices: 23.6 us -> 10.3 us  [swap(): return lax.ppermute(x, axis, [(0, 1), (1, 0)])]
    all_to_all x1, blocking collectives: 23.5 us -> 12.4 us  [body(): dw_y = lax.all_to_all(dw_c, NEAR, 0, 0, tiled=True)]
    all_to_all x1, waiting for transfers between devices: 0.01 us -> 6.92 us  [spread(): lax.all_to_all(jnp.broadcast_to(x[None], (count,) + x.shape), axis, 0, 0,...]
    all_to_all x1, starting transfers between devices: 4.46 us -> 10.8 us  [spread(): lax.all_to_all(jnp.broadcast_to(x[None], (count,) + x.shape), axis, 0, 0,...]
    all_to_all x1, starting transfers between devices: 14.1 us -> 7.81 us  [body(): rows_y = lax.all_to_all(rows_z, ('zl', 'yh', 'co', 'yl'), 0, 0, tiled=True)]
    ppermute x6, waiting for transfers between devices: 17.6 us -> 13.2 us  [hop(): return lax.ppermute(x, 'x', [(i, (i + step) % n) for i in range(n)])]
    ppermute x6, starting transfers between devices: 16.6 us -> 20.2 us  [hop(): return lax.ppermute(x, 'x', [(i, (i + step) % n) for i in range(n)])]
    ppermute x2 -> x3, starting transfers between devices: 4.23 us -> 7.56 us  [swap(): return lax.ppermute(x, axis, [(0, 1), (1, 0)])]
  transfers between devices with their start and end apart: 11 -> 12, of which waited for: 7 -> 8; matrix products, arithmetic and copies ran while one was open for 0% -> 1% of each run, Pallas kernels for 1% -> 3%
where the time goes in v4:
time: 181 us; the launch traced here: 180 us
  blocking collectives  69 us (38%)
  starting transfers between devices  58.3 us (32%)
  waiting for transfers between devices  35.3 us (20%)
  Pallas kernels  8.41 us (5%)
  local copies, waits for them, and re-layouts  7.05 us (4%)
    all_to_all x1, blocking collectives, body(): got = lax.all_to_all(sent, 'zh', 0, 0, tiled=True)  56.6 us
    ppermute x6, starting transfers between devices, hop(): return lax.ppermute(x, 'x', [(i, (i + step) % n) for i in range(n)])  20.2 us
    ppermute x6, waiting for transfers between devices, hop(): return lax.ppermute(x, 'x', [(i, (i + step) % n) for i in range(n)])  13.2 us
    all_to_all x1, blocking collectives, body(): dw_y = lax.all_to_all(dw_c, NEAR, 0, 0, tiled=True)  12.4 us
    all_to_all x1, starting transfers between devices, body(): dw_z = lax.all_to_all(dw_y, 'zh', 0, 0, tiled=True)  12 us
    all_to_all x1, starting transfers between devices, spread(): lax.all_to_all(jnp.broadcast_to(x[None], (count,) + x.shape), axis, 0, 0,...  10.8 us
    ppermute x3, waiting for transfers between devices, swap(): return lax.ppermute(x, axis, [(0, 1), (1, 0)])  10.3 us
    pallas_call x6, Pallas kernels, call(): pl.pallas_call(kernel, in_specs=[smem if a.shape == (2,) else vmem for a...  8.41 us
  transfers between devices with their start and end apart: 12, of which 8 were waited for; matrix products, arithmetic and copies ran while one was open for 1% of the time, Pallas kernels for 3%

profile of v4, /device:TPU:1, one launch (start us, length us, event | category | flops | bytes accessed | tf_op | source)
XLA Modules:
  0.0 179.9 jit_solution(17264586156732016684)
XLA Ops:
  0.6 0.9 copy-done.1
  1.5 0.7 copy-done.2
  2.2 0.7 copy-done.3
  2.9 0.3 shard_map.102
  3.4 0.2 copy-done.4
  3.6 0.1 pad_maximum_fusion.2
  3.8 0.2 pad_maximum_fusion.1
  3.9 56.6 %all_to_all.25 = bf16[16,17,4,128]{3,2,1,0:T(4,128)(2,1)S(1)} all-to-all(bf16[16,17,4,128]{3,2,1,0:T(4,128)(2,1)S(1)} %pad_maximum_fusion.1), channel_id=1, replica_groups=mesh['zh'=16,'zl'=2,'yh'=2,'co'=2,'x'=4,'yl'=2] {'zh'}, dimensions={0} | all-to-all | bytes 557056 | tf_op jit(solution)/shard_map/all_to_all | solution.py:195
  60.6 0.1 copy.33
  60.8 0.9 broadcast_in_dim.26
  61.7 10.8 %all-to-all-start.2 = ((bf16[4,192,384]{2,1,0:T(8,128)(2,1)}), bf16[4,192,384]{2,1,0:T(8,128)(2,1)S(1)}, u32[]{:S(2)}, u32[]{:S(2)}) async-start(bf16[4,192,384]{2,1,0:T(8,128)(2,1)} %broadcast_in_dim.26), calls=%async_computation.2 | async-start | bytes 1179648 | tf_op jit(solution)/shard_map/all_to_all | solution.py:159
  72.6 0.1 copy.29
  72.8 0.1 broadcast_in_dim.23
  72.8 6.9 %all-to-all-done.2 = bf16[4,192,384]{2,1,0:T(8,128)(2,1)S(1)} async-done(((bf16[4,192,384]{2,1,0:T(8,128)(2,1)}), bf16[4,192,384]{2,1,0:T(8,128)(2,1)S(1)}, u32[]{:S(2)}, u32[]{:S(2)}) %all-to-all-start.2) | async-done | bytes 589856 | tf_op jit(solution)/shard_map/all_to_all | solution.py:159
  79.8 0.7 broadcast_in_dim.24
  80.5 7.8 %all-to-all-start.1 = ((bf16[16,32,256]{2,1,0:T(8,128)(2,1)}), bf16[16,32,256]{2,1,0:T(8,128)(2,1)S(1)}, u32[]{:S(2)}, u32[]{:S(2)}) async-start(bf16[16,32,256]{2,1,0:T(8,128)(2,1)} %bitcast.10), calls=%async_computation.1 | async-start | bytes 524288 | tf_op jit(solution)/shard_map/all_to_all | solution.py:198
  88.3 2.1 %collective-permute-start.3 = (bf16[4,192,384]{2,1,0:T(8,128)(2,1)S(1)}, bf16[4,192,384]{2,1,0:T(8,128)(2,1)S(1)}, u32[]{:S(2)}, u32[]{:S(2)}) collective-permute-start(bf16[4,192,384]{2,1,0:T(8,128)(2,1)S(1)} %all-to-all-done.2), channel_id=1, source_target_pairs={{0,8},{8,0},{1,9},{9,1},{2,10},{10,2},{3,11},{11,3},{4,12},{12,4},... | collective-permute-start | bytes 1769480 | tf_op jit(solution)/shard_map/ppermute | solution.py:168
  90.5 0.1 reshape.87
  90.6 0.2 rev.3
  90.8 0.1 pad_add_fusion.own_ref
  90.8 4.9 %all-to-all-done.1 = bf16[16,32,256]{2,1,0:T(8,128)(2,1)S(1)} async-done(((bf16[16,32,256]{2,1,0:T(8,128)(2,1)}), bf16[16,32,256]{2,1,0:T(8,128)(2,1)S(1)}, u32[]{:S(2)}, u32[]{:S(2)}) %all-to-all-start.1) | async-done | bytes 262176 | tf_op jit(solution)/shard_map/all_to_all | solution.py:198
  95.8 1.1 shard_map.103
  96.9 3.1 %collective-permute-start = (bf16[2,192,256]{2,1,0:T(8,128)(2,1)S(1)}, bf16[2,192,256]{2,1,0:T(8,128)(2,1)S(1)}, u32[]{:S(2)}, u32[]{:S(2)}) collective-permute-start(bf16[2,192,256]{2,1,0:T(8,128)(2,1)S(1)} %get-tuple-element.15.refs_0_), channel_id=1, source_target_pairs={{0,2},{2,4},{4,6},{6,0},{1,3},{3,5},{5,7},{7,1},{8,10},{10,12},{12... | collective-permute-start | bytes 589832 | tf_op jit(solution)/shard_map/ppermute | solution.py:164
  100.0 4.4 %collective-permute-start.1 = (bf16[2,192,256]{2,1,0:T(8,128)(2,1)S(1)}, bf16[2,192,256]{2,1,0:T(8,128)(2,1)S(1)}, u32[]{:S(2)}, u32[]{:S(2)}) collective-permute-start(bf16[2,192,256]{2,1,0:T(8,128)(2,1)S(1)} %get-tuple-element.15.refs_0_), channel_id=1, source_target_pairs={{0,4},{2,6},{4,0},{6,2},{1,5},{3,7},{5,1},{7,3},{8,12},{10,14},{12... | collective-permute-start | bytes 589832 | tf_op jit(solution)/shard_map/ppermute | solution.py:164
  104.4 3.1 %collective-permute-start.2 = (bf16[2,192,256]{2,1,0:T(8,128)(2,1)S(1)}, bf16[2,192,256]{2,1,0:T(8,128)(2,1)S(1)}, u32[]{:S(2)}, u32[]{:S(2)}) collective-permute-start(bf16[2,192,256]{2,1,0:T(8,128)(2,1)S(1)} %get-tuple-element.15.refs_0_), channel_id=1, source_target_pairs={{0,6},{2,0},{4,2},{6,4},{1,7},{3,1},{5,3},{7,5},{8,14},{10,8},{12,... | collective-permute-start | bytes 589832 | tf_op jit(solution)/shard_map/ppermute | solution.py:164
  107.6 0.3 reshape.100.gain_ref
  107.9 3.2 %collective-permute-done.1.refs_2_ = bf16[2,192,256]{2,1,0:T(8,128)(2,1)S(1)} collective-permute-done((bf16[2,192,256]{2,1,0:T(8,128)(2,1)S(1)}, bf16[2,192,256]{2,1,0:T(8,128)(2,1)S(1)}, u32[]{:S(2)}, u32[]{:S(2)}) %collective-permute-start.1) | collective-permute-done | bytes 196640 | tf_op jit(solution)/shard_map/ppermute | solution.py:164
  111.1 1.4 collective-permute-done.2.refs_3_
  112.5 1.2 shard_map.104.normed_ref
  113.8 3.1 %shard_map.105 = (bf16[2,192,128]{2,1,0:T(8,128)(2,1)}, bf16[4,8,24,384]{3,2,1,0:T(8,128)(2,1)S(1)}, bf16[4,8,24,384]{3,2,1,0:T(8,128)(2,1)S(1)}, bf16[384,256]{1,0:T(8,128)(2,1)S(1)}) custom-call(s32[2]{0:T(128)S(1)} %pad_add_fusion.own_ref, bf16[8,192,256]{2,1,0:T(8,128)(2,1)S(1)} %shard_map.104.normed_ref, f32[8,256]{1,0:T(8,128)S(1)} %get-tuple-element.14.live_ref, ...), custom_call_target="tpu_custom_call" | custom-call | tf_op jit(solution)/shard_map/pallas_call | solution.py:32
  116.9 3.4 %collective-permute-start.4 = (bf16[4,192,384]{2,1,0:T(8,128)(2,1)S(1)}, bf16[4,192,384]{2,1,0:T(8,128)(2,1)S(1)}, u32[]{:S(2)}, u32[]{:S(2)}) collective-permute-start(bf16[4,192,384]{2,1,0:T(8,128)(2,1)S(1)} %bitcast.53), channel_id=1, source_target_pairs={{0,8},{8,0},{1,9},{9,1},{2,10},{10,2},{3,11},{11,3},{4,12},{12,4},... | collective-permute-start | bytes 1769480 | tf_op jit(solution)/shard_map/ppermute | solution.py:168
  120.3 1.6 collective-permute-done.4
  121.9 0.2 fusion
  122.2 12.4 %all_to_all.26 = bf16[4,192,384]{2,1,0:T(8,128)(2,1)S(1)} all-to-all(bf16[4,192,384]{2,1,0:T(8,128)(2,1)S(1)} %fusion), channel_id=1, replica_groups=mesh['zh'=16,'zl'=2,'yh'=2,'co'=2,'x'=4,'yl'=2] {'zl','yh'}, dimensions={0} | all-to-all | bytes 1179648 | tf_op jit(solution)/shard_map/all_to_all | solution.py:232
  134.5 0.1 reduce_sum.21
  134.7 0.7 copy.35
  135.4 12.0 %all-to-all-start.4 = ((bf16[16,9,4,128]{3,2,1,0:T(4,128)(2,1)}), bf16[16,9,4,128]{3,2,1,0:T(4,128)(2,1)S(1)}, u32[]{:S(2)}, u32[]{:S(2)}) async-start(bf16[16,9,4,128]{3,2,1,0:T(4,128)(2,1)} %copy.35), calls=%async_computation.4 | async-start | bytes 294912 | tf_op jit(solution)/shard_map/all_to_all | solution.py:235
  147.4 1.1 shard_map.106
  148.5 4.3 %collective-permute-start.5 = (bf16[2,192,256]{2,1,0:T(8,128)(2,1)S(1)}, bf16[2,192,256]{2,1,0:T(8,128)(2,1)S(1)}, u32[]{:S(2)}, u32[]{:S(2)}) collective-permute-start(bf16[2,192,256]{2,1,0:T(8,128)(2,1)S(1)} %get-tuple-element.21), channel_id=1, source_target_pairs={{0,6},{2,0},{4,2},{6,4},{1,7},{3,1},{5,3},{7,5},{8,14},{10,8},{12,... | collective-permute-start | bytes 589832 | tf_op jit(solution)/shard_map/ppermute | solution.py:164
  152.8 3.4 %collective-permute-start.6 = (bf16[2,192,256]{2,1,0:T(8,128)(2,1)S(1)}, bf16[2,192,256]{2,1,0:T(8,128)(2,1)S(1)}, u32[]{:S(2)}, u32[]{:S(2)}) collective-permute-start(bf16[2,192,256]{2,1,0:T(8,128)(2,1)S(1)} %get-tuple-element.22), channel_id=1, source_target_pairs={{0,4},{2,6},{4,0},{6,2},{1,5},{3,7},{5,1},{7,3},{8,12},{10,14},{12... | collective-permute-start | bytes 589832 | tf_op jit(solution)/shard_map/ppermute | solution.py:164
  156.3 1.9 %collective-permute-start.7 = (bf16[2,192,256]{2,1,0:T(8,128)(2,1)S(1)}, bf16[2,192,256]{2,1,0:T(8,128)(2,1)S(1)}, u32[]{:S(2)}, u32[]{:S(2)}) collective-permute-start(bf16[2,192,256]{2,1,0:T(8,128)(2,1)S(1)} %get-tuple-element.23), channel_id=1, source_target_pairs={{0,2},{2,4},{4,6},{6,0},{1,3},{3,5},{5,7},{7,1},{8,10},{10,12},{12... | collective-permute-start | bytes 589832 | tf_op jit(solution)/shard_map/ppermute | solution.py:164
  158.2 2.8 %collective-permute-done.6.refs_2_ = bf16[2,192,256]{2,1,0:T(8,128)(2,1)S(1)} collective-permute-done((bf16[2,192,256]{2,1,0:T(8,128)(2,1)S(1)}, bf16[2,192,256]{2,1,0:T(8,128)(2,1)S(1)}, u32[]{:S(2)}, u32[]{:S(2)}) %collective-permute-start.6) | collective-permute-done | bytes 196640 | tf_op jit(solution)/shard_map/ppermute | solution.py:164
  161.1 5.8 %collective-permute-done.7.refs_3_ = bf16[2,192,256]{2,1,0:T(8,128)(2,1)S(1)} collective-permute-done((bf16[2,192,256]{2,1,0:T(8,128)(2,1)S(1)}, bf16[2,192,256]{2,1,0:T(8,128)(2,1)S(1)}, u32[]{:S(2)}, u32[]{:S(2)}) %collective-permute-start.7) | collective-permute-done | bytes 196640 | tf_op jit(solution)/shard_map/ppermute | solution.py:164
  166.9 2.0 %collective-permute-start.8 = (bf16[4,192,256]{2,1,0:T(8,128)(2,1)S(1)}, bf16[4,192,256]{2,1,0:T(8,128)(2,1)S(1)}, u32[]{:S(2)}, u32[]{:S(2)}) collective-permute-start(bf16[4,192,256]{2,1,0:T(8,128)(2,1)S(1)} %pad_maximum_fusion), channel_id=1, source_target_pairs={{0,1},{1,0},{2,3},{3,2},{4,5},{5,4},{6,7},{7,6},{8,9},{9,8},{10,11... | collective-permute-start | bytes 1179656 | tf_op jit(solution)/shard_map/ppermute | solution.py:168
  169.0 8.7 %collective-permute-done.8.refs_4_ = bf16[4,192,256]{2,1,0:T(8,128)(2,1)S(1)} collective-permute-done((bf16[4,192,256]{2,1,0:T(8,128)(2,1)S(1)}, bf16[4,192,256]{2,1,0:T(8,128)(2,1)S(1)}, u32[]{:S(2)}, u32[]{:S(2)}) %collective-permute-start.8) | collective-permute-done | bytes 393248 | tf_op jit(solution)/shard_map/ppermute | solution.py:168
  177.7 1.5 shard_map.107
  179.1 0.1 convert_reduce_fusion
  179.3 0.7 fusion.1
  (39 shorter events, 0.8 us)
Async XLA Ops:
  0.6 0.9 copy-start.1
  1.5 0.7 copy-start.2
  2.2 0.7 copy-start.3
  2.9 0.7 copy-start.4
  2.9 0.7 copy-start.5
  61.7 18.1 %all-to-all-start.2 = ((bf16[4,192,384]{2,1,0:T(8,128)(2,1)}), bf16[4,192,384]{2,1,0:T(8,128)(2,1)S(1)}, u32[]{:S(2)}, u32[]{:S(2)}) async-start(bf16[4,192,384]{2,1,0:T(8,128)(2,1)} %broadcast_in_dim.26), calls=%async_computation.2 | async-start | bytes 1179648 | tf_op jit(solution)/shard_map/all_to_all | solution.py:159
  72.6 17.9 %copy-start.6 = (f32[1536]{0:T(1024)S(1)}, f32[1536]{0:T(1024)}, u32[]{:S(2)}) copy-start(f32[1536]{0:T(1024)} %param.10) | copy-start | bytes 18436
  80.5 15.3 %all-to-all-start.1 = ((bf16[16,32,256]{2,1,0:T(8,128)(2,1)}), bf16[16,32,256]{2,1,0:T(8,128)(2,1)S(1)}, u32[]{:S(2)}, u32[]{:S(2)}) async-start(bf16[16,32,256]{2,1,0:T(8,128)(2,1)} %bitcast.10), calls=%async_computation.1 | async-start | bytes 524288 | tf_op jit(solution)/shard_map/all_to_all | solution.py:198
  88.3 25.5 %collective-permute-start.3 = (bf16[4,192,384]{2,1,0:T(8,128)(2,1)S(1)}, bf16[4,192,384]{2,1,0:T(8,128)(2,1)S(1)}, u32[]{:S(2)}, u32[]{:S(2)}) collective-permute-start(bf16[4,192,384]{2,1,0:T(8,128)(2,1)S(1)} %all-to-all-done.2), channel_id=1, source_target_pairs={{0,8},{8,0},{1,9},{9,1},{2,10},{10,2},{3,11},{11,3},{4,12},{12,4},... | collective-permute-start | bytes 1769480 | tf_op jit(solution)/shard_map/ppermute | solution.py:168
  96.9 11.0 %collective-permute-start = (bf16[2,192,256]{2,1,0:T(8,128)(2,1)S(1)}, bf16[2,192,256]{2,1,0:T(8,128)(2,1)S(1)}, u32[]{:S(2)}, u32[]{:S(2)}) collective-permute-start(bf16[2,192,256]{2,1,0:T(8,128)(2,1)S(1)} %get-tuple-element.15.refs_0_), channel_id=1, source_target_pairs={{0,2},{2,4},{4,6},{6,0},{1,3},{3,5},{5,7},{7,1},{8,10},{10,12},{12... | collective-permute-start | bytes 589832 | tf_op jit(solution)/shard_map/ppermute | solution.py:164
  100.0 11.1 %collective-permute-start.1 = (bf16[2,192,256]{2,1,0:T(8,128)(2,1)S(1)}, bf16[2,192,256]{2,1,0:T(8,128)(2,1)S(1)}, u32[]{:S(2)}, u32[]{:S(2)}) collective-permute-start(bf16[2,192,256]{2,1,0:T(8,128)(2,1)S(1)} %get-tuple-element.15.refs_0_), channel_id=1, source_target_pairs={{0,4},{2,6},{4,0},{6,2},{1,5},{3,7},{5,1},{7,3},{8,12},{10,14},{12... | collective-permute-start | bytes 589832 | tf_op jit(solution)/shard_map/ppermute | solution.py:164
  104.4 8.1 %collective-permute-start.2 = (bf16[2,192,256]{2,1,0:T(8,128)(2,1)S(1)}, bf16[2,192,256]{2,1,0:T(8,128)(2,1)S(1)}, u32[]{:S(2)}, u32[]{:S(2)}) collective-permute-start(bf16[2,192,256]{2,1,0:T(8,128)(2,1)S(1)} %get-tuple-element.15.refs_0_), channel_id=1, source_target_pairs={{0,6},{2,0},{4,2},{6,4},{1,7},{3,1},{5,3},{7,5},{8,14},{10,8},{12,... | collective-permute-start | bytes 589832 | tf_op jit(solution)/shard_map/ppermute | solution.py:164
  112.5 1.3 copy-start
  116.9 5.0 %collective-permute-start.4 = (bf16[4,192,384]{2,1,0:T(8,128)(2,1)S(1)}, bf16[4,192,384]{2,1,0:T(8,128)(2,1)S(1)}, u32[]{:S(2)}, u32[]{:S(2)}) collective-permute-start(bf16[4,192,384]{2,1,0:T(8,128)(2,1)S(1)} %bitcast.53), channel_id=1, source_target_pairs={{0,8},{8,0},{1,9},{9,1},{2,10},{10,2},{3,11},{11,3},{4,12},{12,4},... | collective-permute-start | bytes 1769480 | tf_op jit(solution)/shard_map/ppermute | solution.py:168
  135.4 43.7 %all-to-all-start.4 = ((bf16[16,9,4,128]{3,2,1,0:T(4,128)(2,1)}), bf16[16,9,4,128]{3,2,1,0:T(4,128)(2,1)S(1)}, u32[]{:S(2)}, u32[]{:S(2)}) async-start(bf16[16,9,4,128]{3,2,1,0:T(4,128)(2,1)} %copy.35), calls=%async_computation.4 | async-start | bytes 294912 | tf_op jit(solution)/shard_map/all_to_all | solution.py:235
  148.5 9.7 %collective-permute-start.5 = (bf16[2,192,256]{2,1,0:T(8,128)(2,1)S(1)}, bf16[2,192,256]{2,1,0:T(8,128)(2,1)S(1)}, u32[]{:S(2)}, u32[]{:S(2)}) collective-permute-start(bf16[2,192,256]{2,1,0:T(8,128)(2,1)S(1)} %get-tuple-element.21), channel_id=1, source_target_pairs={{0,6},{2,0},{4,2},{6,4},{1,7},{3,1},{5,3},{7,5},{8,14},{10,8},{12,... | collective-permute-start | bytes 589832 | tf_op jit(solution)/shard_map/ppermute | solution.py:164
  152.8 8.2 %collective-permute-start.6 = (bf16[2,192,256]{2,1,0:T(8,128)(2,1)S(1)}, bf16[2,192,256]{2,1,0:T(8,128)(2,1)S(1)}, u32[]{:S(2)}, u32[]{:S(2)}) collective-permute-start(bf16[2,192,256]{2,1,0:T(8,128)(2,1)S(1)} %get-tuple-element.22), channel_id=1, source_target_pairs={{0,4},{2,6},{4,0},{6,2},{1,5},{3,7},{5,1},{7,3},{8,12},{10,14},{12... | collective-permute-start | bytes 589832 | tf_op jit(solution)/shard_map/ppermute | solution.py:164
  156.3 10.6 %collective-permute-start.7 = (bf16[2,192,256]{2,1,0:T(8,128)(2,1)S(1)}, bf16[2,192,256]{2,1,0:T(8,128)(2,1)S(1)}, u32[]{:S(2)}, u32[]{:S(2)}) collective-permute-start(bf16[2,192,256]{2,1,0:T(8,128)(2,1)S(1)} %get-tuple-element.23), channel_id=1, source_target_pairs={{0,2},{2,4},{4,6},{6,0},{1,3},{3,5},{5,7},{7,1},{8,10},{10,12},{12... | collective-permute-start | bytes 589832 | tf_op jit(solution)/shard_map/ppermute | solution.py:164
  166.9 10.7 %collective-permute-start.8 = (bf16[4,192,256]{2,1,0:T(8,128)(2,1)S(1)}, bf16[4,192,256]{2,1,0:T(8,128)(2,1)S(1)}, u32[]{:S(2)}, u32[]{:S(2)}) collective-permute-start(bf16[4,192,256]{2,1,0:T(8,128)(2,1)S(1)} %pad_maximum_fusion), channel_id=1, source_target_pairs={{0,1},{1,0},{2,3},{3,2},{4,5},{5,4},{6,7},{7,6},{8,9},{9,8},{10,11... | collective-permute-start | bytes 1179656 | tf_op jit(solution)/shard_map/ppermute | solution.py:168

commit v5 on v4

--- a/solution.py
+++ b/solution.py
@@ -26,14 +26,15 @@
     return lax.dot_general(a, b, (((0,), (0,)), ((), ())), preferred_element_type=f32)
 
 
-def call(kernel, outs, *args, limit=12):
+def call(kernel, outs, *args, limit=12, scratch=(), away=False):
     vmem = pl.BlockSpec(memory_space=pltpu.VMEM)
     smem = pl.BlockSpec(memory_space=pltpu.SMEM)
     return pl.pallas_call(
         kernel,
-        in_specs=[smem if a.shape == (2,) else vmem for a in args],
+        in_specs=[pl.BlockSpec(memory_space=pltpu.HBM) if away else smem if a.shape == (2,) else vmem for a in args],
         out_specs=[vmem] * len(outs),
         out_shape=[jax.ShapeDtypeStruct(s, d) for s, d in outs],
+        scratch_shapes=list(scratch),
         compiler_params=pltpu.CompilerParams(vmem_limit_bytes=limit << 20),
         interpret=INTERPRET,
     )(*args)
@@ -44,14 +45,22 @@
     return ((p // 12) % 2) * 96 + (((p // 24) % 4) * 2 + core) * 12 + p % 12
 
 
-def send_kernel(frames_ref, owner_ref, valid_ref, out_ref):
+def send_kernel(frames_hbm, owner_hbm, valid_hbm, out_ref, frames_ref, owner_ref, valid_ref, sems):
+    pairs = ((owner_hbm, owner_ref), (valid_hbm, valid_ref), (frames_hbm, frames_ref))
+    copies = [pltpu.make_async_copy(a, b, sems.at[i]) for i, (a, b) in enumerate(pairs)]
+    for copy in copies:
+        copy.start()
+    for copy in copies:
+        copy.wait()
     rows, width = frames_ref.shape
     slots, lanes = out_ref.shape
+    far = slots // 16
     owner = owner_ref[...]
     down = jnp.transpose(jnp.broadcast_to(owner, (rows, rows)))
     earlier = lax.broadcasted_iota(i32, (rows, rows), 0) < lax.broadcasted_iota(i32, (rows, rows), 1)
     slot = jnp.sum(jnp.where((down == owner) & earlier, 1.0, 0.0), axis=0, keepdims=True).astype(i32)
-    hit = lax.broadcasted_iota(i32, (slots, rows), 0) == owner * 2 + slot
+    place = ((owner % 8) * far + owner // 8) * 2 + slot
+    hit = lax.broadcasted_iota(i32, (slots, rows), 0) == place
     placed = nn(jnp.where(hit, 1.0, 0.0).astype(bf16), frames_ref[...])
     live = jnp.sum(jnp.where(hit & (valid_ref[...] > 0), 1.0, 0.0), axis=1, keepdims=True)
     pad = lax.broadcasted_iota(i32, (slots, lanes - width), 1) == 0
@@ -59,9 +68,8 @@
 
 
 def turn_kernel(own_ref, rows_ref, out_ref, live_ref):
-    width, slots = out_ref.shape[1:]
+    width, slots = out_ref.shape
     peers = slots // 2
-    far = peers // 8
     lanes = rows_ref.shape[-1]
     place = lax.broadcasted_iota(i32, (width, lanes), 0)
     column = lax.broadcasted_iota(i32, (width, lanes), 1)
@@ -70,37 +78,39 @@
     pick = jnp.concatenate([pick, flag], axis=0)
     source = lax.broadcasted_iota(i32, (slots, slots), 0)
     target = lax.broadcasted_iota(i32, (slots, slots), 1)
-    loader = target % peers
-    order = (source == ((loader % 8) * far + loader // 8) * 2 + target // peers).astype(bf16)
-    for y in range(2):
-        rows = jnp.concatenate([rows_ref[n, y] for n in range(8)], axis=0)
-        ordered = nn(nt(pick, rows).astype(bf16), order)
-        out_ref[y] = ordered[:width].astype(bf16)
+    order = (source == (target % peers) * 2 + target // peers).astype(bf16)
+    ordered = nn(nt(pick, rows_ref[...]).astype(bf16), order)
+    out_ref[...] = ordered[:width].astype(bf16)
     live_ref[...] = ordered[width : width + 8]
 
 
-def block_of(own_ref, k, blocks, relative=False):
+def block_of(own_ref, k, blocks):
+    n = blocks // 2
     x, y = own_ref[0] // 2, own_ref[0] % 2
-    y = (y + k) % 2 if relative else k % 2
-    return ((x + (blocks // 2 - k // 2)) % (blocks // 2)) * 2 + y
+    return ((x + n - k % n) % n) * 2 + (y + k // n) % 2
 
 
 def norm_kernel(own_ref, live_ref, gain_ref, *refs):
-    normed_ref = refs[-1]
+    near_refs, across_ref, normed_ref = refs[:-2], refs[-2], refs[-1]
     blocks, width, slots = normed_ref.shape
     total = blocks * width
     live = live_ref[0:1, :]
+
+    def block(k):
+        n = blocks // 2
+        return (near_refs[k][...] if k < n else across_ref[k - n]).astype(f32)
+
     s = jnp.zeros((1, slots), f32)
     for k in range(blocks):
-        s = s + jnp.sum(refs[k // 2][k % 2].astype(f32), axis=0, keepdims=True)
+        s = s + jnp.sum(block(k), axis=0, keepdims=True)
     mean = s * (1.0 / total)
     s = jnp.zeros((1, slots), f32)
     for k in range(blocks):
-        c = refs[k // 2][k % 2].astype(f32) - mean
+        c = block(k) - mean
         s = s + jnp.sum(c * c, axis=0, keepdims=True)
     inv = lax.rsqrt(s * (1.0 / total) + epsilon)
     for k in range(blocks):
-        c = refs[k // 2][k % 2].astype(f32) - mean
+        c = block(k) - mean
         normed_ref[k] = (c * inv * gain_ref[block_of(own_ref, k, blocks)] * live).astype(bf16)
 
 
@@ -136,8 +146,8 @@
 def backward_kernel(own_ref, wa_ref, wb_ref, delta_ref, *partial_refs):
     blocks = 2 * len(partial_refs)
     for k in range(blocks):
-        w = w_block(wa_ref, wb_ref, block_of(own_ref, k, blocks, True))
-        partial_refs[k // 2][k % 2] = nn(w, delta_ref[...]).astype(bf16)
+        w = w_block(wa_ref, wb_ref, block_of(own_ref, k, blocks))
+        partial_refs[k % (blocks // 2)][k // (blocks // 2)] = nn(w, delta_ref[...]).astype(bf16)
 
 
 def join_kernel(own_ref, *refs):
@@ -168,6 +178,10 @@
     return lax.ppermute(x, axis, [(0, 1), (1, 0)])
 
 
+def stay(x):
+    return x if INTERPRET else pltpu.with_memory_space_constraint(x, pltpu.HBM)
+
+
 def tiles(x):
     return x.reshape(x.shape[0] // 4, 4, x.shape[1] // 128, 128).transpose(2, 0, 1, 3)
 
@@ -186,16 +200,24 @@
     core = lax.axis_index("co").astype(i32)
     own = jnp.stack([lax.axis_index(MP).astype(i32), core])
 
+    (sent,) = call(
+        send_kernel,
+        [((slots, lanes), bf16)],
+        *map(stay, (frames, frame_owner.reshape(1, rows), frame_valid.reshape(1, rows))),
+        scratch=[
+            pltpu.VMEM((rows, width), bf16),
+            pltpu.VMEM((1, rows), i32),
+            pltpu.VMEM((1, rows), i32),
+            pltpu.SemaphoreType.DMA((3,)),
+        ],
+        away=True,
+    )
+    sent = lax.all_to_all(sent.reshape(8, 2 * far, lanes), ("zl", "yh", "co"), 0, 0, tiled=True)
     shard = tiles(jnp.concatenate([value_weight, gate_weight], axis=1)).reshape(wt, 4, 128)
-    (sent,) = call(
-        send_kernel, [((slots, lanes), bf16)], frames, frame_owner.reshape(1, rows), frame_valid.reshape(1, rows)
-    )
-    sent = sent.reshape(far, 4, 4, halves, 128).transpose(0, 3, 1, 2, 4).reshape(far, 4 * halves, 4, 128)
-    sent = jnp.concatenate([jnp.broadcast_to(shard[None], (far,) + shard.shape), sent], axis=1)
-    got = lax.all_to_all(sent, "zh", 0, 0, tiled=True)
-    rows_z = got[:, wt:].reshape(far, halves, 8, 2, 128).transpose(2, 0, 3, 1, 4).reshape(8, 1, 2 * far, lanes)
-    rows_z = jnp.broadcast_to(rows_z, (8, 2, 2 * far, lanes)).reshape(16, 2 * far, lanes)
-    rows_y = lax.all_to_all(rows_z, ("zl", "yh", "co", "yl"), 0, 0, tiled=True)
+    shard = jnp.broadcast_to(shard[None], (far,) + shard.shape)
+    sent = sent.reshape(8, far, 2, halves, 128).transpose(1, 3, 0, 2, 4).reshape(far, 4 * halves, 4, 128)
+    got = lax.all_to_all(jnp.concatenate([shard, sent], axis=1), "zh", 0, 0, tiled=True)
+    rows_z = got[:, wt:].reshape(far, halves, 16, 128).transpose(0, 2, 1, 3).reshape(slots, lanes)
     w_rows = got[:, :wt].reshape(far, columns // 128, group, 128).transpose(0, 2, 1, 3)
     w_rows = w_rows.reshape(far * group, columns)
     w_own = spread(w_rows, NEAR, 4)
@@ -204,11 +226,13 @@
     w_other = w_other.reshape(4, blocks, 2 * group, columns)
     turned, live = call(
         turn_kernel,
-        [((2, width, slots), bf16), ((8, slots), f32)],
+        [((width, slots), bf16), ((8, slots), f32)],
         own,
-        rows_y.reshape(8, 2, 2 * far, lanes),
+        rows_z,
     )
     whole = [turned] + [hop(turned, dx) for dx in range(1, blocks // 2)]
+    stacked = jnp.stack(whole)
+    whole.append(swap(stacked, "yl"))
     gain = norm_gain.reshape(blocks, 2, 4, 2, 12).transpose(0, 3, 2, 1, 4)
     gain = jnp.where(core == 0, gain, gain[:, ::-1]).reshape(blocks, width, 1)
     (normed,) = call(norm_kernel, [((blocks, width, slots), bf16)], own, live, gain, *whole)

time: 181 us -> 179 us (0.989)
  starting transfers between devices: 58.3 us -> 70.8 us
  blocking collectives: 69 us -> 58.9 us
  waiting for transfers between devices: 35.3 us -> 32 us
  local copies, waits for them, and re-layouts: 7.05 us -> 3.77 us
    all_to_all x1, blocking collectives: 56.6 us -> 43.7 us  [body(): lax.all_to_all(jnp.concatenate([shard, sent], axis=1), 'zh', 0, 0, tiled=...]
    all_to_all x1, starting transfers between devices: 7.81 us -> 17.4 us  [body(): lax.all_to_all(sent.reshape(8, 2 * far, lanes), ('zl', 'yh', 'co'), 0, 0,...]
    ppermute x3 -> x4, waiting for transfers between devices: 10.3 us -> 18.3 us  [swap(): return lax.ppermute(x, axis, [(0, 1), (1, 0)])]
    ppermute x3 -> x4, starting transfers between devices: 7.56 us -> 15.3 us  [swap(): return lax.ppermute(x, axis, [(0, 1), (1, 0)])]
    all_to_all x1, waiting for transfers between devices: 6.92 us -> 0.01 us  [spread(): lax.all_to_all(jnp.broadcast_to(x[None], (count,) + x.shape), axis, 0, 0,...]
    ppermute x6, waiting for transfers between devices: 13.2 us -> 8.66 us  [hop(): return lax.ppermute(x, 'x', [(i, (i + step) % n) for i in range(n)])]
    all_to_all x1, blocking collectives: 12.4 us -> 15.2 us  [body(): dw_y = lax.all_to_all(dw_c, NEAR, 0, 0, tiled=True)]
    unnamed x19 -> x10, local copies, waits for them, and re-layouts: 2.57 us -> 0.14 us
  transfers between devices with their start and end apart: 12 -> 13, of which waited for: 8 -> 6; matrix products, arithmetic and copies ran while one was open for 1% -> 1% of each run, Pallas kernels for 3% -> 3%
where the time goes in v5:
time: 179 us; the launch traced here: 178 us
  starting transfers between devices  70.8 us (40%)
  blocking collectives  58.9 us (33%)
  waiting for transfers between devices  32 us (18%)
  Pallas kernels  9.86 us (6%)
  local copies, waits for them, and re-layouts  3.77 us (2%)
    all_to_all x1, blocking collectives, body(): lax.all_to_all(jnp.concatenate([shard, sent], axis=1), 'zh', 0, 0, tiled=...  43.7 us
    ppermute x6, starting transfers between devices, hop(): return lax.ppermute(x, 'x', [(i, (i + step) % n) for i in range(n)])  18.4 us
    ppermute x4, waiting for transfers between devices, swap(): return lax.ppermute(x, axis, [(0, 1), (1, 0)])  18.3 us
    all_to_all x1, starting transfers between devices, body(): lax.all_to_all(sent.reshape(8, 2 * far, lanes), ('zl', 'yh', 'co'), 0, 0,...  17.4 us
    ppermute x4, starting transfers between devices, swap(): return lax.ppermute(x, axis, [(0, 1), (1, 0)])  15.3 us
    all_to_all x1, blocking collectives, body(): dw_y = lax.all_to_all(dw_c, NEAR, 0, 0, tiled=True)  15.2 us
    all_to_all x1, starting transfers between devices, body(): dw_z = lax.all_to_all(dw_y, 'zh', 0, 0, tiled=True)  10.1 us
    pallas_call x6, Pallas kernels, call(): pl.pallas_call(kernel, in_specs=[pl.BlockSpec(memory_space=pltpu.HBM) if...  9.86 us
  transfers between devices with their start and end apart: 13, of which 6 were waited for; matrix products, arithmetic and copies ran while one was open for 1% of the time, Pallas kernels for 3%

profile of v5, /device:TPU:1, one launch (start us, length us, event | category | flops | bytes accessed | tf_op | source)
XLA Modules:
  0.0 177.9 jit_solution(15967757211078799317)
XLA Ops:
  0.6 2.0 %shard_map.102 = bf16[256,256]{1,0:T(8,128)(2,1)} custom-call(bf16[192,192]{1,0:T(8,128)(2,1)} %frames_hbm.1, s32[1,192]{1,0:T(1,128)} %bitcast.79, s32[1,192]{1,0:T(1,128)} %bitcast.80), custom_call_target="tpu_custom_call" | custom-call | tf_op jit(solution)/shard_map/pallas_call | solution.py:32
  2.6 17.4 %all-to-all-start = ((bf16[8,32,256]{2,1,0:T(8,128)(2,1)}), bf16[8,32,256]{2,1,0:T(8,128)(2,1)S(1)}, u32[]{:S(2)}, u32[]{:S(2)}) async-start(bf16[8,32,256]{2,1,0:T(8,128)(2,1)} %bitcast.6), calls=%async_computation | async-start | bytes 262144 | tf_op jit(solution)/shard_map/all_to_all | solution.py:215
  20.0 0.8 pad_maximum_fusion.3
  20.8 5.0 %all-to-all-done = bf16[8,32,256]{2,1,0:T(8,128)(2,1)S(1)} async-done(((bf16[8,32,256]{2,1,0:T(8,128)(2,1)}), bf16[8,32,256]{2,1,0:T(8,128)(2,1)S(1)}, u32[]{:S(2)}, u32[]{:S(2)}) %all-to-all-start) | async-done | bytes 131104 | tf_op jit(solution)/shard_map/all_to_all | solution.py:215
  25.9 0.1 copy.27
  26.0 0.2 pad_maximum_fusion.2
  26.2 43.7 %all_to_all.25 = bf16[16,17,4,128]{3,2,1,0:T(4,128)(2,1)S(1)} all-to-all(bf16[16,17,4,128]{3,2,1,0:T(4,128)(2,1)S(1)} %pad_maximum_fusion.2), channel_id=1, replica_groups=mesh['zh'=16,'zl'=2,'yh'=2,'co'=2,'x'=4,'yl'=2] {'zh'}, dimensions={0} | all-to-all | bytes 557056 | tf_op jit(solution)/shard_map/all_to_all | solution.py:219
  69.9 0.1 slice.33
  70.0 0.1 copy.33
  70.2 0.9 broadcast_in_dim.17
  71.1 9.6 %all-to-all-start.2 = ((bf16[4,192,384]{2,1,0:T(8,128)(2,1)}), bf16[4,192,384]{2,1,0:T(8,128)(2,1)S(1)}, u32[]{:S(2)}, u32[]{:S(2)}) async-start(bf16[4,192,384]{2,1,0:T(8,128)(2,1)} %broadcast_in_dim.17), calls=%async_computation.2 | async-start | bytes 1179648 | tf_op jit(solution)/shard_map/all_to_all | solution.py:169
  80.7 0.1 pad_add_fusion.own_ref
  80.8 0.1 copy.37
  80.8 0.0 copy-start.1
  80.9 0.1 copy.29
  81.0 0.9 shard_map.103
  82.0 3.1 %collective-permute-start = (bf16[192,256]{1,0:T(8,128)(2,1)S(1)}, bf16[192,256]{1,0:T(8,128)(2,1)S(1)}, u32[]{:S(2)}, u32[]{:S(2)}) collective-permute-start(bf16[192,256]{1,0:T(8,128)(2,1)S(1)} %get-tuple-element.15.refs_0_), channel_id=1, source_target_pairs={{0,2},{2,4},{4,6},{6,0},{1,3},{3,5},{5,7},{7,1},{8,10},{10,12},{12... | collective-permute-start | bytes 294920 | tf_op jit(solution)/shard_map/ppermute | solution.py:174
  85.1 4.4 %collective-permute-start.1 = (bf16[192,256]{1,0:T(8,128)(2,1)S(1)}, bf16[192,256]{1,0:T(8,128)(2,1)S(1)}, u32[]{:S(2)}, u32[]{:S(2)}) collective-permute-start(bf16[192,256]{1,0:T(8,128)(2,1)S(1)} %get-tuple-element.15.refs_0_), channel_id=1, source_target_pairs={{0,4},{2,6},{4,0},{6,2},{1,5},{3,7},{5,1},{7,3},{8,12},{10,14},{12... | collective-permute-start | bytes 294920 | tf_op jit(solution)/shard_map/ppermute | solution.py:174
  89.5 3.1 %collective-permute-start.2 = (bf16[192,256]{1,0:T(8,128)(2,1)S(1)}, bf16[192,256]{1,0:T(8,128)(2,1)S(1)}, u32[]{:S(2)}, u32[]{:S(2)}) collective-permute-start(bf16[192,256]{1,0:T(8,128)(2,1)S(1)} %get-tuple-element.15.refs_0_), channel_id=1, source_target_pairs={{0,6},{2,0},{4,2},{6,4},{1,7},{3,1},{5,3},{7,5},{8,14},{10,8},{12,... | collective-permute-start | bytes 294920 | tf_op jit(solution)/shard_map/ppermute | solution.py:174
  92.5 0.0 all-to-all-done.2
  92.6 6.8 %collective-permute-start.4 = (bf16[4,192,384]{2,1,0:T(8,128)(2,1)S(1)}, bf16[4,192,384]{2,1,0:T(8,128)(2,1)S(1)}, u32[]{:S(2)}, u32[]{:S(2)}) collective-permute-start(bf16[4,192,384]{2,1,0:T(8,128)(2,1)S(1)} %all-to-all-done.2), channel_id=1, source_target_pairs={{0,8},{8,0},{1,9},{9,1},{2,10},{10,2},{3,11},{11,3},{4,12},{12,4},... | collective-permute-start | bytes 1769480 | tf_op jit(solution)/shard_map/ppermute | solution.py:178
  99.4 0.1 pad_maximum_fusion
  99.4 2.3 %collective-permute-start.3 = (bf16[4,192,256]{2,1,0:T(8,128)(2,1)S(1)}, bf16[4,192,256]{2,1,0:T(8,128)(2,1)S(1)}, u32[]{:S(2)}, u32[]{:S(2)}) collective-permute-start(bf16[4,192,256]{2,1,0:T(8,128)(2,1)S(1)} %pad_maximum_fusion), channel_id=1, source_target_pairs={{0,1},{1,0},{2,3},{3,2},{4,5},{5,4},{6,7},{7,6},{8,9},{9,8},{10,11... | collective-permute-start | bytes 1179656 | tf_op jit(solution)/shard_map/ppermute | solution.py:178
  101.8 0.1 reshape.85
  101.9 0.2 rev.3
  102.2 0.3 reshape.98.gain_ref
  102.5 8.3 %collective-permute-done.3.refs_4_ = bf16[4,192,256]{2,1,0:T(8,128)(2,1)S(1)} collective-permute-done((bf16[4,192,256]{2,1,0:T(8,128)(2,1)S(1)}, bf16[4,192,256]{2,1,0:T(8,128)(2,1)S(1)}, u32[]{:S(2)}, u32[]{:S(2)}) %collective-permute-start.3) | collective-permute-done | bytes 393248 | tf_op jit(solution)/shard_map/ppermute | solution.py:178
  110.8 1.3 shard_map.104.normed_ref
  112.1 3.1 %shard_map.105 = (bf16[2,192,128]{2,1,0:T(8,128)(2,1)}, bf16[4,8,24,384]{3,2,1,0:T(8,128)(2,1)S(1)}, bf16[4,8,24,384]{3,2,1,0:T(8,128)(2,1)S(1)}, bf16[384,256]{1,0:T(8,128)(2,1)S(1)}) custom-call(s32[2]{0:T(128)S(1)} %pad_add_fusion.own_ref, bf16[8,192,256]{2,1,0:T(8,128)(2,1)S(1)} %shard_map.104.normed_ref, f32[8,256]{1,0:T(8,128)S(1)} %get-tuple-element.14.live_ref, ...), custom_call_target="tpu_custom_call" | custom-call | tf_op jit(solution)/shard_map/pallas_call | solution.py:32
  115.2 3.9 %collective-permute-start.5 = (bf16[4,192,384]{2,1,0:T(8,128)(2,1)S(1)}, bf16[4,192,384]{2,1,0:T(8,128)(2,1)S(1)}, u32[]{:S(2)}, u32[]{:S(2)}) collective-permute-start(bf16[4,192,384]{2,1,0:T(8,128)(2,1)S(1)} %bitcast.62), channel_id=1, source_target_pairs={{0,8},{8,0},{1,9},{9,1},{2,10},{10,2},{3,11},{11,3},{4,12},{12,4},... | collective-permute-start | bytes 1769480 | tf_op jit(solution)/shard_map/ppermute | solution.py:178
  119.2 1.6 collective-permute-done.5
  120.8 0.2 fusion
  121.0 15.2 %all_to_all.26 = bf16[4,192,384]{2,1,0:T(8,128)(2,1)S(1)} all-to-all(bf16[4,192,384]{2,1,0:T(8,128)(2,1)S(1)} %fusion), channel_id=1, replica_groups=mesh['zh'=16,'zl'=2,'yh'=2,'co'=2,'x'=4,'yl'=2] {'zl','yh'}, dimensions={0} | all-to-all | bytes 1179648 | tf_op jit(solution)/shard_map/all_to_all | solution.py:256
  136.2 0.1 reduce_sum.21
  136.4 0.7 copy.35
  137.1 10.1 %all-to-all-start.4 = ((bf16[16,9,4,128]{3,2,1,0:T(4,128)(2,1)}), bf16[16,9,4,128]{3,2,1,0:T(4,128)(2,1)S(1)}, u32[]{:S(2)}, u32[]{:S(2)}) async-start(bf16[16,9,4,128]{3,2,1,0:T(4,128)(2,1)} %copy.35), calls=%async_computation.4 | async-start | bytes 294912 | tf_op jit(solution)/shard_map/all_to_all | solution.py:259
  147.2 1.1 shard_map.106
  148.3 2.7 %collective-permute-start.6 = (bf16[2,192,256]{2,1,0:T(8,128)(2,1)S(1)}, bf16[2,192,256]{2,1,0:T(8,128)(2,1)S(1)}, u32[]{:S(2)}, u32[]{:S(2)}) collective-permute-start(bf16[2,192,256]{2,1,0:T(8,128)(2,1)S(1)} %get-tuple-element.21), channel_id=1, source_target_pairs={{0,6},{2,0},{4,2},{6,4},{1,7},{3,1},{5,3},{7,5},{8,14},{10,8},{12,... | collective-permute-start | bytes 589832 | tf_op jit(solution)/shard_map/ppermute | solution.py:174
  151.1 3.2 %collective-permute-start.7 = (bf16[2,192,256]{2,1,0:T(8,128)(2,1)S(1)}, bf16[2,192,256]{2,1,0:T(8,128)(2,1)S(1)}, u32[]{:S(2)}, u32[]{:S(2)}) collective-permute-start(bf16[2,192,256]{2,1,0:T(8,128)(2,1)S(1)} %get-tuple-element.22), channel_id=1, source_target_pairs={{0,4},{2,6},{4,0},{6,2},{1,5},{3,7},{5,1},{7,3},{8,12},{10,14},{12... | collective-permute-start | bytes 589832 | tf_op jit(solution)/shard_map/ppermute | solution.py:174
  154.3 1.9 %collective-permute-start.8 = (bf16[2,192,256]{2,1,0:T(8,128)(2,1)S(1)}, bf16[2,192,256]{2,1,0:T(8,128)(2,1)S(1)}, u32[]{:S(2)}, u32[]{:S(2)}) collective-permute-start(bf16[2,192,256]{2,1,0:T(8,128)(2,1)S(1)} %get-tuple-element.23), channel_id=1, source_target_pairs={{0,2},{2,4},{4,6},{6,0},{1,3},{3,5},{5,7},{7,1},{8,10},{10,12},{12... | collective-permute-start | bytes 589832 | tf_op jit(solution)/shard_map/ppermute | solution.py:174
  156.2 3.0 %collective-permute-done.7.refs_2_ = bf16[2,192,256]{2,1,0:T(8,128)(2,1)S(1)} collective-permute-done((bf16[2,192,256]{2,1,0:T(8,128)(2,1)S(1)}, bf16[2,192,256]{2,1,0:T(8,128)(2,1)S(1)}, u32[]{:S(2)}, u32[]{:S(2)}) %collective-permute-start.7) | collective-permute-done | bytes 196640 | tf_op jit(solution)/shard_map/ppermute | solution.py:174
  159.3 5.6 %collective-permute-done.8.refs_3_ = bf16[2,192,256]{2,1,0:T(8,128)(2,1)S(1)} collective-permute-done((bf16[2,192,256]{2,1,0:T(8,128)(2,1)S(1)}, bf16[2,192,256]{2,1,0:T(8,128)(2,1)S(1)}, u32[]{:S(2)}, u32[]{:S(2)}) %collective-permute-start.8) | collective-permute-done | bytes 196640 | tf_op jit(solution)/shard_map/ppermute | solution.py:174
  164.9 0.1 pad_maximum_fusion.1
  165.0 2.3 %collective-permute-start.9 = (bf16[4,192,256]{2,1,0:T(8,128)(2,1)S(1)}, bf16[4,192,256]{2,1,0:T(8,128)(2,1)S(1)}, u32[]{:S(2)}, u32[]{:S(2)}) collective-permute-start(bf16[4,192,256]{2,1,0:T(8,128)(2,1)S(1)} %pad_maximum_fusion.1), channel_id=1, source_target_pairs={{0,1},{1,0},{2,3},{3,2},{4,5},{5,4},{6,7},{7,6},{8,9},{9,8},{10,11... | collective-permute-start | bytes 1179656 | tf_op jit(solution)/shard_map/ppermute | solution.py:178
  167.3 8.4 %collective-permute-done.9.refs_4_ = bf16[4,192,256]{2,1,0:T(8,128)(2,1)S(1)} collective-permute-done((bf16[4,192,256]{2,1,0:T(8,128)(2,1)S(1)}, bf16[4,192,256]{2,1,0:T(8,128)(2,1)S(1)}, u32[]{:S(2)}, u32[]{:S(2)}) %collective-permute-start.9) | collective-permute-done | bytes 393248 | tf_op jit(solution)/shard_map/ppermute | solution.py:178
  175.6 1.5 shard_map.107
  177.1 0.1 convert_reduce_fusion
  177.2 0.7 fusion.1
  (31 shorter events, 0.5 us)
Async XLA Ops:
  2.6 23.2 %all-to-all-start = ((bf16[8,32,256]{2,1,0:T(8,128)(2,1)}), bf16[8,32,256]{2,1,0:T(8,128)(2,1)S(1)}, u32[]{:S(2)}, u32[]{:S(2)}) async-start(bf16[8,32,256]{2,1,0:T(8,128)(2,1)} %bitcast.6), calls=%async_computation | async-start | bytes 262144 | tf_op jit(solution)/shard_map/all_to_all | solution.py:215
  71.1 21.5 %all-to-all-start.2 = ((bf16[4,192,384]{2,1,0:T(8,128)(2,1)}), bf16[4,192,384]{2,1,0:T(8,128)(2,1)S(1)}, u32[]{:S(2)}, u32[]{:S(2)}) async-start(bf16[4,192,384]{2,1,0:T(8,128)(2,1)} %broadcast_in_dim.17), calls=%async_computation.2 | async-start | bytes 1179648 | tf_op jit(solution)/shard_map/all_to_all | solution.py:169
  80.8 20.9 %copy-start.1 = (f32[1536]{0:T(1024)S(1)}, f32[1536]{0:T(1024)}, u32[]{:S(2)}) copy-start(f32[1536]{0:T(1024)} %param.10) | copy-start | bytes 18436
  82.0 17.4 %collective-permute-start = (bf16[192,256]{1,0:T(8,128)(2,1)S(1)}, bf16[192,256]{1,0:T(8,128)(2,1)S(1)}, u32[]{:S(2)}, u32[]{:S(2)}) collective-permute-start(bf16[192,256]{1,0:T(8,128)(2,1)S(1)} %get-tuple-element.15.refs_0_), channel_id=1, source_target_pairs={{0,2},{2,4},{4,6},{6,0},{1,3},{3,5},{5,7},{7,1},{8,10},{10,12},{12... | collective-permute-start | bytes 294920 | tf_op jit(solution)/shard_map/ppermute | solution.py:174
  85.1 14.3 %collective-permute-start.1 = (bf16[192,256]{1,0:T(8,128)(2,1)S(1)}, bf16[192,256]{1,0:T(8,128)(2,1)S(1)}, u32[]{:S(2)}, u32[]{:S(2)}) collective-permute-start(bf16[192,256]{1,0:T(8,128)(2,1)S(1)} %get-tuple-element.15.refs_0_), channel_id=1, source_target_pairs={{0,4},{2,6},{4,0},{6,2},{1,5},{3,7},{5,1},{7,3},{8,12},{10,14},{12... | collective-permute-start | bytes 294920 | tf_op jit(solution)/shard_map/ppermute | solution.py:174
  89.5 9.9 %collective-permute-start.2 = (bf16[192,256]{1,0:T(8,128)(2,1)S(1)}, bf16[192,256]{1,0:T(8,128)(2,1)S(1)}, u32[]{:S(2)}, u32[]{:S(2)}) collective-permute-start(bf16[192,256]{1,0:T(8,128)(2,1)S(1)} %get-tuple-element.15.refs_0_), channel_id=1, source_target_pairs={{0,6},{2,0},{4,2},{6,4},{1,7},{3,1},{5,3},{7,5},{8,14},{10,8},{12,... | collective-permute-start | bytes 294920 | tf_op jit(solution)/shard_map/ppermute | solution.py:174
  92.6 19.5 %collective-permute-start.4 = (bf16[4,192,384]{2,1,0:T(8,128)(2,1)S(1)}, bf16[4,192,384]{2,1,0:T(8,128)(2,1)S(1)}, u32[]{:S(2)}, u32[]{:S(2)}) collective-permute-start(bf16[4,192,384]{2,1,0:T(8,128)(2,1)S(1)} %all-to-all-done.2), channel_id=1, source_target_pairs={{0,8},{8,0},{1,9},{9,1},{2,10},{10,2},{3,11},{11,3},{4,12},{12,4},... | collective-permute-start | bytes 1769480 | tf_op jit(solution)/shard_map/ppermute | solution.py:178
  99.4 11.4 %collective-permute-start.3 = (bf16[4,192,256]{2,1,0:T(8,128)(2,1)S(1)}, bf16[4,192,256]{2,1,0:T(8,128)(2,1)S(1)}, u32[]{:S(2)}, u32[]{:S(2)}) collective-permute-start(bf16[4,192,256]{2,1,0:T(8,128)(2,1)S(1)} %pad_maximum_fusion), channel_id=1, source_target_pairs={{0,1},{1,0},{2,3},{3,2},{4,5},{5,4},{6,7},{7,6},{8,9},{9,8},{10,11... | collective-permute-start | bytes 1179656 | tf_op jit(solution)/shard_map/ppermute | solution.py:178
  110.8 1.3 copy-start
  115.2 5.6 %collective-permute-start.5 = (bf16[4,192,384]{2,1,0:T(8,128)(2,1)S(1)}, bf16[4,192,384]{2,1,0:T(8,128)(2,1)S(1)}, u32[]{:S(2)}, u32[]{:S(2)}) collective-permute-start(bf16[4,192,384]{2,1,0:T(8,128)(2,1)S(1)} %bitcast.62), channel_id=1, source_target_pairs={{0,8},{8,0},{1,9},{9,1},{2,10},{10,2},{3,11},{11,3},{4,12},{12,4},... | collective-permute-start | bytes 1769480 | tf_op jit(solution)/shard_map/ppermute | solution.py:178
  137.1 40.0 %all-to-all-start.4 = ((bf16[16,9,4,128]{3,2,1,0:T(4,128)(2,1)}), bf16[16,9,4,128]{3,2,1,0:T(4,128)(2,1)S(1)}, u32[]{:S(2)}, u32[]{:S(2)}) async-start(bf16[16,9,4,128]{3,2,1,0:T(4,128)(2,1)} %copy.35), calls=%async_computation.4 | async-start | bytes 294912 | tf_op jit(solution)/shard_map/all_to_all | solution.py:259
  148.3 7.9 %collective-permute-start.6 = (bf16[2,192,256]{2,1,0:T(8,128)(2,1)S(1)}, bf16[2,192,256]{2,1,0:T(8,128)(2,1)S(1)}, u32[]{:S(2)}, u32[]{:S(2)}) collective-permute-start(bf16[2,192,256]{2,1,0:T(8,128)(2,1)S(1)} %get-tuple-element.21), channel_id=1, source_target_pairs={{0,6},{2,0},{4,2},{6,4},{1,7},{3,1},{5,3},{7,5},{8,14},{10,8},{12,... | collective-permute-start | bytes 589832 | tf_op jit(solution)/shard_map/ppermute | solution.py:174
  151.1 8.2 %collective-permute-start.7 = (bf16[2,192,256]{2,1,0:T(8,128)(2,1)S(1)}, bf16[2,192,256]{2,1,0:T(8,128)(2,1)S(1)}, u32[]{:S(2)}, u32[]{:S(2)}) collective-permute-start(bf16[2,192,256]{2,1,0:T(8,128)(2,1)S(1)} %get-tuple-element.22), channel_id=1, source_target_pairs={{0,4},{2,6},{4,0},{6,2},{1,5},{3,7},{5,1},{7,3},{8,12},{10,14},{12... | collective-permute-start | bytes 589832 | tf_op jit(solution)/shard_map/ppermute | solution.py:174
  154.3 10.6 %collective-permute-start.8 = (bf16[2,192,256]{2,1,0:T(8,128)(2,1)S(1)}, bf16[2,192,256]{2,1,0:T(8,128)(2,1)S(1)}, u32[]{:S(2)}, u32[]{:S(2)}) collective-permute-start(bf16[2,192,256]{2,1,0:T(8,128)(2,1)S(1)} %get-tuple-element.23), channel_id=1, source_target_pairs={{0,2},{2,4},{4,6},{6,0},{1,3},{3,5},{5,7},{7,1},{8,10},{10,12},{12... | collective-permute-start | bytes 589832 | tf_op jit(solution)/shard_map/ppermute | solution.py:174
  165.0 10.7 %collective-permute-start.9 = (bf16[4,192,256]{2,1,0:T(8,128)(2,1)S(1)}, bf16[4,192,256]{2,1,0:T(8,128)(2,1)S(1)}, u32[]{:S(2)}, u32[]{:S(2)}) collective-permute-start(bf16[4,192,256]{2,1,0:T(8,128)(2,1)S(1)} %pad_maximum_fusion.1), channel_id=1, source_target_pairs={{0,1},{1,0},{2,3},{3,2},{4,5},{5,4},{6,7},{7,6},{8,9},{9,8},{10,11... | collective-permute-start | bytes 1179656 | tf_op jit(solution)/shard_map/ppermute | solution.py:178

commit v6 on v4

--- a/solution.py
+++ b/solution.py
@@ -26,14 +26,15 @@
     return lax.dot_general(a, b, (((0,), (0,)), ((), ())), preferred_element_type=f32)
 
 
-def call(kernel, outs, *args, limit=12):
+def call(kernel, outs, *args, limit=12, scratch=(), away=False):
     vmem = pl.BlockSpec(memory_space=pltpu.VMEM)
     smem = pl.BlockSpec(memory_space=pltpu.SMEM)
     return pl.pallas_call(
         kernel,
-        in_specs=[smem if a.shape == (2,) else vmem for a in args],
+        in_specs=[pl.BlockSpec(memory_space=pltpu.HBM) if away else smem if a.shape == (2,) else vmem for a in args],
         out_specs=[vmem] * len(outs),
         out_shape=[jax.ShapeDtypeStruct(s, d) for s, d in outs],
+        scratch_shapes=list(scratch),
         compiler_params=pltpu.CompilerParams(vmem_limit_bytes=limit << 20),
         interpret=INTERPRET,
     )(*args)
@@ -44,7 +45,13 @@
     return ((p // 12) % 2) * 96 + (((p // 24) % 4) * 2 + core) * 12 + p % 12
 
 
-def send_kernel(frames_ref, owner_ref, valid_ref, out_ref):
+def send_kernel(frames_hbm, owner_hbm, valid_hbm, out_ref, frames_ref, owner_ref, valid_ref, sems):
+    pairs = ((owner_hbm, owner_ref), (valid_hbm, valid_ref), (frames_hbm, frames_ref))
+    copies = [pltpu.make_async_copy(a, b, sems.at[i]) for i, (a, b) in enumerate(pairs)]
+    for copy in copies:
+        copy.start()
+    for copy in copies:
+        copy.wait()
     rows, width = frames_ref.shape
     slots, lanes = out_ref.shape
     owner = owner_ref[...]
@@ -168,6 +175,10 @@
     return lax.ppermute(x, axis, [(0, 1), (1, 0)])
 
 
+def stay(x):
+    return x if INTERPRET else pltpu.with_memory_space_constraint(x, pltpu.HBM)
+
+
 def tiles(x):
     return x.reshape(x.shape[0] // 4, 4, x.shape[1] // 128, 128).transpose(2, 0, 1, 3)
 
@@ -188,7 +199,16 @@
 
     shard = tiles(jnp.concatenate([value_weight, gate_weight], axis=1)).reshape(wt, 4, 128)
     (sent,) = call(
-        send_kernel, [((slots, lanes), bf16)], frames, frame_owner.reshape(1, rows), frame_valid.reshape(1, rows)
+        send_kernel,
+        [((slots, lanes), bf16)],
+        *map(stay, (frames, frame_owner.reshape(1, rows), frame_valid.reshape(1, rows))),
+        scratch=[
+            pltpu.VMEM((rows, width), bf16),
+            pltpu.VMEM((1, rows), i32),
+            pltpu.VMEM((1, rows), i32),
+            pltpu.SemaphoreType.DMA((3,)),
+        ],
+        away=True,
     )
     sent = sent.reshape(far, 4, 4, halves, 128).transpose(0, 3, 1, 2, 4).reshape(far, 4 * halves, 4, 128)
     sent = jnp.concatenate([jnp.broadcast_to(shard[None], (far,) + shard.shape), sent], axis=1)

time: 181 us -> 180 us (level)
  local copies, waits for them, and re-layouts: 7.05 us -> 4.63 us
    unnamed x19 -> x13, local copies, waits for them, and re-layouts: 2.57 us -> 0.13 us
where the time goes in v6:
time: 180 us; the launch traced here: 179 us
  blocking collectives  69 us (38%)
  starting transfers between devices  58.4 us (32%)
  waiting for transfers between devices  35.3 us (20%)
  Pallas kernels  9.37 us (5%)
  local copies, waits for them, and re-layouts  4.63 us (3%)
    all_to_all x1, blocking collectives, body(): got = lax.all_to_all(sent, 'zh', 0, 0, tiled=True)  56.6 us
    ppermute x6, starting transfers between devices, hop(): return lax.ppermute(x, 'x', [(i, (i + step) % n) for i in range(n)])  20.2 us
    ppermute x6, waiting for transfers between devices, hop(): return lax.ppermute(x, 'x', [(i, (i + step) % n) for i in range(n)])  13.2 us
    all_to_all x1, blocking collectives, body(): dw_y = lax.all_to_all(dw_c, NEAR, 0, 0, tiled=True)  12.4 us
    all_to_all x1, starting transfers between devices, body(): dw_z = lax.all_to_all(dw_y, 'zh', 0, 0, tiled=True)  12 us
    all_to_all x1, starting transfers between devices, spread(): lax.all_to_all(jnp.broadcast_to(x[None], (count,) + x.shape), axis, 0, 0,...  10.8 us
    ppermute x3, waiting for transfers between devices, swap(): return lax.ppermute(x, axis, [(0, 1), (1, 0)])  10.3 us
    pallas_call x6, Pallas kernels, call(): pl.pallas_call(kernel, in_specs=[pl.BlockSpec(memory_space=pltpu.HBM) if...  9.37 us
  transfers between devices with their start and end apart: 12, of which 8 were waited for; matrix products, arithmetic and copies ran while one was open for 1% of the time, Pallas kernels for 3%

profile of v6, /device:TPU:1, one launch (start us, length us, event | category | flops | bytes accessed | tf_op | source)
XLA Modules:
  0.0 178.5 jit_solution(8363067306491321390)
XLA Ops:
  0.7 1.3 shard_map.102
  2.0 0.1 copy.26
  2.1 0.1 pad_maximum_fusion.2
  2.3 0.2 pad_maximum_fusion.1
  2.5 56.6 %all_to_all.25 = bf16[16,17,4,128]{3,2,1,0:T(4,128)(2,1)S(1)} all-to-all(bf16[16,17,4,128]{3,2,1,0:T(4,128)(2,1)S(1)} %pad_maximum_fusion.1), channel_id=1, replica_groups=mesh['zh'=16,'zl'=2,'yh'=2,'co'=2,'x'=4,'yl'=2] {'zh'}, dimensions={0} | all-to-all | bytes 557056 | tf_op jit(solution)/shard_map/all_to_all | solution.py:215
  59.1 0.1 slice.33
  59.2 0.1 copy.33
  59.4 0.9 broadcast_in_dim.26
  60.2 10.8 %all-to-all-start.2 = ((bf16[4,192,384]{2,1,0:T(8,128)(2,1)}), bf16[4,192,384]{2,1,0:T(8,128)(2,1)S(1)}, u32[]{:S(2)}, u32[]{:S(2)}) async-start(bf16[4,192,384]{2,1,0:T(8,128)(2,1)} %broadcast_in_dim.26), calls=%async_computation.2 | async-start | bytes 1179648 | tf_op jit(solution)/shard_map/all_to_all | solution.py:166
  71.1 0.1 copy.37
  71.1 0.1 copy.29
  71.3 0.1 broadcast_in_dim.23
  71.4 6.9 %all-to-all-done.2 = bf16[4,192,384]{2,1,0:T(8,128)(2,1)S(1)} async-done(((bf16[4,192,384]{2,1,0:T(8,128)(2,1)}), bf16[4,192,384]{2,1,0:T(8,128)(2,1)S(1)}, u32[]{:S(2)}, u32[]{:S(2)}) %all-to-all-start.2) | async-done | bytes 589856 | tf_op jit(solution)/shard_map/all_to_all | solution.py:166
  78.3 0.7 broadcast_in_dim.24
  79.0 7.9 %all-to-all-start.1 = ((bf16[16,32,256]{2,1,0:T(8,128)(2,1)}), bf16[16,32,256]{2,1,0:T(8,128)(2,1)S(1)}, u32[]{:S(2)}, u32[]{:S(2)}) async-start(bf16[16,32,256]{2,1,0:T(8,128)(2,1)} %bitcast.10), calls=%async_computation.1 | async-start | bytes 524288 | tf_op jit(solution)/shard_map/all_to_all | solution.py:218
  86.9 2.1 %collective-permute-start.3 = (bf16[4,192,384]{2,1,0:T(8,128)(2,1)S(1)}, bf16[4,192,384]{2,1,0:T(8,128)(2,1)S(1)}, u32[]{:S(2)}, u32[]{:S(2)}) collective-permute-start(bf16[4,192,384]{2,1,0:T(8,128)(2,1)S(1)} %all-to-all-done.2), channel_id=1, source_target_pairs={{0,8},{8,0},{1,9},{9,1},{2,10},{10,2},{3,11},{11,3},{4,12},{12,4},... | collective-permute-start | bytes 1769480 | tf_op jit(solution)/shard_map/ppermute | solution.py:175
  89.0 0.1 reshape.87
  89.2 0.2 rev.3
  89.3 0.1 pad_add_fusion.own_ref
  89.4 4.9 %all-to-all-done.1 = bf16[16,32,256]{2,1,0:T(8,128)(2,1)S(1)} async-done(((bf16[16,32,256]{2,1,0:T(8,128)(2,1)}), bf16[16,32,256]{2,1,0:T(8,128)(2,1)S(1)}, u32[]{:S(2)}, u32[]{:S(2)}) %all-to-all-start.1) | async-done | bytes 262176 | tf_op jit(solution)/shard_map/all_to_all | solution.py:218
  94.3 1.1 shard_map.103
  95.5 3.1 %collective-permute-start = (bf16[2,192,256]{2,1,0:T(8,128)(2,1)S(1)}, bf16[2,192,256]{2,1,0:T(8,128)(2,1)S(1)}, u32[]{:S(2)}, u32[]{:S(2)}) collective-permute-start(bf16[2,192,256]{2,1,0:T(8,128)(2,1)S(1)} %get-tuple-element.15.refs_0_), channel_id=1, source_target_pairs={{0,2},{2,4},{4,6},{6,0},{1,3},{3,5},{5,7},{7,1},{8,10},{10,12},{12... | collective-permute-start | bytes 589832 | tf_op jit(solution)/shard_map/ppermute | solution.py:171
  98.6 4.4 %collective-permute-start.1 = (bf16[2,192,256]{2,1,0:T(8,128)(2,1)S(1)}, bf16[2,192,256]{2,1,0:T(8,128)(2,1)S(1)}, u32[]{:S(2)}, u32[]{:S(2)}) collective-permute-start(bf16[2,192,256]{2,1,0:T(8,128)(2,1)S(1)} %get-tuple-element.15.refs_0_), channel_id=1, source_target_pairs={{0,4},{2,6},{4,0},{6,2},{1,5},{3,7},{5,1},{7,3},{8,12},{10,14},{12... | collective-permute-start | bytes 589832 | tf_op jit(solution)/shard_map/ppermute | solution.py:171
  103.0 3.0 %collective-permute-start.2 = (bf16[2,192,256]{2,1,0:T(8,128)(2,1)S(1)}, bf16[2,192,256]{2,1,0:T(8,128)(2,1)S(1)}, u32[]{:S(2)}, u32[]{:S(2)}) collective-permute-start(bf16[2,192,256]{2,1,0:T(8,128)(2,1)S(1)} %get-tuple-element.15.refs_0_), channel_id=1, source_target_pairs={{0,6},{2,0},{4,2},{6,4},{1,7},{3,1},{5,3},{7,5},{8,14},{10,8},{12,... | collective-permute-start | bytes 589832 | tf_op jit(solution)/shard_map/ppermute | solution.py:171
  106.1 0.3 reshape.100.gain_ref
  106.5 3.2 %collective-permute-done.1.refs_2_ = bf16[2,192,256]{2,1,0:T(8,128)(2,1)S(1)} collective-permute-done((bf16[2,192,256]{2,1,0:T(8,128)(2,1)S(1)}, bf16[2,192,256]{2,1,0:T(8,128)(2,1)S(1)}, u32[]{:S(2)}, u32[]{:S(2)}) %collective-permute-start.1) | collective-permute-done | bytes 196640 | tf_op jit(solution)/shard_map/ppermute | solution.py:171
  109.7 1.4 collective-permute-done.2.refs_3_
  111.1 1.2 shard_map.104.normed_ref
  112.3 3.1 %shard_map.105 = (bf16[2,192,128]{2,1,0:T(8,128)(2,1)}, bf16[4,8,24,384]{3,2,1,0:T(8,128)(2,1)S(1)}, bf16[4,8,24,384]{3,2,1,0:T(8,128)(2,1)S(1)}, bf16[384,256]{1,0:T(8,128)(2,1)S(1)}) custom-call(s32[2]{0:T(128)S(1)} %pad_add_fusion.own_ref, bf16[8,192,256]{2,1,0:T(8,128)(2,1)S(1)} %shard_map.104.normed_ref, f32[8,256]{1,0:T(8,128)S(1)} %get-tuple-element.14.live_ref, ...), custom_call_target="tpu_custom_call" | custom-call | tf_op jit(solution)/shard_map/pallas_call | solution.py:32
  115.4 3.4 %collective-permute-start.4 = (bf16[4,192,384]{2,1,0:T(8,128)(2,1)S(1)}, bf16[4,192,384]{2,1,0:T(8,128)(2,1)S(1)}, u32[]{:S(2)}, u32[]{:S(2)}) collective-permute-start(bf16[4,192,384]{2,1,0:T(8,128)(2,1)S(1)} %bitcast.51), channel_id=1, source_target_pairs={{0,8},{8,0},{1,9},{9,1},{2,10},{10,2},{3,11},{11,3},{4,12},{12,4},... | collective-permute-start | bytes 1769480 | tf_op jit(solution)/shard_map/ppermute | solution.py:175
  118.9 1.6 collective-permute-done.4
  120.5 0.2 fusion
  120.7 12.4 %all_to_all.26 = bf16[4,192,384]{2,1,0:T(8,128)(2,1)S(1)} all-to-all(bf16[4,192,384]{2,1,0:T(8,128)(2,1)S(1)} %fusion), channel_id=1, replica_groups=mesh['zh'=16,'zl'=2,'yh'=2,'co'=2,'x'=4,'yl'=2] {'zl','yh'}, dimensions={0} | all-to-all | bytes 1179648 | tf_op jit(solution)/shard_map/all_to_all | solution.py:252
  133.1 0.1 reduce_sum.21
  133.3 0.7 copy.35
  134.0 12.0 %all-to-all-start.4 = ((bf16[16,9,4,128]{3,2,1,0:T(4,128)(2,1)}), bf16[16,9,4,128]{3,2,1,0:T(4,128)(2,1)S(1)}, u32[]{:S(2)}, u32[]{:S(2)}) async-start(bf16[16,9,4,128]{3,2,1,0:T(4,128)(2,1)} %copy.35), calls=%async_computation.4 | async-start | bytes 294912 | tf_op jit(solution)/shard_map/all_to_all | solution.py:255
  146.0 1.1 shard_map.106
  147.1 4.3 %collective-permute-start.5 = (bf16[2,192,256]{2,1,0:T(8,128)(2,1)S(1)}, bf16[2,192,256]{2,1,0:T(8,128)(2,1)S(1)}, u32[]{:S(2)}, u32[]{:S(2)}) collective-permute-start(bf16[2,192,256]{2,1,0:T(8,128)(2,1)S(1)} %get-tuple-element.21), channel_id=1, source_target_pairs={{0,6},{2,0},{4,2},{6,4},{1,7},{3,1},{5,3},{7,5},{8,14},{10,8},{12,... | collective-permute-start | bytes 589832 | tf_op jit(solution)/shard_map/ppermute | solution.py:171
  151.4 3.4 %collective-permute-start.6 = (bf16[2,192,256]{2,1,0:T(8,128)(2,1)S(1)}, bf16[2,192,256]{2,1,0:T(8,128)(2,1)S(1)}, u32[]{:S(2)}, u32[]{:S(2)}) collective-permute-start(bf16[2,192,256]{2,1,0:T(8,128)(2,1)S(1)} %get-tuple-element.22), channel_id=1, source_target_pairs={{0,4},{2,6},{4,0},{6,2},{1,5},{3,7},{5,1},{7,3},{8,12},{10,14},{12... | collective-permute-start | bytes 589832 | tf_op jit(solution)/shard_map/ppermute | solution.py:171
  154.8 1.9 %collective-permute-start.7 = (bf16[2,192,256]{2,1,0:T(8,128)(2,1)S(1)}, bf16[2,192,256]{2,1,0:T(8,128)(2,1)S(1)}, u32[]{:S(2)}, u32[]{:S(2)}) collective-permute-start(bf16[2,192,256]{2,1,0:T(8,128)(2,1)S(1)} %get-tuple-element.23), channel_id=1, source_target_pairs={{0,2},{2,4},{4,6},{6,0},{1,3},{3,5},{5,7},{7,1},{8,10},{10,12},{12... | collective-permute-start | bytes 589832 | tf_op jit(solution)/shard_map/ppermute | solution.py:171
  156.8 2.8 %collective-permute-done.6.refs_2_ = bf16[2,192,256]{2,1,0:T(8,128)(2,1)S(1)} collective-permute-done((bf16[2,192,256]{2,1,0:T(8,128)(2,1)S(1)}, bf16[2,192,256]{2,1,0:T(8,128)(2,1)S(1)}, u32[]{:S(2)}, u32[]{:S(2)}) %collective-permute-start.6) | collective-permute-done | bytes 196640 | tf_op jit(solution)/shard_map/ppermute | solution.py:171
  159.6 5.8 %collective-permute-done.7.refs_3_ = bf16[2,192,256]{2,1,0:T(8,128)(2,1)S(1)} collective-permute-done((bf16[2,192,256]{2,1,0:T(8,128)(2,1)S(1)}, bf16[2,192,256]{2,1,0:T(8,128)(2,1)S(1)}, u32[]{:S(2)}, u32[]{:S(2)}) %collective-permute-start.7) | collective-permute-done | bytes 196640 | tf_op jit(solution)/shard_map/ppermute | solution.py:171
  165.4 0.1 pad_maximum_fusion
  165.5 2.0 %collective-permute-start.8 = (bf16[4,192,256]{2,1,0:T(8,128)(2,1)S(1)}, bf16[4,192,256]{2,1,0:T(8,128)(2,1)S(1)}, u32[]{:S(2)}, u32[]{:S(2)}) collective-permute-start(bf16[4,192,256]{2,1,0:T(8,128)(2,1)S(1)} %pad_maximum_fusion), channel_id=1, source_target_pairs={{0,1},{1,0},{2,3},{3,2},{4,5},{5,4},{6,7},{7,6},{8,9},{9,8},{10,11... | collective-permute-start | bytes 1179656 | tf_op jit(solution)/shard_map/ppermute | solution.py:175
  167.5 8.7 %collective-permute-done.8.refs_4_ = bf16[4,192,256]{2,1,0:T(8,128)(2,1)S(1)} collective-permute-done((bf16[4,192,256]{2,1,0:T(8,128)(2,1)S(1)}, bf16[4,192,256]{2,1,0:T(8,128)(2,1)S(1)}, u32[]{:S(2)}, u32[]{:S(2)}) %collective-permute-start.8) | collective-permute-done | bytes 393248 | tf_op jit(solution)/shard_map/ppermute | solution.py:175
  176.2 1.5 shard_map.107
  177.7 0.1 convert_reduce_fusion
  177.8 0.7 fusion.1
  (33 shorter events, 0.5 us)
Async XLA Ops:
  0.6 1.5 copy-start.2
  0.6 1.5 copy-start.1
  60.2 18.1 %all-to-all-start.2 = ((bf16[4,192,384]{2,1,0:T(8,128)(2,1)}), bf16[4,192,384]{2,1,0:T(8,128)(2,1)S(1)}, u32[]{:S(2)}, u32[]{:S(2)}) async-start(bf16[4,192,384]{2,1,0:T(8,128)(2,1)} %broadcast_in_dim.26), calls=%async_computation.2 | async-start | bytes 1179648 | tf_op jit(solution)/shard_map/all_to_all | solution.py:166
  71.1 17.9 %copy-start.3 = (f32[1536]{0:T(1024)S(1)}, f32[1536]{0:T(1024)}, u32[]{:S(2)}) copy-start(f32[1536]{0:T(1024)} %param.10) | copy-start | bytes 18436
  79.0 15.3 %all-to-all-start.1 = ((bf16[16,32,256]{2,1,0:T(8,128)(2,1)}), bf16[16,32,256]{2,1,0:T(8,128)(2,1)S(1)}, u32[]{:S(2)}, u32[]{:S(2)}) async-start(bf16[16,32,256]{2,1,0:T(8,128)(2,1)} %bitcast.10), calls=%async_computation.1 | async-start | bytes 524288 | tf_op jit(solution)/shard_map/all_to_all | solution.py:218
  86.9 25.5 %collective-permute-start.3 = (bf16[4,192,384]{2,1,0:T(8,128)(2,1)S(1)}, bf16[4,192,384]{2,1,0:T(8,128)(2,1)S(1)}, u32[]{:S(2)}, u32[]{:S(2)}) collective-permute-start(bf16[4,192,384]{2,1,0:T(8,128)(2,1)S(1)} %all-to-all-done.2), channel_id=1, source_target_pairs={{0,8},{8,0},{1,9},{9,1},{2,10},{10,2},{3,11},{11,3},{4,12},{12,4},... | collective-permute-start | bytes 1769480 | tf_op jit(solution)/shard_map/ppermute | solution.py:175
  95.5 11.0 %collective-permute-start = (bf16[2,192,256]{2,1,0:T(8,128)(2,1)S(1)}, bf16[2,192,256]{2,1,0:T(8,128)(2,1)S(1)}, u32[]{:S(2)}, u32[]{:S(2)}) collective-permute-start(bf16[2,192,256]{2,1,0:T(8,128)(2,1)S(1)} %get-tuple-element.15.refs_0_), channel_id=1, source_target_pairs={{0,2},{2,4},{4,6},{6,0},{1,3},{3,5},{5,7},{7,1},{8,10},{10,12},{12... | collective-permute-start | bytes 589832 | tf_op jit(solution)/shard_map/ppermute | solution.py:171
  98.6 11.1 %collective-permute-start.1 = (bf16[2,192,256]{2,1,0:T(8,128)(2,1)S(1)}, bf16[2,192,256]{2,1,0:T(8,128)(2,1)S(1)}, u32[]{:S(2)}, u32[]{:S(2)}) collective-permute-start(bf16[2,192,256]{2,1,0:T(8,128)(2,1)S(1)} %get-tuple-element.15.refs_0_), channel_id=1, source_target_pairs={{0,4},{2,6},{4,0},{6,2},{1,5},{3,7},{5,1},{7,3},{8,12},{10,14},{12... | collective-permute-start | bytes 589832 | tf_op jit(solution)/shard_map/ppermute | solution.py:171
  103.0 8.1 %collective-permute-start.2 = (bf16[2,192,256]{2,1,0:T(8,128)(2,1)S(1)}, bf16[2,192,256]{2,1,0:T(8,128)(2,1)S(1)}, u32[]{:S(2)}, u32[]{:S(2)}) collective-permute-start(bf16[2,192,256]{2,1,0:T(8,128)(2,1)S(1)} %get-tuple-element.15.refs_0_), channel_id=1, source_target_pairs={{0,6},{2,0},{4,2},{6,4},{1,7},{3,1},{5,3},{7,5},{8,14},{10,8},{12,... | collective-permute-start | bytes 589832 | tf_op jit(solution)/shard_map/ppermute | solution.py:171
  111.1 1.3 copy-start
  115.4 5.0 %collective-permute-start.4 = (bf16[4,192,384]{2,1,0:T(8,128)(2,1)S(1)}, bf16[4,192,384]{2,1,0:T(8,128)(2,1)S(1)}, u32[]{:S(2)}, u32[]{:S(2)}) collective-permute-start(bf16[4,192,384]{2,1,0:T(8,128)(2,1)S(1)} %bitcast.51), channel_id=1, source_target_pairs={{0,8},{8,0},{1,9},{9,1},{2,10},{10,2},{3,11},{11,3},{4,12},{12,4},... | collective-permute-start | bytes 1769480 | tf_op jit(solution)/shard_map/ppermute | solution.py:175
  134.0 43.7 %all-to-all-start.4 = ((bf16[16,9,4,128]{3,2,1,0:T(4,128)(2,1)}), bf16[16,9,4,128]{3,2,1,0:T(4,128)(2,1)S(1)}, u32[]{:S(2)}, u32[]{:S(2)}) async-start(bf16[16,9,4,128]{3,2,1,0:T(4,128)(2,1)} %copy.35), calls=%async_computation.4 | async-start | bytes 294912 | tf_op jit(solution)/shard_map/all_to_all | solution.py:255
  147.1 9.7 %collective-permute-start.5 = (bf16[2,192,256]{2,1,0:T(8,128)(2,1)S(1)}, bf16[2,192,256]{2,1,0:T(8,128)(2,1)S(1)}, u32[]{:S(2)}, u32[]{:S(2)}) collective-permute-start(bf16[2,192,256]{2,1,0:T(8,128)(2,1)S(1)} %get-tuple-element.21), channel_id=1, source_target_pairs={{0,6},{2,0},{4,2},{6,4},{1,7},{3,1},{5,3},{7,5},{8,14},{10,8},{12,... | collective-permute-start | bytes 589832 | tf_op jit(solution)/shard_map/ppermute | solution.py:171
  151.4 8.2 %collective-permute-start.6 = (bf16[2,192,256]{2,1,0:T(8,128)(2,1)S(1)}, bf16[2,192,256]{2,1,0:T(8,128)(2,1)S(1)}, u32[]{:S(2)}, u32[]{:S(2)}) collective-permute-start(bf16[2,192,256]{2,1,0:T(8,128)(2,1)S(1)} %get-tuple-element.22), channel_id=1, source_target_pairs={{0,4},{2,6},{4,0},{6,2},{1,5},{3,7},{5,1},{7,3},{8,12},{10,14},{12... | collective-permute-start | bytes 589832 | tf_op jit(solution)/shard_map/ppermute | solution.py:171
  154.8 10.6 %collective-permute-start.7 = (bf16[2,192,256]{2,1,0:T(8,128)(2,1)S(1)}, bf16[2,192,256]{2,1,0:T(8,128)(2,1)S(1)}, u32[]{:S(2)}, u32[]{:S(2)}) collective-permute-start(bf16[2,192,256]{2,1,0:T(8,128)(2,1)S(1)} %get-tuple-element.23), channel_id=1, source_target_pairs={{0,2},{2,4},{4,6},{6,0},{1,3},{3,5},{5,7},{7,1},{8,10},{10,12},{12... | collective-permute-start | bytes 589832 | tf_op jit(solution)/shard_map/ppermute | solution.py:171
  165.5 10.7 %collective-permute-start.8 = (bf16[4,192,256]{2,1,0:T(8,128)(2,1)S(1)}, bf16[4,192,256]{2,1,0:T(8,128)(2,1)S(1)}, u32[]{:S(2)}, u32[]{:S(2)}) collective-permute-start(bf16[4,192,256]{2,1,0:T(8,128)(2,1)S(1)} %pad_maximum_fusion), channel_id=1, source_target_pairs={{0,1},{1,0},{2,3},{3,2},{4,5},{5,4},{6,7},{7,6},{8,9},{9,8},{10,11... | collective-permute-start | bytes 1179656 | tf_op jit(solution)/shard_map/ppermute | solution.py:175

commit v7 on v5

v7 whole, which is shorter than its diff:
```python
import jax
import jax.numpy as jnp
from jax import lax
from jax.experimental import pallas as pl
from jax.experimental.pallas import tpu as pltpu
from jax.sharding import Mesh, PartitionSpec as P


epsilon = 1e-05
bf16, f32, i32 = jnp.bfloat16, jnp.float32, jnp.int32
NEAR = ("zl", "yh")
DP = ("zh", "zl", "yh", "co")
MP = ("x", "yl")
INTERPRET = False


def nt(a, b):
    return lax.dot_general(a, b, (((1,), (1,)), ((), ())), preferred_element_type=f32)


def nn(a, b):
    return lax.dot_general(a, b, (((1,), (0,)), ((), ())), preferred_element_type=f32)


def tn(a, b):
    return lax.dot_general(a, b, (((0,), (0,)), ((), ())), preferred_element_type=f32)


def call(kernel, outs, *args, limit=12, scratch=(), away=False):
    vmem = pl.BlockSpec(memory_space=pltpu.VMEM)
    smem = pl.BlockSpec(memory_space=pltpu.SMEM)
    return pl.pallas_call(
        kernel,
        in_specs=[pl.BlockSpec(memory_space=pltpu.HBM) if away else smem if a.shape == (2,) else vmem for a in args],
        out_specs=[vmem] * len(outs),
        out_shape=[jax.ShapeDtypeStruct(s, d) for s, d in outs],
        scratch_shapes=list(scratch),
        compiler_params=pltpu.CompilerParams(vmem_limit_bytes=limit << 20),
        interpret=INTERPRET,
    )(*args)


def row_order(p):
    return (p % 16) * 12 + (p // 48) * 3 + (p // 16) % 3


def owner_order(p, co):
    core = (p // 96 + co) % 2
    return ((p // 12) % 2) * 96 + (((p // 24) % 4) * 2 + core) * 12 + p % 12


def send_kernel(frames_hbm, owner_hbm, valid_hbm, vw_hbm, gw_hbm, out_ref, frames_ref, owner_ref, valid_ref, vw_ref, gw_ref, sems):
    pairs = ((owner_hbm, owner_ref), (valid_hbm, valid_ref), (frames_hbm, frames_ref), (vw_hbm, vw_ref), (gw_hbm, gw_ref))
    copies = [pltpu.make_async_copy(a, b, sems.at[i]) for i, (a, b) in enumerate(pairs)]
    for copy in copies:
        copy.start()
    for copy in copies:
        copy.wait()
    rows, _ = frames_ref.shape
    peers = out_ref.shape[1]
    owner = owner_ref[...]
    down = jnp.transpose(jnp.broadcast_to(owner, (rows, rows)))
    earlier = lax.broadcasted_iota(i32, (rows, rows), 0) < lax.broadcasted_iota(i32, (rows, rows), 1)
    slot = jnp.sum(jnp.where((down == owner) & earlier, 1.0, 0.0), axis=0, keepdims=True).astype(i32)
    hit = lax.broadcasted_iota(i32, (2 * peers, rows), 0) == slot * peers + owner
    placed = nn(jnp.where(hit, 1.0, 0.0).astype(bf16), frames_ref[...])
    live = jnp.sum(jnp.where(hit & (valid_ref[...] > 0), 1.0, 0.0), axis=1, keepdims=True)
    first, second = placed[:peers], placed[peers:]
    out_ref[0] = first[:, :128].astype(bf16)
    out_ref[1] = second[:, :128].astype(bf16)
    out_ref[2] = jnp.concatenate([first[:, 128:], second[:, 128:]], axis=1).astype(bf16)
    shard = jnp.concatenate([vw_ref[...].astype(f32), gw_ref[...].astype(f32)], axis=1)

    def lines(units):
        picked = [shard[3 * q + u // 3 : 3 * q + u // 3 + 1, 128 * (u % 3) : 128 * (u % 3) + 128] for q, u in units]
        return jnp.concatenate([jnp.concatenate(picked, axis=0)] * (peers // 8), axis=0)

    for k in range(4):
        out_ref[3 + k] = lines([(n // 2, 4 * (n % 2) + k) for n in range(8)]).astype(bf16)
    last = lines([(n // 2, 8) for n in range(8)])
    core = lax.broadcasted_iota(i32, (peers, 128), 0) % 2
    lane = lax.broadcasted_iota(i32, (peers, 128), 1)
    flag = lane - 64 * (1 - core)
    flags = jnp.where(flag == 0, live[:peers], 0.0) + jnp.where(flag == 1, live[peers:], 0.0)
    out_ref[7] = jnp.where(lane // 64 == core, last, flags).astype(bf16)


def turn_kernel(own_ref, rows_ref, out_ref, live_ref):
    width, slots = out_ref.shape
    peers = slots // 2
    channel = row_order(lax.broadcasted_iota(i32, (width, 128), 0))
    lane = lax.broadcasted_iota(i32, (width, 128), 1)
    low = (lane == channel).astype(bf16)
    at = lax.broadcasted_iota(i32, (16, 128), 1)
    for c in range(2):
        high = (lane == channel - 128 + 64 * c).astype(bf16)
        high = jnp.where((channel >= 128), high.astype(f32), 0.0).astype(bf16)
        turned = nt(low, rows_ref[c]) + nt(high, rows_ref[2])
        out_ref[:, c * peers : (c + 1) * peers] = turned.astype(bf16)
        flag = (at == 64 * (1 - own_ref[1]) + c).astype(bf16)
        live_ref[:, c * peers : (c + 1) * peers] = nt(flag, rows_ref[7])[:8]


def block_of(own_ref, k, blocks):
    n = blocks // 2
    x, y = own_ref[0] // 2, own_ref[0] % 2
    return ((x + n - k % n) % n) * 2 + (y + k // n) % 2


def norm_kernel(own_ref, live_ref, gain_ref, *refs):
    near_refs, across_ref, normed_ref = refs[:-2], refs[-2], refs[-1]
    blocks, width, slots = normed_ref.shape
    total = blocks * width
    live = live_ref[0:1, :]

    def block(k):
        n = blocks // 2
        return (near_refs[k][...] if k < n else across_ref[k - n]).astype(f32)

    s = jnp.zeros((1, slots), f32)
    for k in range(blocks):
        s = s + jnp.sum(block(k), axis=0, keepdims=True)
    mean = s * (1.0 / total)
    s = jnp.zeros((1, slots), f32)
    for k in range(blocks):
        c = block(k) - mean
        s = s + jnp.sum(c * c, axis=0, keepdims=True)
    inv = lax.rsqrt(s * (1.0 / total) + epsilon)
    for k in range(blocks):
        c = block(k) - mean
        normed_ref[k] = (c * inv * gain_ref[block_of(own_ref, k, blocks)] * live).astype(bf16)


def forward_kernel(own_ref, normed_ref, live_ref, wa_ref, wb_ref, up_ref, gated_ref, da_ref, db_ref, delta_ref, w_ref):
    blocks, width, slots = normed_ref.shape
    peers = slots // 2
    live = live_ref[0:1, :]
    first = own_ref[1] == 0
    lane = lax.broadcasted_iota(i32, (16, 128), 1)

    def unit(q, u, m):
        at = pl.ds(pl.multiple_of(16 * m, 16), 16)
        a, b = wa_ref[q, u % 4 if u < 8 else 4, at, :], wb_ref[q, u % 4 if u < 8 else 4, at, :]
        if u < 4:
            return jnp.where(first, a, b)
        if u < 8:
            return jnp.where(first, b, a)
        low, high = jnp.where(first, a, b).astype(f32), jnp.where(first, b, a).astype(f32)
        return jnp.where(lane < 64, low, high).astype(bf16)

    acc = jnp.zeros((2 * width, slots), f32)
    for k in range(blocks):
        m = block_of(own_ref, k, blocks)
        for q in range(4):
            for r in range(3):
                row = 48 * q + 16 * r
                w_ref[k, row : row + 16, :] = jnp.concatenate([unit(q, 3 * r + i, m) for i in range(3)], axis=1)
        acc = acc + tn(w_ref[k], normed_ref[k])
    value, gate = acc[:width], acc[width:]
    sig = jax.nn.sigmoid(gate)
    up = jnp.concatenate([up_ref[0], up_ref[1]], axis=1).astype(f32)
    gated = (value * sig).astype(bf16)
    gated_ref[0] = gated[:, :peers]
    gated_ref[1] = gated[:, peers:]
    value_delta = (up * sig * live).astype(bf16)
    gate_delta = (up * value * sig * (1.0 - sig) * live).astype(bf16)
    delta = jnp.concatenate([value_delta, gate_delta], axis=0)
    delta_ref[...] = delta
    target = owner_order(lax.broadcasted_iota(i32, (width, width), 0), own_ref[1])
    move = (target == row_order(lax.broadcasted_iota(i32, (width, width), 1))).astype(bf16)
    for k in range(blocks):
        dw = nt(nn(move, normed_ref[k]).astype(bf16), delta)
        m = block_of(own_ref, k, blocks)
        for j in range(4):
            da_ref[j, m] = dw[24 * j : 24 * j + 24].astype(bf16)
            db_ref[j, m] = dw[24 * j + 96 : 24 * j + 120].astype(bf16)


def backward_kernel(w_ref, delta_ref, *partial_refs):
    blocks = 2 * len(partial_refs)
    for k in range(blocks):
        n = blocks // 2
        partial_refs[k % n][k // n] = nn(w_ref[k], delta_ref[...]).astype(bf16)


def join_kernel(*refs):
    across_ref, out_ref = refs[-2:]
    width, slots = across_ref.shape[1:]
    peers = slots // 2
    s = jnp.zeros((width, slots), f32)
    for k, ref in enumerate(refs[:-2]):
        s = s + ref[0].astype(f32) + across_ref[k].astype(f32)
    place = lax.broadcasted_iota(i32, (width, width), 1)
    natural = lax.broadcasted_iota(i32, (width, width), 0)
    back = (row_order(place) == natural).astype(bf16)
    out = nn(back, s.astype(bf16)).astype(bf16)
    out_ref[0] = out[:, :peers]
    out_ref[1] = out[:, peers:]


def spread(x, axis, count):
    return lax.all_to_all(jnp.broadcast_to(x[None], (count,) + x.shape), axis, 0, 0, tiled=True)


def hop(x, step):
    n = lax.axis_size("x")
    return lax.ppermute(x, "x", [(i, (i + step) % n) for i in range(n)])


def swap(x, axis):
    return lax.ppermute(x, axis, [(0, 1), (1, 0)])


def stay(x):
    return x if INTERPRET else pltpu.with_memory_space_constraint(x, pltpu.HBM)


def body(frames, frame_owner, frame_valid, norm_gain, value_weight, gate_weight, grad_owned):
    far = lax.axis_size("zh")
    blocks = lax.axis_size(MP)
    peers = 8 * far
    slots = 2 * peers
    rows, width = frames.shape
    group = value_weight.shape[0]
    columns = 2 * width
    wt = columns // 128 * group // 4
    core = lax.axis_index("co").astype(i32)
    own = jnp.stack([lax.axis_index(MP).astype(i32), core])

    (sent,) = call(
        send_kernel,
        [((8, peers, 128), bf16)],
        *map(stay, (frames, frame_owner.reshape(1, rows), frame_valid.reshape(1, rows), value_weight, gate_weight)),
        scratch=[
            pltpu.VMEM((rows, width), bf16),
            pltpu.VMEM((1, rows), i32),
            pltpu.VMEM((1, rows), i32),
            pltpu.VMEM((group, width), bf16),
            pltpu.VMEM((group, width), bf16),
            pltpu.SemaphoreType.DMA((5,)),
        ],
        away=True,
    )
    got = lax.all_to_all(sent.transpose(1, 0, 2), DP, 0, 0, tiled=True)
    got = got.transpose(1, 0, 2)
    w_own = spread(got[3:], NEAR, 4)
    w_other = swap(w_own, "co")
    turned, live = call(turn_kernel, [((width, slots), bf16), ((8, slots), f32)], own, got)
    whole = [turned] + [hop(turned, dx) for dx in range(1, blocks // 2)]
    stacked = jnp.stack(whole)
    whole.append(swap(stacked, "yl"))
    gain = norm_gain.reshape(blocks, 16, 4, 3).transpose(0, 2, 3, 1).reshape(blocks, width, 1)
    (normed,) = call(norm_kernel, [((blocks, width, slots), bf16)], own, live, gain, *whole)
    up = grad_owned.reshape(peers, 2, width).transpose(1, 2, 0)
    near = (4, blocks, 2 * group, columns)
    gated, dw_own, dw_other, delta, w_all = call(
        forward_kernel,
        [((2, width, peers), bf16), (near, bf16), (near, bf16), ((columns, slots), bf16), ((blocks, width, columns), bf16)],
        own,
        normed,
        live,
        w_own,
        w_other,
        up,
    )
    dw_c = swap(dw_other.reshape(4, far * group, columns), "co")
    partial = call(backward_kernel, [((2, width, slots), bf16)] * (blocks // 2), w_all, delta)
    dw_c = (dw_c.astype(f32) + dw_own.reshape(4, far * group, columns).astype(f32)).astype(bf16)
    dw_y = lax.all_to_all(dw_c, NEAR, 0, 0, tiled=True)
    dw_y = jnp.sum(dw_y.astype(f32), axis=0).astype(bf16)
    dw_y = dw_y.reshape(far, group, columns // 128, 128).transpose(0, 2, 1, 3).reshape(far, wt, 4, 128)
    dw_z = lax.all_to_all(dw_y, "zh", 0, 0, tiled=True)
    parts = [partial[0]] + [hop(partial[dx], -dx) for dx in range(1, blocks // 2)]
    other = []
    for part in parts:
        other.append(part[1:])
    across = swap(jnp.concatenate(other), "yl")
    (normed_grad,) = call(join_kernel, [((2, width, peers), bf16)], *parts, across)
    scale = float(rows * peers) ** (-0.5)
    grads = jnp.sum(dw_z.astype(f32), axis=0) * scale
    grads = grads.reshape(columns // 128, group, 128).transpose(1, 0, 2).reshape(group, columns)

    def restore(x):
        return x.transpose(2, 0, 1).reshape(1, peers, 2, width)

    return (restore(gated), grads[:, :width], grads[:, width:], restore(normed_grad))


def solution(mesh):
    mp = mesh.shape["mp"]
    far = mesh.shape["dp"] // 8
    fine = Mesh(mesh.devices.reshape(far, 2, 2, 2, mp // 2, 2), DP + MP)
    slots = P(DP, None, None, MP)
    weights = P(DP, MP)
    return jax.shard_map(
        body,
        mesh=fine,
        in_specs=(P(DP, MP), P(DP, None), P(DP), P(), weights, weights, slots),
        out_specs=(slots, weights, weights, slots),
        check_vma=False,
    )
```

time: 179 us -> 183 us (1.022)
  starting transfers between devices: 70.8 us -> 39.6 us
  blocking collectives: 58.9 us -> 84.9 us
  waiting for transfers between devices: 32 us -> 41.5 us
    all_to_all x1, blocking collectives: 43.7 us -> 72.6 us  [body(): got = lax.all_to_all(sent.transpose(1, 0, 2), DP, 0, 0, tiled=True)]
    all_to_all x1 -> x0, starting transfers between devices: 17.4 us -> none  [body(): lax.all_to_all(sent.reshape(8, 2 * far, lanes), ('zl', 'yh', 'co'), 0, 0,...]
    all_to_all x1, waiting for transfers between devices: 0.01 us -> 11.3 us  [spread(): lax.all_to_all(jnp.broadcast_to(x[None], (count,) + x.shape), axis, 0, 0,...]
    all_to_all x1, starting transfers between devices: 10.1 us -> 4.08 us  [body(): dw_z = lax.all_to_all(dw_y, 'zh', 0, 0, tiled=True)]
    all_to_all x1 -> x0, waiting for transfers between devices: 5.01 us -> none  [body(): lax.all_to_all(sent.reshape(8, 2 * far, lanes), ('zl', 'yh', 'co'), 0, 0,...]
    ppermute x4, starting transfers between devices: 15.3 us -> 11.2 us  [swap(): return lax.ppermute(x, axis, [(0, 1), (1, 0)])]
    ppermute x6, waiting for transfers between devices: 8.66 us -> 12.3 us  [hop(): return lax.ppermute(x, 'x', [(i, (i + step) % n) for i in range(n)])]
    all_to_all x1, blocking collectives: 15.2 us -> 12.3 us  [body(): dw_y = lax.all_to_all(dw_c, NEAR, 0, 0, tiled=True)]
  transfers between devices with their start and end apart: 13 -> 12, of which waited for: 6 -> 8; matrix products, arithmetic and copies ran while one was open for 1% -> 1% of each run, Pallas kernels for 3% -> 2%
where the time goes in v7:
time: 183 us; the launch traced here: 180 us
  blocking collectives  84.9 us (46%)
  waiting for transfers between devices  41.5 us (23%)
  starting transfers between devices  39.6 us (22%)
  Pallas kernels  8.45 us (5%)
  local copies, waits for them, and re-layouts  3.82 us (2%)
    all_to_all x1, blocking collectives, body(): got = lax.all_to_all(sent.transpose(1, 0, 2), DP, 0, 0, tiled=True)  72.6 us
    ppermute x4, waiting for transfers between devices, swap(): return lax.ppermute(x, axis, [(0, 1), (1, 0)])  17.9 us
    ppermute x6, starting transfers between devices, hop(): return lax.ppermute(x, 'x', [(i, (i + step) % n) for i in range(n)])  17 us
    all_to_all x1, blocking collectives, body(): dw_y = lax.all_to_all(dw_c, NEAR, 0, 0, tiled=True)  12.3 us
    ppermute x6, waiting for transfers between devices, hop(): return lax.ppermute(x, 'x', [(i, (i + step) % n) for i in range(n)])  12.3 us
    all_to_all x1, waiting for transfers between devices, spread(): lax.all_to_all(jnp.broadcast_to(x[None], (count,) + x.shape), axis, 0, 0,...  11.3 us
    ppermute x4, starting transfers between devices, swap(): return lax.ppermute(x, axis, [(0, 1), (1, 0)])  11.2 us
    pallas_call x6, Pallas kernels, call(): pl.pallas_call(kernel, in_specs=[pl.BlockSpec(memory_space=pltpu.HBM) if...  8.45 us
  transfers between devices with their start and end apart: 12, of which 8 were waited for; matrix products, arithmetic and copies ran while one was open for 1% of the time, Pallas kernels for 2%

profile of v7, /device:TPU:1, one launch (start us, length us, event | category | flops | bytes accessed | tf_op | source)
XLA Modules:
  0.0 180.5 jit_solution(8372014298470306632)
XLA Ops:
  0.6 1.4 shard_map.102
  2.0 0.2 copy.18
  2.2 72.6 %all_to_all.20 = bf16[128,8,128]{2,1,0:T(8,128)(2,1)S(1)} all-to-all(bf16[128,8,128]{2,1,0:T(8,128)(2,1)S(1)} %copy.18), channel_id=1, replica_groups=mesh['zh'=16,'zl'=2,'yh'=2,'co'=2,'x'=4,'yl'=2] {'zh','zl','yh','co'}, dimensions={0} | all-to-all | bytes 524288 | tf_op jit(solution)/shard_map/all_to_all | solution.py:244
  74.8 1.0 broadcast_in_dim.2
  75.8 0.0 copy-start.1
  75.8 7.4 %all-to-all-start.1 = ((bf16[4,5,128,128]{3,2,1,0:T(8,128)(2,1)}), bf16[4,5,128,128]{3,2,1,0:T(8,128)(2,1)S(1)}, u32[]{:S(2)}, u32[]{:S(2)}) async-start(bf16[4,5,128,128]{3,2,1,0:T(8,128)(2,1)} %broadcast_in_dim.2), calls=%async_computation.1 | async-start | bytes 1310720 | tf_op jit(solution)/shard_map/all_to_all | solution.py:202
  83.2 11.3 %all-to-all-done.1.wa_ref = bf16[4,5,128,128]{3,2,1,0:T(8,128)(2,1)S(1)} async-done(((bf16[4,5,128,128]{3,2,1,0:T(8,128)(2,1)}), bf16[4,5,128,128]{3,2,1,0:T(8,128)(2,1)S(1)}, u32[]{:S(2)}, u32[]{:S(2)}) %all-to-all-start.1) | async-done | bytes 655392 | tf_op jit(solution)/shard_map/all_to_all | solution.py:202
  94.5 2.4 %collective-permute-start.4 = (bf16[4,5,128,128]{3,2,1,0:T(8,128)(2,1)S(1)}, bf16[4,5,128,128]{3,2,1,0:T(8,128)(2,1)S(1)}, u32[]{:S(2)}, u32[]{:S(2)}) collective-permute-start(bf16[4,5,128,128]{3,2,1,0:T(8,128)(2,1)S(1)} %all-to-all-done.1.wa_ref), channel_id=1, source_target_pairs={{0,8},{8,0},{1,9},{9,1},{2,10},{10,2},{3,11},{11,3},{4,12},{12,4},... | collective-permute-start | bytes 1966088 | tf_op jit(solution)/shard_map/ppermute | solution.py:211
  96.9 0.1 pad_add_fusion.own_ref
  97.0 0.8 shard_map.103
  97.8 4.4 %collective-permute-start.2 = (bf16[192,256]{1,0:T(8,128)(2,1)S(1)}, bf16[192,256]{1,0:T(8,128)(2,1)S(1)}, u32[]{:S(2)}, u32[]{:S(2)}) collective-permute-start(bf16[192,256]{1,0:T(8,128)(2,1)S(1)} %get-tuple-element.16.refs_0_), channel_id=1, source_target_pairs={{0,6},{2,0},{4,2},{6,4},{1,7},{3,1},{5,3},{7,5},{8,14},{10,8},{12,... | collective-permute-start | bytes 294920 | tf_op jit(solution)/shard_map/ppermute | solution.py:207
  102.2 2.4 %collective-permute-start.1 = (bf16[192,256]{1,0:T(8,128)(2,1)S(1)}, bf16[192,256]{1,0:T(8,128)(2,1)S(1)}, u32[]{:S(2)}, u32[]{:S(2)}) collective-permute-start(bf16[192,256]{1,0:T(8,128)(2,1)S(1)} %get-tuple-element.16.refs_0_), channel_id=1, source_target_pairs={{0,4},{2,6},{4,0},{6,2},{1,5},{3,7},{5,1},{7,3},{8,12},{10,14},{12... | collective-permute-start | bytes 294920 | tf_op jit(solution)/shard_map/ppermute | solution.py:207
  104.6 2.5 %collective-permute-start = (bf16[192,256]{1,0:T(8,128)(2,1)S(1)}, bf16[192,256]{1,0:T(8,128)(2,1)S(1)}, u32[]{:S(2)}, u32[]{:S(2)}) collective-permute-start(bf16[192,256]{1,0:T(8,128)(2,1)S(1)} %get-tuple-element.16.refs_0_), channel_id=1, source_target_pairs={{0,2},{2,4},{4,6},{6,0},{1,3},{3,5},{5,7},{7,1},{8,10},{10,12},{12... | collective-permute-start | bytes 294920 | tf_op jit(solution)/shard_map/ppermute | solution.py:207
  107.2 0.0 collective-permute-done.2.refs_3_
  107.2 2.5 %collective-permute-done.1.refs_2_ = bf16[192,256]{1,0:T(8,128)(2,1)S(1)} collective-permute-done((bf16[192,256]{1,0:T(8,128)(2,1)S(1)}, bf16[192,256]{1,0:T(8,128)(2,1)S(1)}, u32[]{:S(2)}, u32[]{:S(2)}) %collective-permute-start.1) | collective-permute-done | bytes 98336 | tf_op jit(solution)/shard_map/ppermute | solution.py:207
  109.7 2.0 %collective-permute-done.refs_1_ = bf16[192,256]{1,0:T(8,128)(2,1)S(1)} collective-permute-done((bf16[192,256]{1,0:T(8,128)(2,1)S(1)}, bf16[192,256]{1,0:T(8,128)(2,1)S(1)}, u32[]{:S(2)}, u32[]{:S(2)}) %collective-permute-start) | collective-permute-done | bytes 98336 | tf_op jit(solution)/shard_map/ppermute | solution.py:207
  111.7 0.8 pad_maximum_fusion
  112.5 2.3 %collective-permute-start.3 = (bf16[4,192,256]{2,1,0:T(8,128)(2,1)}, bf16[4,192,256]{2,1,0:T(8,128)(2,1)S(1)}, u32[]{:S(2)}, u32[]{:S(2)}) collective-permute-start(bf16[4,192,256]{2,1,0:T(8,128)(2,1)} %pad_maximum_fusion), channel_id=1, source_target_pairs={{0,1},{1,0},{2,3},{3,2},{4,5},{5,4},{6,7},{7,6},{8,9},{9,8},{10,11... | collective-permute-start | bytes 1179656 | tf_op jit(solution)/shard_map/ppermute | solution.py:211
  114.8 0.0 copy-done.1
  114.8 0.3 reshape.51
  115.1 0.3 copy.20
  115.3 0.5 reshape.61.gain_ref
  115.8 8.0 %collective-permute-done.3.refs_4_ = bf16[4,192,256]{2,1,0:T(8,128)(2,1)S(1)} collective-permute-done((bf16[4,192,256]{2,1,0:T(8,128)(2,1)}, bf16[4,192,256]{2,1,0:T(8,128)(2,1)S(1)}, u32[]{:S(2)}, u32[]{:S(2)}) %collective-permute-start.3) | collective-permute-done | bytes 393248 | tf_op jit(solution)/shard_map/ppermute | solution.py:211
  123.9 1.3 shard_map.104.normed_ref
  125.1 0.0 collective-permute-done.4.wb_ref
  125.1 0.0 copy-done
  125.1 3.6 %shard_map.105 = (bf16[2,192,128]{2,1,0:T(8,128)(2,1)}, bf16[4,8,24,384]{3,2,1,0:T(8,128)(2,1)S(1)}, bf16[4,8,24,384]{3,2,1,0:T(8,128)(2,1)S(1)}, bf16[384,256]{1,0:T(8,128)(2,1)S(1)}, bf16[8,192,384]{2,1,0:T(8,128)(2,1)S(1)}) custom-call(s32[2]{0:T(128)S(1)} %pad_add_fusion.own_ref, bf16[8,192,256]{2,1,0:T(8,128)(2,1)S(1)} %shard_map.104.normed_ref, ...), custom_call_target="tpu_custom_call" | custom-call | tf_op jit(solution)/shard_map/pallas_call | solution.py:32
  128.7 4.1 %collective-permute-start.5 = (bf16[4,192,384]{2,1,0:T(8,128)(2,1)S(1)}, bf16[4,192,384]{2,1,0:T(8,128)(2,1)S(1)}, u32[]{:S(2)}, u32[]{:S(2)}) collective-permute-start(bf16[4,192,384]{2,1,0:T(8,128)(2,1)S(1)} %bitcast.40), channel_id=1, source_target_pairs={{0,8},{8,0},{1,9},{9,1},{2,10},{10,2},{3,11},{11,3},{4,12},{12,4},... | collective-permute-start | bytes 1769480 | tf_op jit(solution)/shard_map/ppermute | solution.py:211
  132.8 1.6 collective-permute-done.5
  134.4 0.2 fusion
  134.6 12.3 %all_to_all.21 = bf16[4,192,384]{2,1,0:T(8,128)(2,1)S(1)} all-to-all(bf16[4,192,384]{2,1,0:T(8,128)(2,1)S(1)} %fusion), channel_id=1, replica_groups=mesh['zh'=16,'zl'=2,'yh'=2,'co'=2,'x'=4,'yl'=2] {'zl','yh'}, dimensions={0} | all-to-all | bytes 1179648 | tf_op jit(solution)/shard_map/all_to_all | solution.py:269
  147.0 0.1 reduce_sum.21
  147.2 0.7 copy.23
  147.9 4.1 %all-to-all-start.3 = ((bf16[16,9,4,128]{3,2,1,0:T(4,128)(2,1)}), bf16[16,9,4,128]{3,2,1,0:T(4,128)(2,1)S(1)}, u32[]{:S(2)}, u32[]{:S(2)}) async-start(bf16[16,9,4,128]{3,2,1,0:T(4,128)(2,1)} %copy.23), calls=%async_computation.3 | async-start | bytes 294912 | tf_op jit(solution)/shard_map/all_to_all | solution.py:272
  152.0 0.6 shard_map.106
  152.6 2.5 %collective-permute-start.6 = (bf16[2,192,256]{2,1,0:T(8,128)(2,1)S(1)}, bf16[2,192,256]{2,1,0:T(8,128)(2,1)S(1)}, u32[]{:S(2)}, u32[]{:S(2)}) collective-permute-start(bf16[2,192,256]{2,1,0:T(8,128)(2,1)S(1)} %get-tuple-element.23), channel_id=1, source_target_pairs={{0,6},{2,0},{4,2},{6,4},{1,7},{3,1},{5,3},{7,5},{8,14},{10,8},{12,... | collective-permute-start | bytes 589832 | tf_op jit(solution)/shard_map/ppermute | solution.py:207
  155.1 2.5 %collective-permute-start.7 = (bf16[2,192,256]{2,1,0:T(8,128)(2,1)S(1)}, bf16[2,192,256]{2,1,0:T(8,128)(2,1)S(1)}, u32[]{:S(2)}, u32[]{:S(2)}) collective-permute-start(bf16[2,192,256]{2,1,0:T(8,128)(2,1)S(1)} %get-tuple-element.24), channel_id=1, source_target_pairs={{0,4},{2,6},{4,0},{6,2},{1,5},{3,7},{5,1},{7,3},{8,12},{10,14},{12... | collective-permute-start | bytes 589832 | tf_op jit(solution)/shard_map/ppermute | solution.py:207
  157.5 2.8 %collective-permute-start.8 = (bf16[2,192,256]{2,1,0:T(8,128)(2,1)S(1)}, bf16[2,192,256]{2,1,0:T(8,128)(2,1)S(1)}, u32[]{:S(2)}, u32[]{:S(2)}) collective-permute-start(bf16[2,192,256]{2,1,0:T(8,128)(2,1)S(1)} %get-tuple-element.25), channel_id=1, source_target_pairs={{0,2},{2,4},{4,6},{6,0},{1,3},{3,5},{5,7},{7,1},{8,10},{10,12},{12... | collective-permute-start | bytes 589832 | tf_op jit(solution)/shard_map/ppermute | solution.py:207
  160.3 0.0 collective-permute-done.6.refs_1_
  160.3 2.9 %collective-permute-done.7.refs_2_ = bf16[2,192,256]{2,1,0:T(8,128)(2,1)S(1)} collective-permute-done((bf16[2,192,256]{2,1,0:T(8,128)(2,1)S(1)}, bf16[2,192,256]{2,1,0:T(8,128)(2,1)S(1)}, u32[]{:S(2)}, u32[]{:S(2)}) %collective-permute-start.7) | collective-permute-done | bytes 196640 | tf_op jit(solution)/shard_map/ppermute | solution.py:207
  163.3 4.8 %collective-permute-done.8.refs_3_ = bf16[2,192,256]{2,1,0:T(8,128)(2,1)S(1)} collective-permute-done((bf16[2,192,256]{2,1,0:T(8,128)(2,1)S(1)}, bf16[2,192,256]{2,1,0:T(8,128)(2,1)S(1)}, u32[]{:S(2)}, u32[]{:S(2)}) %collective-permute-start.8) | collective-permute-done | bytes 196640 | tf_op jit(solution)/shard_map/ppermute | solution.py:207
  168.1 0.1 pad_maximum_fusion.1
  168.2 2.3 %collective-permute-start.9 = (bf16[4,192,256]{2,1,0:T(8,128)(2,1)S(1)}, bf16[4,192,256]{2,1,0:T(8,128)(2,1)S(1)}, u32[]{:S(2)}, u32[]{:S(2)}) collective-permute-start(bf16[4,192,256]{2,1,0:T(8,128)(2,1)S(1)} %pad_maximum_fusion.1), channel_id=1, source_target_pairs={{0,1},{1,0},{2,3},{3,2},{4,5},{5,4},{6,7},{7,6},{8,9},{9,8},{10,11... | collective-permute-start | bytes 1179656 | tf_op jit(solution)/shard_map/ppermute | solution.py:211
  170.5 8.2 %collective-permute-done.9.refs_4_ = bf16[4,192,256]{2,1,0:T(8,128)(2,1)S(1)} collective-permute-done((bf16[4,192,256]{2,1,0:T(8,128)(2,1)S(1)}, bf16[4,192,256]{2,1,0:T(8,128)(2,1)S(1)}, u32[]{:S(2)}, u32[]{:S(2)}) %collective-permute-start.9) | collective-permute-done | bytes 393248 | tf_op jit(solution)/shard_map/ppermute | solution.py:211
  178.7 0.9 shard_map.107
  179.7 0.0 all-to-all-done.3
  179.7 0.1 convert_reduce_fusion
  179.8 0.7 fusion.1
  (14 shorter events, 0.2 us)
Async XLA Ops:
  75.8 39.0 %copy-start.1 = (f32[1536]{0:T(1024)S(1)}, f32[1536]{0:T(1024)}, u32[]{:S(2)}) copy-start(f32[1536]{0:T(1024)} %param.10) | copy-start | bytes 18436
  75.8 18.7 %all-to-all-start.1 = ((bf16[4,5,128,128]{3,2,1,0:T(8,128)(2,1)}), bf16[4,5,128,128]{3,2,1,0:T(8,128)(2,1)S(1)}, u32[]{:S(2)}, u32[]{:S(2)}) async-start(bf16[4,5,128,128]{3,2,1,0:T(8,128)(2,1)} %broadcast_in_dim.2), calls=%async_computation.1 | async-start | bytes 1310720 | tf_op jit(solution)/shard_map/all_to_all | solution.py:202
  94.5 30.7 %collective-permute-start.4 = (bf16[4,5,128,128]{3,2,1,0:T(8,128)(2,1)S(1)}, bf16[4,5,128,128]{3,2,1,0:T(8,128)(2,1)S(1)}, u32[]{:S(2)}, u32[]{:S(2)}) collective-permute-start(bf16[4,5,128,128]{3,2,1,0:T(8,128)(2,1)S(1)} %all-to-all-done.1.wa_ref), channel_id=1, source_target_pairs={{0,8},{8,0},{1,9},{9,1},{2,10},{10,2},{3,11},{11,3},{4,12},{12,4},... | collective-permute-start | bytes 1966088 | tf_op jit(solution)/shard_map/ppermute | solution.py:211
  97.8 9.4 %collective-permute-start.2 = (bf16[192,256]{1,0:T(8,128)(2,1)S(1)}, bf16[192,256]{1,0:T(8,128)(2,1)S(1)}, u32[]{:S(2)}, u32[]{:S(2)}) collective-permute-start(bf16[192,256]{1,0:T(8,128)(2,1)S(1)} %get-tuple-element.16.refs_0_), channel_id=1, source_target_pairs={{0,6},{2,0},{4,2},{6,4},{1,7},{3,1},{5,3},{7,5},{8,14},{10,8},{12,... | collective-permute-start | bytes 294920 | tf_op jit(solution)/shard_map/ppermute | solution.py:207
  102.2 7.5 %collective-permute-start.1 = (bf16[192,256]{1,0:T(8,128)(2,1)S(1)}, bf16[192,256]{1,0:T(8,128)(2,1)S(1)}, u32[]{:S(2)}, u32[]{:S(2)}) collective-permute-start(bf16[192,256]{1,0:T(8,128)(2,1)S(1)} %get-tuple-element.16.refs_0_), channel_id=1, source_target_pairs={{0,4},{2,6},{4,0},{6,2},{1,5},{3,7},{5,1},{7,3},{8,12},{10,14},{12... | collective-permute-start | bytes 294920 | tf_op jit(solution)/shard_map/ppermute | solution.py:207
  104.6 7.0 %collective-permute-start = (bf16[192,256]{1,0:T(8,128)(2,1)S(1)}, bf16[192,256]{1,0:T(8,128)(2,1)S(1)}, u32[]{:S(2)}, u32[]{:S(2)}) collective-permute-start(bf16[192,256]{1,0:T(8,128)(2,1)S(1)} %get-tuple-element.16.refs_0_), channel_id=1, source_target_pairs={{0,2},{2,4},{4,6},{6,0},{1,3},{3,5},{5,7},{7,1},{8,10},{10,12},{12... | collective-permute-start | bytes 294920 | tf_op jit(solution)/shard_map/ppermute | solution.py:207
  112.5 11.4 %collective-permute-start.3 = (bf16[4,192,256]{2,1,0:T(8,128)(2,1)}, bf16[4,192,256]{2,1,0:T(8,128)(2,1)S(1)}, u32[]{:S(2)}, u32[]{:S(2)}) collective-permute-start(bf16[4,192,256]{2,1,0:T(8,128)(2,1)} %pad_maximum_fusion), channel_id=1, source_target_pairs={{0,1},{1,0},{2,3},{3,2},{4,5},{5,4},{6,7},{7,6},{8,9},{9,8},{10,11... | collective-permute-start | bytes 1179656 | tf_op jit(solution)/shard_map/ppermute | solution.py:211
  123.9 1.3 copy-start
  128.7 5.7 %collective-permute-start.5 = (bf16[4,192,384]{2,1,0:T(8,128)(2,1)S(1)}, bf16[4,192,384]{2,1,0:T(8,128)(2,1)S(1)}, u32[]{:S(2)}, u32[]{:S(2)}) collective-permute-start(bf16[4,192,384]{2,1,0:T(8,128)(2,1)S(1)} %bitcast.40), channel_id=1, source_target_pairs={{0,8},{8,0},{1,9},{9,1},{2,10},{10,2},{3,11},{11,3},{4,12},{12,4},... | collective-permute-start | bytes 1769480 | tf_op jit(solution)/shard_map/ppermute | solution.py:211
  147.9 31.7 %all-to-all-start.3 = ((bf16[16,9,4,128]{3,2,1,0:T(4,128)(2,1)}), bf16[16,9,4,128]{3,2,1,0:T(4,128)(2,1)S(1)}, u32[]{:S(2)}, u32[]{:S(2)}) async-start(bf16[16,9,4,128]{3,2,1,0:T(4,128)(2,1)} %copy.23), calls=%async_computation.3 | async-start | bytes 294912 | tf_op jit(solution)/shard_map/all_to_all | solution.py:272
  152.6 7.7 %collective-permute-start.6 = (bf16[2,192,256]{2,1,0:T(8,128)(2,1)S(1)}, bf16[2,192,256]{2,1,0:T(8,128)(2,1)S(1)}, u32[]{:S(2)}, u32[]{:S(2)}) collective-permute-start(bf16[2,192,256]{2,1,0:T(8,128)(2,1)S(1)} %get-tuple-element.23), channel_id=1, source_target_pairs={{0,6},{2,0},{4,2},{6,4},{1,7},{3,1},{5,3},{7,5},{8,14},{10,8},{12,... | collective-permute-start | bytes 589832 | tf_op jit(solution)/shard_map/ppermute | solution.py:207
  155.1 8.2 %collective-permute-start.7 = (bf16[2,192,256]{2,1,0:T(8,128)(2,1)S(1)}, bf16[2,192,256]{2,1,0:T(8,128)(2,1)S(1)}, u32[]{:S(2)}, u32[]{:S(2)}) collective-permute-start(bf16[2,192,256]{2,1,0:T(8,128)(2,1)S(1)} %get-tuple-element.24), channel_id=1, source_target_pairs={{0,4},{2,6},{4,0},{6,2},{1,5},{3,7},{5,1},{7,3},{8,12},{10,14},{12... | collective-permute-start | bytes 589832 | tf_op jit(solution)/shard_map/ppermute | solution.py:207
  157.5 10.6 %collective-permute-start.8 = (bf16[2,192,256]{2,1,0:T(8,128)(2,1)S(1)}, bf16[2,192,256]{2,1,0:T(8,128)(2,1)S(1)}, u32[]{:S(2)}, u32[]{:S(2)}) collective-permute-start(bf16[2,192,256]{2,1,0:T(8,128)(2,1)S(1)} %get-tuple-element.25), channel_id=1, source_target_pairs={{0,2},{2,4},{4,6},{6,0},{1,3},{3,5},{5,7},{7,1},{8,10},{10,12},{12... | collective-permute-start | bytes 589832 | tf_op jit(solution)/shard_map/ppermute | solution.py:207
  168.2 10.6 %collective-permute-start.9 = (bf16[4,192,256]{2,1,0:T(8,128)(2,1)S(1)}, bf16[4,192,256]{2,1,0:T(8,128)(2,1)S(1)}, u32[]{:S(2)}, u32[]{:S(2)}) collective-permute-start(bf16[4,192,256]{2,1,0:T(8,128)(2,1)S(1)} %pad_maximum_fusion.1), channel_id=1, source_target_pairs={{0,1},{1,0},{2,3},{3,2},{4,5},{5,4},{6,7},{7,6},{8,9},{9,8},{10,11... | collective-permute-start | bytes 1179656 | tf_op jit(solution)/shard_map/ppermute | solution.py:211

commit v8 on v7

--- a/solution.py
+++ b/solution.py
@@ -104,18 +104,17 @@
 def block_of(own_ref, k, blocks):
     n = blocks // 2
     x, y = own_ref[0] // 2, own_ref[0] % 2
-    return ((x + n - k % n) % n) * 2 + (y + k // n) % 2
+    return ((x + n - k // 2) % n) * 2 + (y + k) % 2
 
 
 def norm_kernel(own_ref, live_ref, gain_ref, *refs):
-    near_refs, across_ref, normed_ref = refs[:-2], refs[-2], refs[-1]
+    normed_ref = refs[-1]
     blocks, width, slots = normed_ref.shape
     total = blocks * width
     live = live_ref[0:1, :]
 
     def block(k):
-        n = blocks // 2
-        return (near_refs[k][...] if k < n else across_ref[k - n]).astype(f32)
+        return refs[k // 2][k % 2].astype(f32)
 
     s = jnp.zeros((1, slots), f32)
     for k in range(blocks):
@@ -179,8 +178,7 @@
 def backward_kernel(w_ref, delta_ref, *partial_refs):
     blocks = 2 * len(partial_refs)
     for k in range(blocks):
-        n = blocks // 2
-        partial_refs[k % n][k // n] = nn(w_ref[k], delta_ref[...]).astype(bf16)
+        partial_refs[k // 2][k % 2] = nn(w_ref[k], delta_ref[...]).astype(bf16)
 
 
 def join_kernel(*refs):
@@ -246,9 +244,8 @@
     w_own = spread(got[3:], NEAR, 4)
     w_other = swap(w_own, "co")
     turned, live = call(turn_kernel, [((width, slots), bf16), ((8, slots), f32)], own, got)
-    whole = [turned] + [hop(turned, dx) for dx in range(1, blocks // 2)]
-    stacked = jnp.stack(whole)
-    whole.append(swap(stacked, "yl"))
+    pair = jnp.stack([turned, swap(turned, "yl")])
+    whole = [pair] + [hop(pair, dx) for dx in range(1, blocks // 2)]
     gain = norm_gain.reshape(blocks, 16, 4, 3).transpose(0, 2, 3, 1).reshape(blocks, width, 1)
     (normed,) = call(norm_kernel, [((blocks, width, slots), bf16)], own, live, gain, *whole)
     up = grad_owned.reshape(peers, 2, width).transpose(1, 2, 0)

time: 183 us -> 179 us (0.978); the launches traced: 180 us -> 179 us
  blocking collectives: 84.9 us -> 104 us
  waiting for transfers between devices: 41.5 us -> 31.6 us
  starting transfers between devices: 39.6 us -> 30.3 us
    all_to_all x0 -> x1, blocking collectives: none -> 18.5 us  [spread(): lax.all_to_all(jnp.broadcast_to(x[None], (count,) + x.shape), axis, 0, 0,...]
    all_to_all x1 -> x0, waiting for transfers between devices: 11.3 us -> none  [spread(): lax.all_to_all(jnp.broadcast_to(x[None], (count,) + x.shape), axis, 0, 0,...]
    all_to_all x1 -> x0, starting transfers between devices: 7.38 us -> none  [spread(): lax.all_to_all(jnp.broadcast_to(x[None], (count,) + x.shape), axis, 0, 0,...]
    ppermute x6, waiting for transfers between devices: 12.3 us -> 16.9 us  [hop(): return lax.ppermute(x, 'x', [(i, (i + step) % n) for i in range(n)])]
    ppermute x4, waiting for transfers between devices: 17.9 us -> 14.8 us  [swap(): return lax.ppermute(x, axis, [(0, 1), (1, 0)])]
  transfers between devices with their start and end apart: 12 -> 11, of which waited for: 8 -> 7; matrix products, arithmetic and copies ran while one was open for 1% -> 1% of each run, Pallas kernels for 2% -> 2%
where the time goes in v8:
time: 179 us
  blocking collectives  104 us (58%)
  waiting for transfers between devices  31.6 us (18%)
  starting transfers between devices  30.3 us (17%)
  Pallas kernels  8.45 us (5%)
  local copies, waits for them, and re-layouts  2.96 us (2%)
    all_to_all x1, blocking collectives, body(): got = lax.all_to_all(sent.transpose(1, 0, 2), DP, 0, 0, tiled=True)  72.6 us
    all_to_all x1, blocking collectives, spread(): lax.all_to_all(jnp.broadcast_to(x[None], (count,) + x.shape), axis, 0, 0,...  18.5 us
    ppermute x6, waiting for transfers between devices, hop(): return lax.ppermute(x, 'x', [(i, (i + step) % n) for i in range(n)])  16.9 us
    ppermute x6, starting transfers between devices, hop(): return lax.ppermute(x, 'x', [(i, (i + step) % n) for i in range(n)])  16.6 us
    ppermute x4, waiting for transfers between devices, swap(): return lax.ppermute(x, axis, [(0, 1), (1, 0)])  14.8 us
    all_to_all x1, blocking collectives, body(): dw_y = lax.all_to_all(dw_c, NEAR, 0, 0, tiled=True)  12.8 us
    ppermute x4, starting transfers between devices, swap(): return lax.ppermute(x, axis, [(0, 1), (1, 0)])  10.2 us
    pallas_call x6, Pallas kernels, call(): pl.pallas_call(kernel, in_specs=[pl.BlockSpec(memory_space=pltpu.HBM) if...  8.45 us
  transfers between devices with their start and end apart: 11, of which 7 were waited for; matrix products, arithmetic and copies ran while one was open for 1% of the time, Pallas kernels for 2%

profile of v8, /device:TPU:1, one launch (start us, length us, event | category | flops | bytes accessed | tf_op | source)
XLA Modules:
  0.0 178.8 jit_solution(10091674094932410218)
XLA Ops:
  0.6 1.4 shard_map.102
  2.0 0.2 copy.18
  2.2 72.6 %all_to_all.20 = bf16[128,8,128]{2,1,0:T(8,128)(2,1)S(1)} all-to-all(bf16[128,8,128]{2,1,0:T(8,128)(2,1)S(1)} %copy.18), channel_id=1, replica_groups=mesh['zh'=16,'zl'=2,'yh'=2,'co'=2,'x'=4,'yl'=2] {'zh','zl','yh','co'}, dimensions={0} | all-to-all | bytes 524288 | tf_op jit(solution)/shard_map/all_to_all | solution.py:242
  74.8 0.1 broadcast_in_dim.2
  74.9 0.0 copy-start.1
  75.0 18.5 %all_to_all.21.wa_ref = bf16[4,5,128,128]{3,2,1,0:T(8,128)(2,1)S(1)} all-to-all(bf16[4,5,128,128]{3,2,1,0:T(8,128)(2,1)S(1)} %broadcast_in_dim.2), channel_id=1, replica_groups=mesh['zh'=16,'zl'=2,'yh'=2,'co'=2,'x'=4,'yl'=2] {'zl','yh'}, dimensions={0} | all-to-all | bytes 1310720 | tf_op jit(solution)/shard_map/all_to_all | solution.py:200
  93.5 2.6 %collective-permute-start.4 = (bf16[4,5,128,128]{3,2,1,0:T(8,128)(2,1)S(1)}, bf16[4,5,128,128]{3,2,1,0:T(8,128)(2,1)S(1)}, u32[]{:S(2)}, u32[]{:S(2)}) collective-permute-start(bf16[4,5,128,128]{3,2,1,0:T(8,128)(2,1)S(1)} %all_to_all.21.wa_ref), channel_id=1, source_target_pairs={{0,8},{8,0},{1,9},{9,1},{2,10},{10,2},{3,11},{11,3},{4,12},{12,4},... | collective-permute-start | bytes 1966088 | tf_op jit(solution)/shard_map/ppermute | solution.py:209
  96.1 0.1 pad_add_fusion.own_ref
  96.2 0.8 shard_map.103
  97.0 2.3 %collective-permute-start = (bf16[192,256]{1,0:T(8,128)(2,1)S(1)}, bf16[192,256]{1,0:T(8,128)(2,1)S(1)}, u32[]{:S(2)}, u32[]{:S(2)}) collective-permute-start(bf16[192,256]{1,0:T(8,128)(2,1)S(1)} %get-tuple-element.16), channel_id=1, source_target_pairs={{0,1},{1,0},{2,3},{3,2},{4,5},{5,4},{6,7},{7,6},{8,9},{9,8},{10,11... | collective-permute-start | bytes 294920 | tf_op jit(solution)/shard_map/ppermute | solution.py:209
  99.3 3.9 %collective-permute-done = bf16[192,256]{1,0:T(8,128)(2,1)S(1)} collective-permute-done((bf16[192,256]{1,0:T(8,128)(2,1)S(1)}, bf16[192,256]{1,0:T(8,128)(2,1)S(1)}, u32[]{:S(2)}, u32[]{:S(2)}) %collective-permute-start) | collective-permute-done | bytes 98336 | tf_op jit(solution)/shard_map/ppermute | solution.py:209
  103.2 4.4 %collective-permute-start.3 = (bf16[2,192,256]{2,1,0:T(8,128)(2,1)S(1)}, bf16[2,192,256]{2,1,0:T(8,128)(2,1)S(1)}, u32[]{:S(2)}, u32[]{:S(2)}) collective-permute-start(bf16[2,192,256]{2,1,0:T(8,128)(2,1)S(1)} %pad_maximum_fusion.1.refs_0_), channel_id=1, source_target_pairs={{0,6},{2,0},{4,2},{6,4},{1,7},{3,1},{5,3},{7,5},{8,14},{10,8},{12,... | collective-permute-start | bytes 589832 | tf_op jit(solution)/shard_map/ppermute | solution.py:205
  107.6 2.4 %collective-permute-start.2 = (bf16[2,192,256]{2,1,0:T(8,128)(2,1)S(1)}, bf16[2,192,256]{2,1,0:T(8,128)(2,1)S(1)}, u32[]{:S(2)}, u32[]{:S(2)}) collective-permute-start(bf16[2,192,256]{2,1,0:T(8,128)(2,1)S(1)} %pad_maximum_fusion.1.refs_0_), channel_id=1, source_target_pairs={{0,4},{2,6},{4,0},{6,2},{1,5},{3,7},{5,1},{7,3},{8,12},{10,14},{12... | collective-permute-start | bytes 589832 | tf_op jit(solution)/shard_map/ppermute | solution.py:205
  110.1 2.5 %collective-permute-start.1 = (bf16[2,192,256]{2,1,0:T(8,128)(2,1)S(1)}, bf16[2,192,256]{2,1,0:T(8,128)(2,1)S(1)}, u32[]{:S(2)}, u32[]{:S(2)}) collective-permute-start(bf16[2,192,256]{2,1,0:T(8,128)(2,1)S(1)} %pad_maximum_fusion.1.refs_0_), channel_id=1, source_target_pairs={{0,2},{2,4},{4,6},{6,0},{1,3},{3,5},{5,7},{7,1},{8,10},{10,12},{12... | collective-permute-start | bytes 589832 | tf_op jit(solution)/shard_map/ppermute | solution.py:205
  112.6 0.0 copy-done.1
  112.6 0.3 reshape.51
  112.9 0.3 copy.20
  113.2 0.5 reshape.61.gain_ref
  113.7 0.0 collective-permute-done.3.refs_3_
  113.7 2.7 %collective-permute-done.2.refs_2_ = bf16[2,192,256]{2,1,0:T(8,128)(2,1)S(1)} collective-permute-done((bf16[2,192,256]{2,1,0:T(8,128)(2,1)S(1)}, bf16[2,192,256]{2,1,0:T(8,128)(2,1)S(1)}, u32[]{:S(2)}, u32[]{:S(2)}) %collective-permute-start.2) | collective-permute-done | bytes 196640 | tf_op jit(solution)/shard_map/ppermute | solution.py:205
  116.3 5.1 %collective-permute-done.1.refs_1_ = bf16[2,192,256]{2,1,0:T(8,128)(2,1)S(1)} collective-permute-done((bf16[2,192,256]{2,1,0:T(8,128)(2,1)S(1)}, bf16[2,192,256]{2,1,0:T(8,128)(2,1)S(1)}, u32[]{:S(2)}, u32[]{:S(2)}) %collective-permute-start.1) | collective-permute-done | bytes 196640 | tf_op jit(solution)/shard_map/ppermute | solution.py:205
  121.4 0.0 copy-start
  121.4 1.3 shard_map.104.normed_ref
  122.7 0.0 collective-permute-done.4.wb_ref
  122.7 0.0 copy-done
  122.7 3.6 %shard_map.105 = (bf16[2,192,128]{2,1,0:T(8,128)(2,1)}, bf16[4,8,24,384]{3,2,1,0:T(8,128)(2,1)S(1)}, bf16[4,8,24,384]{3,2,1,0:T(8,128)(2,1)S(1)}, bf16[384,256]{1,0:T(8,128)(2,1)S(1)}, bf16[8,192,384]{2,1,0:T(8,128)(2,1)S(1)}) custom-call(s32[2]{0:T(128)S(1)} %pad_add_fusion.own_ref, bf16[8,192,256]{2,1,0:T(8,128)(2,1)S(1)} %shard_map.104.normed_ref, ...), custom_call_target="tpu_custom_call" | custom-call | tf_op jit(solution)/shard_map/pallas_call | solution.py:32
  126.3 3.0 %collective-permute-start.5 = (bf16[4,192,384]{2,1,0:T(8,128)(2,1)S(1)}, bf16[4,192,384]{2,1,0:T(8,128)(2,1)S(1)}, u32[]{:S(2)}, u32[]{:S(2)}) collective-permute-start(bf16[4,192,384]{2,1,0:T(8,128)(2,1)S(1)} %bitcast.35), channel_id=1, source_target_pairs={{0,8},{8,0},{1,9},{9,1},{2,10},{10,2},{3,11},{11,3},{4,12},{12,4},... | collective-permute-start | bytes 1769480 | tf_op jit(solution)/shard_map/ppermute | solution.py:209
  129.3 1.6 collective-permute-done.5
  130.9 0.2 fusion
  131.1 12.8 %all_to_all.22 = bf16[4,192,384]{2,1,0:T(8,128)(2,1)S(1)} all-to-all(bf16[4,192,384]{2,1,0:T(8,128)(2,1)S(1)} %fusion), channel_id=1, replica_groups=mesh['zh'=16,'zl'=2,'yh'=2,'co'=2,'x'=4,'yl'=2] {'zl','yh'}, dimensions={0} | all-to-all | bytes 1179648 | tf_op jit(solution)/shard_map/all_to_all | solution.py:266
  144.0 0.1 reduce_sum.21
  144.2 0.7 copy.23
  144.9 3.5 %all-to-all-start.3 = ((bf16[16,9,4,128]{3,2,1,0:T(4,128)(2,1)}), bf16[16,9,4,128]{3,2,1,0:T(4,128)(2,1)S(1)}, u32[]{:S(2)}, u32[]{:S(2)}) async-start(bf16[16,9,4,128]{3,2,1,0:T(4,128)(2,1)} %copy.23), calls=%async_computation.3 | async-start | bytes 294912 | tf_op jit(solution)/shard_map/all_to_all | solution.py:269
  148.4 0.6 shard_map.106
  149.0 2.2 %collective-permute-start.6 = (bf16[2,192,256]{2,1,0:T(8,128)(2,1)S(1)}, bf16[2,192,256]{2,1,0:T(8,128)(2,1)S(1)}, u32[]{:S(2)}, u32[]{:S(2)}) collective-permute-start(bf16[2,192,256]{2,1,0:T(8,128)(2,1)S(1)} %get-tuple-element.23), channel_id=1, source_target_pairs={{0,6},{2,0},{4,2},{6,4},{1,7},{3,1},{5,3},{7,5},{8,14},{10,8},{12,... | collective-permute-start | bytes 589832 | tf_op jit(solution)/shard_map/ppermute | solution.py:205
  151.2 2.4 %collective-permute-start.7 = (bf16[2,192,256]{2,1,0:T(8,128)(2,1)S(1)}, bf16[2,192,256]{2,1,0:T(8,128)(2,1)S(1)}, u32[]{:S(2)}, u32[]{:S(2)}) collective-permute-start(bf16[2,192,256]{2,1,0:T(8,128)(2,1)S(1)} %get-tuple-element.24), channel_id=1, source_target_pairs={{0,4},{2,6},{4,0},{6,2},{1,5},{3,7},{5,1},{7,3},{8,12},{10,14},{12... | collective-permute-start | bytes 589832 | tf_op jit(solution)/shard_map/ppermute | solution.py:205
  153.6 2.6 %collective-permute-start.8 = (bf16[2,192,256]{2,1,0:T(8,128)(2,1)S(1)}, bf16[2,192,256]{2,1,0:T(8,128)(2,1)S(1)}, u32[]{:S(2)}, u32[]{:S(2)}) collective-permute-start(bf16[2,192,256]{2,1,0:T(8,128)(2,1)S(1)} %get-tuple-element.25), channel_id=1, source_target_pairs={{0,2},{2,4},{4,6},{6,0},{1,3},{3,5},{5,7},{7,1},{8,10},{10,12},{12... | collective-permute-start | bytes 589832 | tf_op jit(solution)/shard_map/ppermute | solution.py:205
  156.3 0.0 collective-permute-done.6.refs_1_
  156.3 3.1 %collective-permute-done.7.refs_2_ = bf16[2,192,256]{2,1,0:T(8,128)(2,1)S(1)} collective-permute-done((bf16[2,192,256]{2,1,0:T(8,128)(2,1)S(1)}, bf16[2,192,256]{2,1,0:T(8,128)(2,1)S(1)}, u32[]{:S(2)}, u32[]{:S(2)}) %collective-permute-start.7) | collective-permute-done | bytes 196640 | tf_op jit(solution)/shard_map/ppermute | solution.py:205
  159.4 6.0 %collective-permute-done.8.refs_3_ = bf16[2,192,256]{2,1,0:T(8,128)(2,1)S(1)} collective-permute-done((bf16[2,192,256]{2,1,0:T(8,128)(2,1)S(1)}, bf16[2,192,256]{2,1,0:T(8,128)(2,1)S(1)}, u32[]{:S(2)}, u32[]{:S(2)}) %collective-permute-start.8) | collective-permute-done | bytes 196640 | tf_op jit(solution)/shard_map/ppermute | solution.py:205
  165.4 0.1 pad_maximum_fusion
  165.4 2.3 %collective-permute-start.9 = (bf16[4,192,256]{2,1,0:T(8,128)(2,1)S(1)}, bf16[4,192,256]{2,1,0:T(8,128)(2,1)S(1)}, u32[]{:S(2)}, u32[]{:S(2)}) collective-permute-start(bf16[4,192,256]{2,1,0:T(8,128)(2,1)S(1)} %pad_maximum_fusion), channel_id=1, source_target_pairs={{0,1},{1,0},{2,3},{3,2},{4,5},{5,4},{6,7},{7,6},{8,9},{9,8},{10,11... | collective-permute-start | bytes 1179656 | tf_op jit(solution)/shard_map/ppermute | solution.py:209
  167.8 9.3 %collective-permute-done.9.refs_4_ = bf16[4,192,256]{2,1,0:T(8,128)(2,1)S(1)} collective-permute-done((bf16[4,192,256]{2,1,0:T(8,128)(2,1)S(1)}, bf16[4,192,256]{2,1,0:T(8,128)(2,1)S(1)}, u32[]{:S(2)}, u32[]{:S(2)}) %collective-permute-start.9) | collective-permute-done | bytes 393248 | tf_op jit(solution)/shard_map/ppermute | solution.py:209
  177.0 0.9 shard_map.107
  177.9 0.0 all-to-all-done.3
  177.9 0.1 convert_reduce_fusion
  178.1 0.7 fusion.1
  (14 shorter events, 0.2 us)
Async XLA Ops:
  74.9 37.6 %copy-start.1 = (f32[1536]{0:T(1024)S(1)}, f32[1536]{0:T(1024)}, u32[]{:S(2)}) copy-start(f32[1536]{0:T(1024)} %param.10) | copy-start | bytes 18436
  93.5 29.2 %collective-permute-start.4 = (bf16[4,5,128,128]{3,2,1,0:T(8,128)(2,1)S(1)}, bf16[4,5,128,128]{3,2,1,0:T(8,128)(2,1)S(1)}, u32[]{:S(2)}, u32[]{:S(2)}) collective-permute-start(bf16[4,5,128,128]{3,2,1,0:T(8,128)(2,1)S(1)} %all_to_all.21.wa_ref), channel_id=1, source_target_pairs={{0,8},{8,0},{1,9},{9,1},{2,10},{10,2},{3,11},{11,3},{4,12},{12,4},... | collective-permute-start | bytes 1966088 | tf_op jit(solution)/shard_map/ppermute | solution.py:209
  97.0 6.2 %collective-permute-start = (bf16[192,256]{1,0:T(8,128)(2,1)S(1)}, bf16[192,256]{1,0:T(8,128)(2,1)S(1)}, u32[]{:S(2)}, u32[]{:S(2)}) collective-permute-start(bf16[192,256]{1,0:T(8,128)(2,1)S(1)} %get-tuple-element.16), channel_id=1, source_target_pairs={{0,1},{1,0},{2,3},{3,2},{4,5},{5,4},{6,7},{7,6},{8,9},{9,8},{10,11... | collective-permute-start | bytes 294920 | tf_op jit(solution)/shard_map/ppermute | solution.py:209
  103.2 10.4 %collective-permute-start.3 = (bf16[2,192,256]{2,1,0:T(8,128)(2,1)S(1)}, bf16[2,192,256]{2,1,0:T(8,128)(2,1)S(1)}, u32[]{:S(2)}, u32[]{:S(2)}) collective-permute-start(bf16[2,192,256]{2,1,0:T(8,128)(2,1)S(1)} %pad_maximum_fusion.1.refs_0_), channel_id=1, source_target_pairs={{0,6},{2,0},{4,2},{6,4},{1,7},{3,1},{5,3},{7,5},{8,14},{10,8},{12,... | collective-permute-start | bytes 589832 | tf_op jit(solution)/shard_map/ppermute | solution.py:205
  107.6 8.7 %collective-permute-start.2 = (bf16[2,192,256]{2,1,0:T(8,128)(2,1)S(1)}, bf16[2,192,256]{2,1,0:T(8,128)(2,1)S(1)}, u32[]{:S(2)}, u32[]{:S(2)}) collective-permute-start(bf16[2,192,256]{2,1,0:T(8,128)(2,1)S(1)} %pad_maximum_fusion.1.refs_0_), channel_id=1, source_target_pairs={{0,4},{2,6},{4,0},{6,2},{1,5},{3,7},{5,1},{7,3},{8,12},{10,14},{12... | collective-permute-start | bytes 589832 | tf_op jit(solution)/shard_map/ppermute | solution.py:205
  110.1 11.4 %collective-permute-start.1 = (bf16[2,192,256]{2,1,0:T(8,128)(2,1)S(1)}, bf16[2,192,256]{2,1,0:T(8,128)(2,1)S(1)}, u32[]{:S(2)}, u32[]{:S(2)}) collective-permute-start(bf16[2,192,256]{2,1,0:T(8,128)(2,1)S(1)} %pad_maximum_fusion.1.refs_0_), channel_id=1, source_target_pairs={{0,2},{2,4},{4,6},{6,0},{1,3},{3,5},{5,7},{7,1},{8,10},{10,12},{12... | collective-permute-start | bytes 589832 | tf_op jit(solution)/shard_map/ppermute | solution.py:205
  121.4 1.3 copy-start
  126.3 4.6 %collective-permute-start.5 = (bf16[4,192,384]{2,1,0:T(8,128)(2,1)S(1)}, bf16[4,192,384]{2,1,0:T(8,128)(2,1)S(1)}, u32[]{:S(2)}, u32[]{:S(2)}) collective-permute-start(bf16[4,192,384]{2,1,0:T(8,128)(2,1)S(1)} %bitcast.35), channel_id=1, source_target_pairs={{0,8},{8,0},{1,9},{9,1},{2,10},{10,2},{3,11},{11,3},{4,12},{12,4},... | collective-permute-start | bytes 1769480 | tf_op jit(solution)/shard_map/ppermute | solution.py:209
  144.9 33.0 %all-to-all-start.3 = ((bf16[16,9,4,128]{3,2,1,0:T(4,128)(2,1)}), bf16[16,9,4,128]{3,2,1,0:T(4,128)(2,1)S(1)}, u32[]{:S(2)}, u32[]{:S(2)}) async-start(bf16[16,9,4,128]{3,2,1,0:T(4,128)(2,1)} %copy.23), calls=%async_computation.3 | async-start | bytes 294912 | tf_op jit(solution)/shard_map/all_to_all | solution.py:269
  149.0 7.3 %collective-permute-start.6 = (bf16[2,192,256]{2,1,0:T(8,128)(2,1)S(1)}, bf16[2,192,256]{2,1,0:T(8,128)(2,1)S(1)}, u32[]{:S(2)}, u32[]{:S(2)}) collective-permute-start(bf16[2,192,256]{2,1,0:T(8,128)(2,1)S(1)} %get-tuple-element.23), channel_id=1, source_target_pairs={{0,6},{2,0},{4,2},{6,4},{1,7},{3,1},{5,3},{7,5},{8,14},{10,8},{12,... | collective-permute-start | bytes 589832 | tf_op jit(solution)/shard_map/ppermute | solution.py:205
  151.2 8.2 %collective-permute-start.7 = (bf16[2,192,256]{2,1,0:T(8,128)(2,1)S(1)}, bf16[2,192,256]{2,1,0:T(8,128)(2,1)S(1)}, u32[]{:S(2)}, u32[]{:S(2)}) collective-permute-start(bf16[2,192,256]{2,1,0:T(8,128)(2,1)S(1)} %get-tuple-element.24), channel_id=1, source_target_pairs={{0,4},{2,6},{4,0},{6,2},{1,5},{3,7},{5,1},{7,3},{8,12},{10,14},{12... | collective-permute-start | bytes 589832 | tf_op jit(solution)/shard_map/ppermute | solution.py:205
  153.6 11.7 %collective-permute-start.8 = (bf16[2,192,256]{2,1,0:T(8,128)(2,1)S(1)}, bf16[2,192,256]{2,1,0:T(8,128)(2,1)S(1)}, u32[]{:S(2)}, u32[]{:S(2)}) collective-permute-start(bf16[2,192,256]{2,1,0:T(8,128)(2,1)S(1)} %get-tuple-element.25), channel_id=1, source_target_pairs={{0,2},{2,4},{4,6},{6,0},{1,3},{3,5},{5,7},{7,1},{8,10},{10,12},{12... | collective-permute-start | bytes 589832 | tf_op jit(solution)/shard_map/ppermute | solution.py:205
  165.4 11.6 %collective-permute-start.9 = (bf16[4,192,256]{2,1,0:T(8,128)(2,1)S(1)}, bf16[4,192,256]{2,1,0:T(8,128)(2,1)S(1)}, u32[]{:S(2)}, u32[]{:S(2)}) collective-permute-start(bf16[4,192,256]{2,1,0:T(8,128)(2,1)S(1)} %pad_maximum_fusion), channel_id=1, source_target_pairs={{0,1},{1,0},{2,3},{3,2},{4,5},{5,4},{6,7},{7,6},{8,9},{9,8},{10,11... | collective-permute-start | bytes 1179656 | tf_op jit(solution)/shard_map/ppermute | solution.py:209

commit v9 on v8

--- a/solution.py
+++ b/solution.py
@@ -130,7 +130,7 @@
         normed_ref[k] = (c * inv * gain_ref[block_of(own_ref, k, blocks)] * live).astype(bf16)
 
 
-def forward_kernel(own_ref, normed_ref, live_ref, wa_ref, wb_ref, up_ref, gated_ref, da_ref, db_ref, delta_ref, w_ref):
+def forward_kernel(own_ref, normed_ref, live_ref, wa_ref, wb_ref, up_ref, gated_ref, db_ref, delta_ref, w_ref):
     blocks, width, slots = normed_ref.shape
     peers = slots // 2
     live = live_ref[0:1, :]
@@ -165,14 +165,22 @@
     gate_delta = (up * value * sig * (1.0 - sig) * live).astype(bf16)
     delta = jnp.concatenate([value_delta, gate_delta], axis=0)
     delta_ref[...] = delta
-    target = owner_order(lax.broadcasted_iota(i32, (width, width), 0), own_ref[1])
-    move = (target == row_order(lax.broadcasted_iota(i32, (width, width), 1))).astype(bf16)
+    owner_rows(own_ref, normed_ref, delta, db_ref, 96)
+
+
+def owner_rows(own_ref, normed_ref, delta, out_ref, start):
+    blocks, width, _ = normed_ref.shape
+    target = owner_order(lax.broadcasted_iota(i32, (96, width), 0) + start, own_ref[1])
+    move = (target == row_order(lax.broadcasted_iota(i32, (96, width), 1))).astype(bf16)
     for k in range(blocks):
         dw = nt(nn(move, normed_ref[k]).astype(bf16), delta)
         m = block_of(own_ref, k, blocks)
         for j in range(4):
-            da_ref[j, m] = dw[24 * j : 24 * j + 24].astype(bf16)
-            db_ref[j, m] = dw[24 * j + 96 : 24 * j + 120].astype(bf16)
+            out_ref[j, m] = dw[24 * j : 24 * j + 24].astype(bf16)
+
+
+def own_rows_kernel(own_ref, normed_ref, delta_ref, da_ref):
+    owner_rows(own_ref, normed_ref, delta_ref[...], da_ref, 0)
 
 
 def backward_kernel(w_ref, delta_ref, *partial_refs):
@@ -250,9 +258,9 @@
     (normed,) = call(norm_kernel, [((blocks, width, slots), bf16)], own, live, gain, *whole)
     up = grad_owned.reshape(peers, 2, width).transpose(1, 2, 0)
     near = (4, blocks, 2 * group, columns)
-    gated, dw_own, dw_other, delta, w_all = call(
+    gated, dw_other, delta, w_all = call(
         forward_kernel,
-        [((2, width, peers), bf16), (near, bf16), (near, bf16), ((columns, slots), bf16), ((blocks, width, columns), bf16)],
+        [((2, width, peers), bf16), (near, bf16), ((columns, slots), bf16), ((blocks, width, columns), bf16)],
         own,
         normed,
         live,
@@ -261,6 +269,7 @@
         up,
     )
     dw_c = swap(dw_other.reshape(4, far * group, columns), "co")
+    (dw_own,) = call(own_rows_kernel, [(near, bf16)], own, normed, delta)
     partial = call(backward_kernel, [((2, width, slots), bf16)] * (blocks // 2), w_all, delta)
     dw_c = (dw_c.astype(f32) + dw_own.reshape(4, far * group, columns).astype(f32)).astype(bf16)
     dw_y = lax.all_to_all(dw_c, NEAR, 0, 0, tiled=True)

time: 179 us -> 180 us (level)
  Pallas kernels: 8.45 us -> 10.4 us
    pallas_call x6 -> x7, Pallas kernels: 8.45 us -> 10.4 us  [call(): pl.pallas_call(kernel, in_specs=[pl.BlockSpec(memory_space=pltpu.HBM) if...]
  transfers between devices with their start and end apart: 11 -> 11, of which waited for: 7 -> 6; matrix products, arithmetic and copies ran while one was open for 1% -> 1% of each run, Pallas kernels for 2% -> 3%
where the time goes in v9:
time: 180 us; the launch traced here: 179 us
  blocking collectives  104 us (58%)
  starting transfers between devices  30.3 us (17%)
  waiting for transfers between devices  30.1 us (17%)
  Pallas kernels  10.4 us (6%)
  local copies, waits for them, and re-layouts  2.96 us (2%)
    all_to_all x1, blocking collectives, body(): got = lax.all_to_all(sent.transpose(1, 0, 2), DP, 0, 0, tiled=True)  72.6 us
    all_to_all x1, blocking collectives, spread(): lax.all_to_all(jnp.broadcast_to(x[None], (count,) + x.shape), axis, 0, 0,...  18.5 us
    ppermute x6, waiting for transfers between devices, hop(): return lax.ppermute(x, 'x', [(i, (i + step) % n) for i in range(n)])  16.7 us
    ppermute x6, starting transfers between devices, hop(): return lax.ppermute(x, 'x', [(i, (i + step) % n) for i in range(n)])  16.6 us
    ppermute x4, waiting for transfers between devices, swap(): return lax.ppermute(x, axis, [(0, 1), (1, 0)])  13.3 us
    all_to_all x1, blocking collectives, body(): dw_y = lax.all_to_all(dw_c, NEAR, 0, 0, tiled=True)  13.1 us
    pallas_call x7, Pallas kernels, call(): pl.pallas_call(kernel, in_specs=[pl.BlockSpec(memory_space=pltpu.HBM) if...  10.4 us
    ppermute x4, starting transfers between devices, swap(): return lax.ppermute(x, axis, [(0, 1), (1, 0)])  10.2 us
  transfers between devices with their start and end apart: 11, of which 6 were waited for; matrix products, arithmetic and copies ran while one was open for 1% of the time, Pallas kernels for 3%

profile of v9, /device:TPU:1, one launch (start us, length us, event | category | flops | bytes accessed | tf_op | source)
XLA Modules:
  0.0 179.3 jit_solution(11263124412540235239)
XLA Ops:
  0.6 1.4 shard_map.102
  2.0 0.2 copy.18
  2.2 72.6 %all_to_all.20 = bf16[128,8,128]{2,1,0:T(8,128)(2,1)S(1)} all-to-all(bf16[128,8,128]{2,1,0:T(8,128)(2,1)S(1)} %copy.18), channel_id=1, replica_groups=mesh['zh'=16,'zl'=2,'yh'=2,'co'=2,'x'=4,'yl'=2] {'zh','zl','yh','co'}, dimensions={0} | all-to-all | bytes 524288 | tf_op jit(solution)/shard_map/all_to_all | solution.py:250
  74.8 0.1 broadcast_in_dim.2
  74.9 0.0 copy-start.1
  75.0 18.5 %all_to_all.21.wa_ref = bf16[4,5,128,128]{3,2,1,0:T(8,128)(2,1)S(1)} all-to-all(bf16[4,5,128,128]{3,2,1,0:T(8,128)(2,1)S(1)} %broadcast_in_dim.2), channel_id=1, replica_groups=mesh['zh'=16,'zl'=2,'yh'=2,'co'=2,'x'=4,'yl'=2] {'zl','yh'}, dimensions={0} | all-to-all | bytes 1310720 | tf_op jit(solution)/shard_map/all_to_all | solution.py:208
  93.5 2.6 %collective-permute-start.4 = (bf16[4,5,128,128]{3,2,1,0:T(8,128)(2,1)S(1)}, bf16[4,5,128,128]{3,2,1,0:T(8,128)(2,1)S(1)}, u32[]{:S(2)}, u32[]{:S(2)}) collective-permute-start(bf16[4,5,128,128]{3,2,1,0:T(8,128)(2,1)S(1)} %all_to_all.21.wa_ref), channel_id=1, source_target_pairs={{0,8},{8,0},{1,9},{9,1},{2,10},{10,2},{3,11},{11,3},{4,12},{12,4},... | collective-permute-start | bytes 1966088 | tf_op jit(solution)/shard_map/ppermute | solution.py:217
  96.1 0.1 pad_add_fusion.own_ref
  96.2 0.8 shard_map.103
  97.0 2.3 %collective-permute-start = (bf16[192,256]{1,0:T(8,128)(2,1)S(1)}, bf16[192,256]{1,0:T(8,128)(2,1)S(1)}, u32[]{:S(2)}, u32[]{:S(2)}) collective-permute-start(bf16[192,256]{1,0:T(8,128)(2,1)S(1)} %get-tuple-element.15), channel_id=1, source_target_pairs={{0,1},{1,0},{2,3},{3,2},{4,5},{5,4},{6,7},{7,6},{8,9},{9,8},{10,11... | collective-permute-start | bytes 294920 | tf_op jit(solution)/shard_map/ppermute | solution.py:217
  99.3 3.9 %collective-permute-done = bf16[192,256]{1,0:T(8,128)(2,1)S(1)} collective-permute-done((bf16[192,256]{1,0:T(8,128)(2,1)S(1)}, bf16[192,256]{1,0:T(8,128)(2,1)S(1)}, u32[]{:S(2)}, u32[]{:S(2)}) %collective-permute-start) | collective-permute-done | bytes 98336 | tf_op jit(solution)/shard_map/ppermute | solution.py:217
  103.2 4.4 %collective-permute-start.3 = (bf16[2,192,256]{2,1,0:T(8,128)(2,1)S(1)}, bf16[2,192,256]{2,1,0:T(8,128)(2,1)S(1)}, u32[]{:S(2)}, u32[]{:S(2)}) collective-permute-start(bf16[2,192,256]{2,1,0:T(8,128)(2,1)S(1)} %pad_maximum_fusion.1.refs_0_), channel_id=1, source_target_pairs={{0,6},{2,0},{4,2},{6,4},{1,7},{3,1},{5,3},{7,5},{8,14},{10,8},{12,... | collective-permute-start | bytes 589832 | tf_op jit(solution)/shard_map/ppermute | solution.py:213
  107.6 2.4 %collective-permute-start.2 = (bf16[2,192,256]{2,1,0:T(8,128)(2,1)S(1)}, bf16[2,192,256]{2,1,0:T(8,128)(2,1)S(1)}, u32[]{:S(2)}, u32[]{:S(2)}) collective-permute-start(bf16[2,192,256]{2,1,0:T(8,128)(2,1)S(1)} %pad_maximum_fusion.1.refs_0_), channel_id=1, source_target_pairs={{0,4},{2,6},{4,0},{6,2},{1,5},{3,7},{5,1},{7,3},{8,12},{10,14},{12... | collective-permute-start | bytes 589832 | tf_op jit(solution)/shard_map/ppermute | solution.py:213
  110.1 2.5 %collective-permute-start.1 = (bf16[2,192,256]{2,1,0:T(8,128)(2,1)S(1)}, bf16[2,192,256]{2,1,0:T(8,128)(2,1)S(1)}, u32[]{:S(2)}, u32[]{:S(2)}) collective-permute-start(bf16[2,192,256]{2,1,0:T(8,128)(2,1)S(1)} %pad_maximum_fusion.1.refs_0_), channel_id=1, source_target_pairs={{0,2},{2,4},{4,6},{6,0},{1,3},{3,5},{5,7},{7,1},{8,10},{10,12},{12... | collective-permute-start | bytes 589832 | tf_op jit(solution)/shard_map/ppermute | solution.py:213
  112.6 0.0 copy-done.1
  112.6 0.3 reshape.51
  112.9 0.3 copy.20
  113.2 0.5 reshape.61.gain_ref
  113.7 0.0 collective-permute-done.3.refs_3_
  113.7 2.7 %collective-permute-done.2.refs_2_ = bf16[2,192,256]{2,1,0:T(8,128)(2,1)S(1)} collective-permute-done((bf16[2,192,256]{2,1,0:T(8,128)(2,1)S(1)}, bf16[2,192,256]{2,1,0:T(8,128)(2,1)S(1)}, u32[]{:S(2)}, u32[]{:S(2)}) %collective-permute-start.2) | collective-permute-done | bytes 196640 | tf_op jit(solution)/shard_map/ppermute | solution.py:213
  116.3 5.1 %collective-permute-done.1.refs_1_ = bf16[2,192,256]{2,1,0:T(8,128)(2,1)S(1)} collective-permute-done((bf16[2,192,256]{2,1,0:T(8,128)(2,1)S(1)}, bf16[2,192,256]{2,1,0:T(8,128)(2,1)S(1)}, u32[]{:S(2)}, u32[]{:S(2)}) %collective-permute-start.1) | collective-permute-done | bytes 196640 | tf_op jit(solution)/shard_map/ppermute | solution.py:213
  121.4 0.0 copy-start
  121.4 1.3 shard_map.104.normed_ref
  122.7 0.0 collective-permute-done.4.wb_ref
  122.7 0.0 copy-done
  122.7 3.5 %shard_map.105 = (bf16[2,192,128]{2,1,0:T(8,128)(2,1)}, bf16[4,8,24,384]{3,2,1,0:T(8,128)(2,1)S(1)}, bf16[384,256]{1,0:T(8,128)(2,1)S(1)}, bf16[8,192,384]{2,1,0:T(8,128)(2,1)S(1)}) custom-call(s32[2]{0:T(128)S(1)} %pad_add_fusion.own_ref, bf16[8,192,256]{2,1,0:T(8,128)(2,1)S(1)} %shard_map.104.normed_ref, f32[8,256]{1,0:T(8,128)S(1)} %get-tuple-element.14.live_ref, ...), custom_call_target="tpu_custom_call" | custom-call | tf_op jit(solution)/shard_map/pallas_call | solution.py:32
  126.2 3.0 %collective-permute-start.5 = (bf16[4,192,384]{2,1,0:T(8,128)(2,1)S(1)}, bf16[4,192,384]{2,1,0:T(8,128)(2,1)S(1)}, u32[]{:S(2)}, u32[]{:S(2)}) collective-permute-start(bf16[4,192,384]{2,1,0:T(8,128)(2,1)S(1)} %bitcast.35), channel_id=1, source_target_pairs={{0,8},{8,0},{1,9},{9,1},{2,10},{10,2},{3,11},{11,3},{4,12},{12,4},... | collective-permute-start | bytes 1769480 | tf_op jit(solution)/shard_map/ppermute | solution.py:217
  129.2 2.0 %shard_map.106 = bf16[4,8,24,384]{3,2,1,0:T(8,128)(2,1)S(1)} custom-call(s32[2]{0:T(128)S(1)} %pad_add_fusion.own_ref, bf16[8,192,256]{2,1,0:T(8,128)(2,1)S(1)} %shard_map.104.normed_ref, bf16[384,256]{1,0:T(8,128)(2,1)S(1)} %get-tuple-element.18.delta_ref), custom_call_target="tpu_custom_call" | custom-call | tf_op jit(solution)/shard_map/pallas_call | solution.py:32
  131.2 0.0 collective-permute-done.5
  131.2 0.2 fusion
  131.4 13.1 %all_to_all.22 = bf16[4,192,384]{2,1,0:T(8,128)(2,1)S(1)} all-to-all(bf16[4,192,384]{2,1,0:T(8,128)(2,1)S(1)} %fusion), channel_id=1, replica_groups=mesh['zh'=16,'zl'=2,'yh'=2,'co'=2,'x'=4,'yl'=2] {'zl','yh'}, dimensions={0} | all-to-all | bytes 1179648 | tf_op jit(solution)/shard_map/all_to_all | solution.py:275
  144.5 0.1 reduce_sum.21
  144.7 0.7 copy.23
  145.5 3.5 %all-to-all-start.3 = ((bf16[16,9,4,128]{3,2,1,0:T(4,128)(2,1)}), bf16[16,9,4,128]{3,2,1,0:T(4,128)(2,1)S(1)}, u32[]{:S(2)}, u32[]{:S(2)}) async-start(bf16[16,9,4,128]{3,2,1,0:T(4,128)(2,1)} %copy.23), calls=%async_computation.3 | async-start | bytes 294912 | tf_op jit(solution)/shard_map/all_to_all | solution.py:278
  149.0 0.6 shard_map.107
  149.6 2.2 %collective-permute-start.6 = (bf16[2,192,256]{2,1,0:T(8,128)(2,1)S(1)}, bf16[2,192,256]{2,1,0:T(8,128)(2,1)S(1)}, u32[]{:S(2)}, u32[]{:S(2)}) collective-permute-start(bf16[2,192,256]{2,1,0:T(8,128)(2,1)S(1)} %get-tuple-element.21), channel_id=1, source_target_pairs={{0,6},{2,0},{4,2},{6,4},{1,7},{3,1},{5,3},{7,5},{8,14},{10,8},{12,... | collective-permute-start | bytes 589832 | tf_op jit(solution)/shard_map/ppermute | solution.py:213
  151.7 2.4 %collective-permute-start.7 = (bf16[2,192,256]{2,1,0:T(8,128)(2,1)S(1)}, bf16[2,192,256]{2,1,0:T(8,128)(2,1)S(1)}, u32[]{:S(2)}, u32[]{:S(2)}) collective-permute-start(bf16[2,192,256]{2,1,0:T(8,128)(2,1)S(1)} %get-tuple-element.22), channel_id=1, source_target_pairs={{0,4},{2,6},{4,0},{6,2},{1,5},{3,7},{5,1},{7,3},{8,12},{10,14},{12... | collective-permute-start | bytes 589832 | tf_op jit(solution)/shard_map/ppermute | solution.py:213
  154.2 2.6 %collective-permute-start.8 = (bf16[2,192,256]{2,1,0:T(8,128)(2,1)S(1)}, bf16[2,192,256]{2,1,0:T(8,128)(2,1)S(1)}, u32[]{:S(2)}, u32[]{:S(2)}) collective-permute-start(bf16[2,192,256]{2,1,0:T(8,128)(2,1)S(1)} %get-tuple-element.23), channel_id=1, source_target_pairs={{0,2},{2,4},{4,6},{6,0},{1,3},{3,5},{5,7},{7,1},{8,10},{10,12},{12... | collective-permute-start | bytes 589832 | tf_op jit(solution)/shard_map/ppermute | solution.py:213
  156.8 0.0 collective-permute-done.6.refs_1_
  156.9 3.1 %collective-permute-done.7.refs_2_ = bf16[2,192,256]{2,1,0:T(8,128)(2,1)S(1)} collective-permute-done((bf16[2,192,256]{2,1,0:T(8,128)(2,1)S(1)}, bf16[2,192,256]{2,1,0:T(8,128)(2,1)S(1)}, u32[]{:S(2)}, u32[]{:S(2)}) %collective-permute-start.7) | collective-permute-done | bytes 196640 | tf_op jit(solution)/shard_map/ppermute | solution.py:213
  160.0 5.8 %collective-permute-done.8.refs_3_ = bf16[2,192,256]{2,1,0:T(8,128)(2,1)S(1)} collective-permute-done((bf16[2,192,256]{2,1,0:T(8,128)(2,1)S(1)}, bf16[2,192,256]{2,1,0:T(8,128)(2,1)S(1)}, u32[]{:S(2)}, u32[]{:S(2)}) %collective-permute-start.8) | collective-permute-done | bytes 196640 | tf_op jit(solution)/shard_map/ppermute | solution.py:213
  165.8 0.1 pad_maximum_fusion
  165.9 2.3 %collective-permute-start.9 = (bf16[4,192,256]{2,1,0:T(8,128)(2,1)S(1)}, bf16[4,192,256]{2,1,0:T(8,128)(2,1)S(1)}, u32[]{:S(2)}, u32[]{:S(2)}) collective-permute-start(bf16[4,192,256]{2,1,0:T(8,128)(2,1)S(1)} %pad_maximum_fusion), channel_id=1, source_target_pairs={{0,1},{1,0},{2,3},{3,2},{4,5},{5,4},{6,7},{7,6},{8,9},{9,8},{10,11... | collective-permute-start | bytes 1179656 | tf_op jit(solution)/shard_map/ppermute | solution.py:217
  168.2 9.4 %collective-permute-done.9.refs_4_ = bf16[4,192,256]{2,1,0:T(8,128)(2,1)S(1)} collective-permute-done((bf16[4,192,256]{2,1,0:T(8,128)(2,1)S(1)}, bf16[4,192,256]{2,1,0:T(8,128)(2,1)S(1)}, u32[]{:S(2)}, u32[]{:S(2)}) %collective-permute-start.9) | collective-permute-done | bytes 393248 | tf_op jit(solution)/shard_map/ppermute | solution.py:217
  177.6 0.9 shard_map.108
  178.5 0.0 all-to-all-done.3
  178.5 0.1 convert_reduce_fusion
  178.7 0.7 fusion.1
  (14 shorter events, 0.2 us)
Async XLA Ops:
  74.9 37.6 %copy-start.1 = (f32[1536]{0:T(1024)S(1)}, f32[1536]{0:T(1024)}, u32[]{:S(2)}) copy-start(f32[1536]{0:T(1024)} %param.10) | copy-start | bytes 18436
  93.5 29.2 %collective-permute-start.4 = (bf16[4,5,128,128]{3,2,1,0:T(8,128)(2,1)S(1)}, bf16[4,5,128,128]{3,2,1,0:T(8,128)(2,1)S(1)}, u32[]{:S(2)}, u32[]{:S(2)}) collective-permute-start(bf16[4,5,128,128]{3,2,1,0:T(8,128)(2,1)S(1)} %all_to_all.21.wa_ref), channel_id=1, source_target_pairs={{0,8},{8,0},{1,9},{9,1},{2,10},{10,2},{3,11},{11,3},{4,12},{12,4},... | collective-permute-start | bytes 1966088 | tf_op jit(solution)/shard_map/ppermute | solution.py:217
  97.0 6.2 %collective-permute-start = (bf16[192,256]{1,0:T(8,128)(2,1)S(1)}, bf16[192,256]{1,0:T(8,128)(2,1)S(1)}, u32[]{:S(2)}, u32[]{:S(2)}) collective-permute-start(bf16[192,256]{1,0:T(8,128)(2,1)S(1)} %get-tuple-element.15), channel_id=1, source_target_pairs={{0,1},{1,0},{2,3},{3,2},{4,5},{5,4},{6,7},{7,6},{8,9},{9,8},{10,11... | collective-permute-start | bytes 294920 | tf_op jit(solution)/shard_map/ppermute | solution.py:217
  103.2 10.4 %collective-permute-start.3 = (bf16[2,192,256]{2,1,0:T(8,128)(2,1)S(1)}, bf16[2,192,256]{2,1,0:T(8,128)(2,1)S(1)}, u32[]{:S(2)}, u32[]{:S(2)}) collective-permute-start(bf16[2,192,256]{2,1,0:T(8,128)(2,1)S(1)} %pad_maximum_fusion.1.refs_0_), channel_id=1, source_target_pairs={{0,6},{2,0},{4,2},{6,4},{1,7},{3,1},{5,3},{7,5},{8,14},{10,8},{12,... | collective-permute-start | bytes 589832 | tf_op jit(solution)/shard_map/ppermute | solution.py:213
  107.6 8.7 %collective-permute-start.2 = (bf16[2,192,256]{2,1,0:T(8,128)(2,1)S(1)}, bf16[2,192,256]{2,1,0:T(8,128)(2,1)S(1)}, u32[]{:S(2)}, u32[]{:S(2)}) collective-permute-start(bf16[2,192,256]{2,1,0:T(8,128)(2,1)S(1)} %pad_maximum_fusion.1.refs_0_), channel_id=1, source_target_pairs={{0,4},{2,6},{4,0},{6,2},{1,5},{3,7},{5,1},{7,3},{8,12},{10,14},{12... | collective-permute-start | bytes 589832 | tf_op jit(solution)/shard_map/ppermute | solution.py:213
  110.1 11.4 %collective-permute-start.1 = (bf16[2,192,256]{2,1,0:T(8,128)(2,1)S(1)}, bf16[2,192,256]{2,1,0:T(8,128)(2,1)S(1)}, u32[]{:S(2)}, u32[]{:S(2)}) collective-permute-start(bf16[2,192,256]{2,1,0:T(8,128)(2,1)S(1)} %pad_maximum_fusion.1.refs_0_), channel_id=1, source_target_pairs={{0,2},{2,4},{4,6},{6,0},{1,3},{3,5},{5,7},{7,1},{8,10},{10,12},{12... | collective-permute-start | bytes 589832 | tf_op jit(solution)/shard_map/ppermute | solution.py:213
  121.4 1.3 copy-start
  126.2 5.0 %collective-permute-start.5 = (bf16[4,192,384]{2,1,0:T(8,128)(2,1)S(1)}, bf16[4,192,384]{2,1,0:T(8,128)(2,1)S(1)}, u32[]{:S(2)}, u32[]{:S(2)}) collective-permute-start(bf16[4,192,384]{2,1,0:T(8,128)(2,1)S(1)} %bitcast.35), channel_id=1, source_target_pairs={{0,8},{8,0},{1,9},{9,1},{2,10},{10,2},{3,11},{11,3},{4,12},{12,4},... | collective-permute-start | bytes 1769480 | tf_op jit(solution)/shard_map/ppermute | solution.py:217
  145.5 33.0 %all-to-all-start.3 = ((bf16[16,9,4,128]{3,2,1,0:T(4,128)(2,1)}), bf16[16,9,4,128]{3,2,1,0:T(4,128)(2,1)S(1)}, u32[]{:S(2)}, u32[]{:S(2)}) async-start(bf16[16,9,4,128]{3,2,1,0:T(4,128)(2,1)} %copy.23), calls=%async_computation.3 | async-start | bytes 294912 | tf_op jit(solution)/shard_map/all_to_all | solution.py:278
  149.6 7.3 %collective-permute-start.6 = (bf16[2,192,256]{2,1,0:T(8,128)(2,1)S(1)}, bf16[2,192,256]{2,1,0:T(8,128)(2,1)S(1)}, u32[]{:S(2)}, u32[]{:S(2)}) collective-permute-start(bf16[2,192,256]{2,1,0:T(8,128)(2,1)S(1)} %get-tuple-element.21), channel_id=1, source_target_pairs={{0,6},{2,0},{4,2},{6,4},{1,7},{3,1},{5,3},{7,5},{8,14},{10,8},{12,... | collective-permute-start | bytes 589832 | tf_op jit(solution)/shard_map/ppermute | solution.py:213
  151.7 8.2 %collective-permute-start.7 = (bf16[2,192,256]{2,1,0:T(8,128)(2,1)S(1)}, bf16[2,192,256]{2,1,0:T(8,128)(2,1)S(1)}, u32[]{:S(2)}, u32[]{:S(2)}) collective-permute-start(bf16[2,192,256]{2,1,0:T(8,128)(2,1)S(1)} %get-tuple-element.22), channel_id=1, source_target_pairs={{0,4},{2,6},{4,0},{6,2},{1,5},{3,7},{5,1},{7,3},{8,12},{10,14},{12... | collective-permute-start | bytes 589832 | tf_op jit(solution)/shard_map/ppermute | solution.py:213
  154.2 11.6 %collective-permute-start.8 = (bf16[2,192,256]{2,1,0:T(8,128)(2,1)S(1)}, bf16[2,192,256]{2,1,0:T(8,128)(2,1)S(1)}, u32[]{:S(2)}, u32[]{:S(2)}) collective-permute-start(bf16[2,192,256]{2,1,0:T(8,128)(2,1)S(1)} %get-tuple-element.23), channel_id=1, source_target_pairs={{0,2},{2,4},{4,6},{6,0},{1,3},{3,5},{5,7},{7,1},{8,10},{10,12},{12... | collective-permute-start | bytes 589832 | tf_op jit(solution)/shard_map/ppermute | solution.py:213
  165.9 11.7 %collective-permute-start.9 = (bf16[4,192,256]{2,1,0:T(8,128)(2,1)S(1)}, bf16[4,192,256]{2,1,0:T(8,128)(2,1)S(1)}, u32[]{:S(2)}, u32[]{:S(2)}) collective-permute-start(bf16[4,192,256]{2,1,0:T(8,128)(2,1)S(1)} %pad_maximum_fusion), channel_id=1, source_target_pairs={{0,1},{1,0},{2,3},{3,2},{4,5},{5,4},{6,7},{7,6},{8,9},{9,8},{10,11... | collective-permute-start | bytes 1179656 | tf_op jit(solution)/shard_map/ppermute | solution.py:217
